TPU v7x, 32 devices: a whole 2x2x4 slice. The times are simulated.
32 devices in a mesh: row: 8 (over z, x), ba: 4 (over y, core).
Axes of the slice: x: 2, y: 2, z: 4, core: 2. Of those that a mesh axis runs over, the one named last changes fastest.
Arguments:
- constants: float32 [8, 192, 36864], P('row', 'ba'), may hold values from -6 to 6
- current_modes: float32 [8, 2, 192, 4], P('row', None, 'ba'), may hold values from -0.4375 to 0.4375
- owner_id: int32 [1], replicated, may hold values from 0 to 7
- live_count: int32 [8], P('row'), may hold values from 0 to 1, as said below
- triplets: int32 [8, 6], P('row'), may hold values from -3 to 3
- center_point: int32 [3], replicated, may hold values from 0 to 31
- pair_points: int32 [64, 3], P('row'), may hold values from 0 to 31
- first_vectors: float32 [64, 2, 36864], P('row'), may hold values from -0.4375 to 0.4375
- second_vectors: float32 [64, 2, 36864], P('row'), may hold values from -0.4375 to 0.4375
Outputs:
- strength: float32 [64, 4, 36864], P('row', 'ba')
Inputs may be any that keep to these rules, and one draw needn't show every extreme that they name: Shard j uses its first live_count[j] slots; the constants and triplets of the other slots are ignored. A shard may use none. Some shard uses all 1 slots.
All inputs are finite; a program needn't handle non-finite values.
Results may differ from a plain program's by a relative error of at most 0.00008.
Values sent between devices are 32-bit elements; how exact they have to be, the bound alone decides.
No kernel may reach another device: no remote copies, remote signals or barrier semaphores. Data moves between devices by JAX's collectives and lax.ppermute only.
A program may use at most 128 MiB of HBM per device.

v0:
```python
import math

import jax
import jax.numpy as jnp
from jax import lax
from jax.sharding import PartitionSpec as P

B = 192
G = 32


HIGHEST = lax.Precision.HIGHEST
FULL_TURN = 2.0 * math.pi


def broadcast(shard, axis, root):
    mine = lax.axis_index(axis) == root
    return lax.psum(jnp.where(mine, shard, jnp.zeros_like(shard)), axis)


def rotation_table(pair_rows, shift_rows, grid_size):
    turns = (
        jnp.sum(pair_rows[:, :, None] * shift_rows[None, 0:3, :], axis=1) - shift_rows[3][None, :]
    )
    angle = jnp.mod(turns, grid_size).astype(jnp.float32) * (FULL_TURN / grid_size)
    cosine = jnp.cos(angle)
    sine = jnp.sin(angle)
    upper_row = jnp.stack([cosine, -sine], axis=1)
    lower_row = jnp.stack([sine, cosine], axis=1)
    return jnp.stack([upper_row, lower_row], axis=1)


def complex_block(vectors, branches):
    pair_count = vectors.shape[0]
    real_part = vectors[:, 0].reshape(pair_count, branches, branches)
    imag_part = vectors[:, 1].reshape(pair_count, branches, branches)
    upper_row = jnp.stack([real_part, -imag_part], axis=1)
    lower_row = jnp.stack([imag_part, real_part], axis=1)
    return jnp.stack([upper_row, lower_row], axis=1)


def strengths(phase_sum, first_vectors, second_vectors, branches, total_slots):
    pair_count = phase_sum.shape[0]
    band_count = phase_sum.shape[1]
    shaped = phase_sum.reshape(pair_count, band_count, 2, branches, branches)
    partial_sum = jnp.einsum(
        "knibc,koicm->knobm", shaped, complex_block(second_vectors, branches), precision=HIGHEST
    )
    amplitude = jnp.einsum(
        "kojbp,knjbm->knopm", complex_block(first_vectors, branches), partial_sum, precision=HIGHEST
    )
    result = (
        amplitude[:, :, 0] * amplitude[:, :, 0] + amplitude[:, :, 1] * amplitude[:, :, 1]
    ) / total_slots
    return result.reshape(pair_count, band_count, branches * branches)


def body(
    constants,
    current_modes,
    owner_id,
    live_count,
    triplets,
    center_point,
    pair_points,
    first_vectors,
    second_vectors,
):
    slot_count = constants.shape[0]
    eigen = broadcast(current_modes[0], "row", owner_id[0])
    weight = (jnp.arange(slot_count, dtype=jnp.int32) < live_count[0]).astype(jnp.float32)
    term = jnp.einsum("san,rax->nsrx", eigen, constants, precision=HIGHEST)
    contracted = lax.psum_scatter(
        term * weight[None, None, :, None], "ba", scatter_dimension=0, tiled=True
    )
    second_cell = triplets[:, 3:6]
    offsets = triplets[:, 0:3] - second_cell
    point_shift = jnp.sum(second_cell * center_point[None, :], axis=1)
    shift_rows = jnp.concatenate([offsets.T, point_shift[None, :]], axis=0)
    geometry = shift_rows.astype(jnp.float32)[None]
    shard_block = lax.all_gather(contracted, "row", axis=2, tiled=True)
    shard_geometry = lax.all_gather(geometry, "row", axis=2, tiled=True)
    rotation = rotation_table(pair_points, shard_geometry[0].astype(jnp.int32), G)
    phase_sum = jnp.einsum("kuir,nirx->knux", rotation, shard_block, precision=HIGHEST)
    total_slots = slot_count * lax.axis_size("row")
    return strengths(phase_sum, first_vectors, second_vectors, B, total_slots)


def solution(mesh):
    return jax.shard_map(
        body,
        mesh=mesh,
        in_specs=(
            P("row", "ba", None),
            P("row", None, "ba", None),
            P(),
            P("row"),
            P("row", None),
            P(),
            P("row", None),
            P("row", None, None),
            P("row", None, None),
        ),
        out_specs=P("row", "ba", None),
        check_vma=False,
    )
```

profile of v0, /device:TPU:0, one launch (start us, length us, event | category | flops | bytes accessed | tf_op | source)
XLA Modules:
  0.0 172.8 jit_solution(9790825967752891447)
XLA Ops:
  6.5 0.0 all-reduce.3.cloned.1.call-start
  7.2 23.1 %psum.7 = f32[2,48,4]{1,2,0:T(4,128)S(1)} all-reduce(f32[2,48,4]{1,2,0:T(4,128)S(1)} %select_bitcast_fusion), channel_id=1, replica_groups=mesh['row'=8,'ba'=4] {'row'}, use_global_device_ids=true, to_apply=%region_0.1 | all-reduce | flops 384 | bytes 3072 | tf_op jit(solution)/shard_map/psum | solution.py:18
  31.0 5.8 %fusion = f32[4,2,1,36864]{3,0,1,2:T(4,128)S(1)} fusion(f32[2,48,4]{1,2,0:T(4,128)S(1)} %psum.7, f32[1,48,36864]{2,1,0:T(8,128)} %param.9, f32[]{:T(128)} %bitcast.6), kind=kOutput, calls=%fused_computation.2 | convolution fusion | flops 170164224 | bytes 8259076 | tf_op jit(solution)/shard_map/san,rax->nsrx/dot_general | solution.py:72
  36.8 0.0 copy-start.7
  36.8 0.0 copy-start.4
  36.8 0.0 copy-start.6
  36.8 0.0 copy-start.3
  36.9 1.9 %copy.51 = f32[4,2,1,36864]{3,1,2,0:T(2,128)} copy(f32[4,2,1,36864]{3,0,1,2:T(4,128)S(1)} %fusion) | data formatting | bytes 2359296 | tf_op jit(solution)/shard_map/mul | solution.py:74
  38.8 0.0 all-reduce.3.cloned.1.call-update
  38.8 0.0 all-gather.2.cloned.1.call-start
  38.9 0.0 copy-done.7
  38.9 0.6 dynamic-slice
  39.5 34.3 %all-reduce.3.cloned.1.call-done = f32[4,2,1,36864]{3,1,2,0:T(2,128)} async-done(((f32[4,2,1,36864]{3,1,2,0:T(2,128)}), f32[4,2,1,36864]{3,1,2,0:T(2,128)}) %all-reduce.3.cloned.1.call-update) | async-done | bytes 1179664
  73.8 2.3 %dynamic-slice_bitcast_fusion = f32[1,2,1,36864]{3,1,0,2:T(2,128)} fusion(f32[4,2,1,36864]{3,1,2,0:T(2,128)} %all-reduce.3.cloned.1.call-done, u32[]{:T(128)} %bitcast.46), kind=kLoop, calls=%fused_computation.29 | loop fusion | bytes 589828 | tf_op jit(solution)/shard_map/reduce_scatter | solution.py:73
  76.1 0.0 all-gather.2.cloned.1.call-update
  76.2 0.0 copy-done.4
  76.2 0.0 copy-done.6
  76.2 0.7 subtract_bitcast_fusion
  76.9 0.7 fusion.29
  77.6 20.7 %all_gather.7 = f32[1,4,8]{1,0,2:T(1,128)S(1)} all-gather(f32[1,4,1]{1,0,2:T(1,128)S(1)} %fusion.29), channel_id=1, replica_groups=mesh['row'=8,'ba'=4] {'row'}, dimensions={2}, use_global_device_ids=true | all-gather | bytes 144 | tf_op jit(solution)/shard_map/all_gather | solution.py:82
  98.3 0.1 copy.55
  98.4 7.2 %slice_reduce_fusion.2 = (f32[8,36864]{1,0:T(8,128)S(1)}, f32[8,36864]{1,0:T(8,128)}) fusion(f32[8,2,36864]{2,1,0:T(2,128)S(1)} %copy-done.3), kind=kLoop, calls=%fused_computation.27 | loop fusion | bytes 4718592 | tf_op jit(solution)/shard_map/slice | solution.py:36
  105.6 0.7 reshape_squeeze.6
  106.3 0.6 copy.47
  106.9 1.3 neg.30
  108.2 2.0 %stack_reshape_squeeze.4 = f32[8,1,192,192]{3,2,0,1:T(8,128)S(1)} reshape(f32[8,36864]{1,0:T(8,128)} %get-tuple-element.6) | data formatting | bytes 2359296 | tf_op jit(solution)/shard_map/stack;reshape;squeeze | solution.py:37
  110.2 1.8 %copy.48 = f32[8,1,192,192]{2,3,1,0:T(8,128)} copy(f32[8,1,192,192]{3,2,0,1:T(8,128)S(1)} %stack_reshape_squeeze.4) | data formatting | bytes 2359296 | tf_op jit(solution)/shard_map/stack;reshape;squeeze | solution.py:37
  112.0 10.4 %slice_reduce_fusion = (f32[8,36864]{1,0:T(8,128)}, f32[8,36864]{1,0:T(8,128)}) fusion(f32[8,2,36864]{2,1,0:T(2,128)} %param.16), kind=kLoop, calls=%fused_computation.25 | loop fusion | bytes 4718592 | tf_op jit(solution)/shard_map/slice | solution.py:36
  122.4 2.0 %reshape_squeeze.7 = f32[8,1,192,192]{3,2,0,1:T(8,128)S(1)} reshape(f32[8,36864]{1,0:T(8,128)} %get-tuple-element.7) | data formatting | bytes 2359296 | tf_op jit(solution)/shard_map/reshape;squeeze | solution.py:36
  124.4 3.2 %stack_reshape_squeeze.5 = f32[8,1,192,192]{3,2,0,1:T(8,128)} reshape(f32[8,36864]{1,0:T(8,128)} %get-tuple-element.8) | data formatting | bytes 2359296 | tf_op jit(solution)/shard_map/stack;reshape;squeeze | solution.py:37
  127.6 0.3 slice_reduce_fusion.4
  127.9 0.1 multiply_reduce_fusion
  128.0 0.1 fusion.34
  128.0 5.7 %maximum_bitcast_fusion = (f32[8,1,2,192,192]{3,4,2,1,0:T(8,128)}, f32[8,1,2,192,192]{3,4,2,1,0:T(8,128)}) fusion(f32[8,1,192,192]{2,3,1,0:T(8,128)} %neg.30, f32[8,1,192,192]{2,3,1,0:T(8,128)} %copy.48, f32[8,1,192,192]{2,3,1,0:T(8,128)S(1)} %copy.47), kind=kLoop, calls=%fused_computation.12 | loop fusion | flops 1179648 | bytes 8257536 | tf_op jit(solution)/shard_map/stack | solution.py:39
  133.7 0.1 bitcast_negate_fusion
  133.9 1.3 copy-done.2
  135.2 3.5 %maximum_bitcast_fusion.2 = (f32[8,1,2,192,192]{4,3,2,1,0:T(8,128)}, f32[8,1,2,192,192]{4,3,2,1,0:T(8,128)}) fusion(f32[8,1,192,192]{3,2,1,0:T(8,128)S(1)} %bitcast_negate_fusion, f32[8,1,192,192]{3,2,1,0:T(8,128)S(1)} %bitcast.102, f32[8,1,192,192]{3,2,1,0:T(8,128)S(1)} %bitcast.101), kind=kLoop, calls=%fused_computation.14 | loop fusion | flops 1179648 | bytes 8257536 | tf_op jit(solution)/shard_map/stack | solution.py:39
  138.7 6.4 %convolution_bitcast_fusion = f32[8,1,2,36864]{3,0,2,1:T(8,128)} fusion(f32[1,2,8,36864]{3,1,0,2:T(2,128)} %all-gather.2.cloned.1.call-done, f32[8,1,2,8]{3,0,2,1:T(8,128)S(1)} %get-tuple-element.17, f32[8,1,2,8]{3,0,2,1:T(8,128)S(1)} %get-tuple-element.16), kind=kOutput, calls=%fused_computation | convolution fusion | flops 113246464 | bytes 4719616 | tf_op jit(solution)/shard_map/kuir,nirx->knux/dot_general | solution.py:84
  145.1 2.9 %reshape.272 = f32[8,2,192,192]{3,2,0,1:T(8,128)S(1)} reshape(f32[8,1,2,36864]{3,0,2,1:T(8,128)} %convolution_bitcast_fusion) | data formatting | bytes 4718592 | tf_op jit(solution)/shard_map/reshape.7
  148.0 0.0 copy-start
  148.0 0.0 copy-start.1
  148.1 8.1 %fusion.2 = f32[8,2,192,192,1]{3,2,4,1,0:T(8,128)S(1)} fusion(f32[8,1,2,192,192]{3,4,2,1,0:T(8,128)} %get-tuple-element.12, f32[8,1,2,192,192]{3,4,2,1,0:T(8,128)} %get-tuple-element.11, f32[8,2,192,192]{3,2,0,1:T(8,128)S(1)} %reshape.272), kind=kOutput, calls=%fused_computation.4 | convolution fusion | flops 2719088640 | bytes 9437184 | tf_op jit(solution)/shard_map/knibc,koicm->knobm/dot_general | solution.py:46
  156.2 0.0 copy-done
  156.2 0.0 copy-done.1
  156.2 6.0 %fusion.14 = f32[8,1,2,192,192]{3,4,2,0,1:T(8,128)S(1)} fusion(f32[8,1,2,192,192]{4,3,2,1,0:T(8,128)S(1)} %copy-done.1, f32[8,1,2,192,192]{4,3,2,1,0:T(8,128)S(1)} %copy-done, f32[8,2,192,192,1]{3,2,4,1,0:T(8,128)S(1)} %fusion.2), kind=kOutput, calls=%fused_computation.20 | convolution fusion | flops 2719088640 | bytes 9437184 | tf_op jit(solution)/shard_map/kojbp,knjbm->knopm/dot_general | solution.py:49
  162.2 0.2 fusion.20
  162.5 0.6 copy.61
  163.0 2.5 %div.11 = f32[8,1,36864]{2,1,0:T(1,128)} reshape(f32[8,1,1,192,192]{4,3,0,2,1:T(8,128)S(1)} %copy.61) | data formatting | bytes 2359296 | tf_op jit(solution)/shard_map/div | solution.py:52
  (8 shorter events, 0.0 us)
Async XLA Ops:
  6.5 67.3 %all-reduce.3.cloned.1.call-start = ((), (), s32[]{:S(2)}) async-start(), calls=%async_computation.1 | async-start | bytes 2359296
  36.8 2.1 %copy-start.7 = (u32[32]{0:T(128)S(1)}, u32[32]{0:T(128)}, u32[]{:S(2)}) copy-start(u32[32]{0:T(128)} %constant.37) | copy-start | bytes 388
  36.8 39.4 %copy-start.4 = (s32[1,6]{1,0:T(1,128)S(1)}, s32[1,6]{1,0:T(1,128)}, u32[]{:S(2)}) copy-start(s32[1,6]{1,0:T(1,128)} %param.13) | copy-start | bytes 76
  36.8 39.4 %copy-start.6 = (s32[3]{0:T(128)S(1)}, s32[3]{0:T(128)}, u32[]{:S(2)}) copy-start(s32[3]{0:T(128)} %param.14) | copy-start | bytes 40
  36.8 61.5 %copy-start.3 = (f32[8,2,36864]{2,1,0:T(2,128)S(1)}, f32[8,2,36864]{2,1,0:T(2,128)}, u32[]{:S(2)}) copy-start(f32[8,2,36864]{2,1,0:T(2,128)} %param.17) | copy-start | bytes 7077892
  38.8 99.9 %all-gather.2.cloned.1.call-start = ((), (), s32[]{:S(2)}) async-start(), calls=%async_computation | async-start | bytes 2654208 | tf_op jit(solution)/shard_map/all_gather | solution.py:81
  122.4 5.5 %copy-start.5 = (s32[8,3]{0,1:T(4,128)S(1)}, s32[8,3]{0,1:T(4,128)}, u32[]{:S(2)}) copy-start(s32[8,3]{0,1:T(4,128)} %param.15) | copy-start | bytes 292
  133.7 1.4 copy-start.2
  148.0 8.1 %copy-start = (f32[8,1,2,192,192]{4,3,2,1,0:T(8,128)S(1)}, f32[8,1,2,192,192]{4,3,2,1,0:T(8,128)}, u32[]{:S(2)}) copy-start(f32[8,1,2,192,192]{4,3,2,1,0:T(8,128)} %get-tuple-element.13) | copy-start | bytes 7077892
  148.0 8.1 %copy-start.1 = (f32[8,1,2,192,192]{4,3,2,1,0:T(8,128)S(1)}, f32[8,1,2,192,192]{4,3,2,1,0:T(8,128)}, u32[]{:S(2)}) copy-start(f32[8,1,2,192,192]{4,3,2,1,0:T(8,128)} %get-tuple-element.14) | copy-start | bytes 7077892
Sparse Core Ops, SparseCore 0:
  38.9 34.8 all-reduce.2
  76.3 51.9 all-gather.1
where the time goes:
time: 176 us; the launch traced here: 173 us
  blocking collectives  43.8 us (25%)
  local copies, waits for them, and re-layouts  40.5 us (23%)
  waiting for transfers between devices  34.3 us (19%)
  matrix products  26.4 us (15%)
  between operations  15.4 us (9%)
  other arithmetic  12.4 us (7%)
    unnamed x3, waiting for transfers between devices  34.3 us
    psum x1, blocking collectives, broadcast(): return lax.psum(jnp.where(mine, shard, jnp.zeros_like(shard)), axis)  23.1 us
    all_gather x1, blocking collectives, body(): shard_geometry = lax.all_gather(geometry, 'row', axis=2, tiled=True)  20.7 us
    slice x2, local copies, waits for them, and re-layouts, complex_block(): imag_part = vectors[:, 1].reshape(pair_count, branches, branches)  17.6 us
    another operation x2, other arithmetic, complex_block(): return jnp.stack([upper_row, lower_row], axis=1)  9.22 us
    dot_general x1, matrix products, strengths(): jnp.einsum('knibc,koicm->knobm', shaped, complex_block(second_vectors, br...  8.12 us
    another operation x3, local copies, waits for them, and re-layouts, complex_block(): upper_row = jnp.stack([real_part, -imag_part], axis=1)  6.96 us
    dot_general x1, matrix products, body(): jnp.einsum('kuir,nirx->knux', rotation, shard_block, precision=HIGHEST)  6.41 us
  transfers between devices with their start and end apart: 2, of which 1 were waited for; matrix products, arithmetic and copies ran while one was open for 24% of the time, Pallas kernels for 0%

commit v1 on v0

v1 whole, which is shorter than its diff:
```python
import functools
import math

import jax
import jax.numpy as jnp
import numpy as np
from jax import lax
from jax.experimental import pallas as pl
from jax.experimental.pallas import tpu as pltpu
from jax.sharding import PartitionSpec as P

G = 32
FULL_TURN = 2.0 * math.pi
LANES = 128
F32 = jnp.float32
BF16 = jnp.bfloat16
VMEM = pltpu.VMEM
SMEM = pltpu.SMEM


def split(x):
    hi = x.astype(BF16)
    lo = (x - hi.astype(F32)).astype(BF16)
    return hi, lo


def dot(a, b):
    return jnp.dot(a, b, preferred_element_type=F32)


def pack_kernel(bands, slots, ids, owner, trip, center, modes, out):
    row, ba = ids[0], ids[1]
    out[...] = jnp.zeros_like(out)
    mine = (owner[0] == row).astype(F32)
    width = modes.shape[-1]
    order = [j for j in range(bands) if j % 2 == 0] + [j for j in range(bands) if j % 2]
    for place, j in enumerate(order):
        for s in range(2):
            line = modes[s, pl.ds(lax.bitwise_xor(ba, j), 1), :]
            out[pl.ds(place * 2 + s, 1), 0:width] = line * mine
    lane = lax.broadcasted_iota(jnp.int32, (1, LANES), 1)
    for r in range(slots):
        entry = jnp.zeros((1, LANES), jnp.int32)
        shift = 0
        for d in range(3):
            entry = jnp.where(lane == d, trip[r, d] - trip[r, 3 + d], entry)
            shift = shift + trip[r, 3 + d] * center[d]
        entry = jnp.where(lane == 3, shift, entry)
        out[pl.ds(2 * bands + row * slots + r, 1), :] = entry.astype(F32)


def pack(modes, owner, trip, center, ids, bands, slots, total):
    rows = 2 * bands + -(-total // 8) * 8
    return pl.pallas_call(
        functools.partial(pack_kernel, bands, slots),
        out_shape=jax.ShapeDtypeStruct((rows, LANES), F32),
        in_specs=[pl.BlockSpec(memory_space=SMEM)] * 4 + [pl.BlockSpec(memory_space=VMEM)],
        out_specs=pl.BlockSpec(memory_space=VMEM),
        name="pack",
    )(ids, owner, trip, center, modes)


def contract_kernel(bands, slots, lines, live, e0, e1, const, keep, send):
    width = const.shape[1]
    total = e0[...] + e1[...]
    eigen = total[0 : 2 * bands, 0:width]
    chunk = 3 * LANES
    for r in range(slots):
        weight = (r < live[0]).astype(F32)
        eh, el = split(eigen * weight)
        ch, cl = split(const[r])
        both = dot(jnp.concatenate([eh, el], axis=0), ch)
        res = both[0 : 2 * bands] + both[2 * bands :] + dot(eh, cl)
        for q in range(lines):
            part = res[:, q * chunk : (q + 1) * chunk]
            keep[:, r, q, :] = part[0:bands]
            send[:, r, q, :] = part[bands:]


def contract(constants, e0, e1, live, bands):
    slots, width, bb = constants.shape
    chunk = 3 * LANES
    pairs = bb // chunk
    lines = 8
    out = jax.ShapeDtypeStruct((bands, slots, pairs, chunk), F32)
    whole = pl.BlockSpec(e0.shape, lambda i: (0, 0))
    return pl.pallas_call(
        functools.partial(contract_kernel, bands, slots, lines),
        out_shape=(out, out),
        grid=(pairs // lines,),
        in_specs=[
            pl.BlockSpec(memory_space=SMEM),
            whole,
            whole,
            pl.BlockSpec((slots, width, lines * chunk), lambda i: (0, 0, i)),
        ],
        out_specs=[pl.BlockSpec((bands, slots, lines, chunk), lambda i: (0, 0, i, 0))] * 2,
        name="contract",
    )(live, e0, e1, constants)


def unpack_matrix(ref, s, size):
    half = size // 2
    step = 6
    j0, j1, j2 = (ref[0, pl.ds(2 * j + s, half, stride=step), :] for j in range(3))
    lane = lax.broadcasted_iota(jnp.int32, j0.shape, 1)
    r1 = pltpu.roll(j1, 64, 1)
    r2 = pltpu.roll(j2, 64, 1)
    return (j0, j1), (jnp.where(lane < 64, r1, r2), r2)


def join(a, b, size):
    return jnp.concatenate([a, b[:, 0 : size - LANES]], axis=1)


def prep_kernel(size, first, second, gh, gl, wh, wl, lo, hi):
    half = size // 2
    mats = []
    for s in range(2):
        even, odd = unpack_matrix(first, s, size)
        turned = jnp.concatenate([join(*even, size), join(*odd, size)], axis=0).T
        lo[...] = turned[:, 0:LANES]
        hi[:, 0 : size - LANES] = turned[:, LANES:size]
        rows = [
            join(lo[pl.ds(p, half, stride=2), :], hi[pl.ds(p, half, stride=2), :], size)
            for p in range(2)
        ]
        mats.append(jnp.concatenate(rows, axis=0))
    for i, m in enumerate((mats[0] + mats[1], mats[0], mats[1])):
        gh[0, i], gl[0, i] = split(m)
    mats = []
    for s in range(2):
        for p, (a, b) in enumerate(unpack_matrix(second, s, size)):
            lo[pl.ds(p, half, stride=2), :] = a
            hi[pl.ds(p, half, stride=2), :] = b
        mats.append(join(lo[...], hi[...], size))
    for i, m in enumerate((mats[0], mats[1] - mats[0], mats[0] + mats[1])):
        wh[0, i], wl[0, i] = split(m)


def prep(first, second, size):
    count, _, bb = first.shape
    tiles = bb // LANES

    def view(a):
        return a.reshape(count, 2, tiles, LANES).swapaxes(1, 2).reshape(count, 2 * tiles, LANES)

    out = jax.ShapeDtypeStruct((count, 3, size, size), BF16)
    return pl.pallas_call(
        functools.partial(prep_kernel, size),
        out_shape=(out,) * 4,
        grid=(count,),
        in_specs=[pl.BlockSpec((1, 2 * tiles, LANES), lambda k: (k, 0, 0))] * 2,
        out_specs=[pl.BlockSpec((1, 3, size, size), lambda k: (k, 0, 0, 0))] * 4,
        scratch_shapes=[VMEM((size, LANES), F32)] * 2,
        name="prep",
    )(view(first), view(second))


def final_kernel(spec, scale, size, *refs):
    blocks = refs[: len(spec)]
    cs, gh, gl, wh, wl, out, ph, plo, ares = refs[len(spec) :]
    half = size // 2
    k = pl.program_id(0)
    group = 16
    for g in range(half // group):
        q0 = g * group
        re = im = None
        for ref, (base, lines, slots) in zip(blocks, spec):
            if not base <= q0 < base + lines:
                continue
            local = pl.ds(q0 - base, group)
            if len(slots) <= 8:
                for t, slot in enumerate(slots):
                    c, s = cs[k, 2 * slot], cs[k, 2 * slot + 1]
                    a, b = ref[t, 0, local, :], ref[t, 1, local, :]
                    r_new, i_new = a * c - b * s, a * s + b * c
                    re = r_new if re is None else re + r_new
                    im = i_new if im is None else im + i_new
            else:
                zero = jnp.zeros((group, 3 * LANES), F32)

                def step(t, carry):
                    c, s = cs[k, 2 * t], cs[k, 2 * t + 1]
                    a, b = ref[t, 0, local, :], ref[t, 1, local, :]
                    return carry[0] + (a * c - b * s), carry[1] + (a * s + b * c)

                re, im = lax.fori_loop(0, len(slots), step, (zero, zero))
        for i, m in enumerate((re + im, re, im)):
            hi, lo = split(m)
            for base, lanes in ((0, slice(0, size)), (half, slice(size, 2 * size))):
                ph[i, pl.ds(base + q0, group), :] = hi[:, lanes]
                plo[i, pl.ds(base + q0, group), :] = lo[:, lanes]

    def triple(xh, xl, yh, yl):
        return dot(xh, yh) + dot(xl, yh) + dot(xh, yl)

    k1, k2, k3 = (triple(ph[i], plo[i], wh[0, i], wl[0, i]) for i in range(3))
    tr, ti = k1 - k3, k1 + k2
    terms = []
    for i, m in enumerate((tr, ti - tr, tr + ti)):
        mh, ml = split(m)
        terms.append(triple(gh[0, i], gl[0, i], mh, ml))
    ar, ai = terms[0] - terms[2], terms[0] + terms[1]
    ares[:, 0:size] = (ar * ar + ai * ai) * scale
    e0, e1 = ares[0:half, 0:LANES], ares[0:half, LANES : 2 * LANES]
    o0, o1 = ares[half:size, 0:LANES], ares[half:size, LANES : 2 * LANES]
    low = lax.broadcasted_iota(jnp.int32, e0.shape, 1) < 64
    r0, r1 = pltpu.roll(o0, 64, 1), pltpu.roll(o1, 64, 1)
    out[0, pl.ds(0, half, stride=3), :] = e0
    out[0, pl.ds(1, half, stride=3), :] = jnp.where(low, e1, r0)
    out[0, pl.ds(2, half, stride=3), :] = jnp.where(low, r0, r1)


def final(blocks, spec, cs, operands, total):
    count, _, size, _ = operands[0].shape
    tiles = size * size // LANES
    mats = [pl.BlockSpec((1, 3, size, size), lambda k: (k, 0, 0, 0))] * 4
    result = pl.pallas_call(
        functools.partial(final_kernel, spec, 1.0 / total, size),
        out_shape=jax.ShapeDtypeStruct((count, tiles, LANES), F32),
        grid=(count,),
        in_specs=[pl.BlockSpec(memory_space=VMEM)] * len(blocks)
        + [pl.BlockSpec(memory_space=SMEM)]
        + mats,
        out_specs=pl.BlockSpec((1, tiles, LANES), lambda k: (k, 0, 0)),
        scratch_shapes=[
            VMEM((3, size, size), BF16),
            VMEM((3, size, size), BF16),
            VMEM((size, 2 * LANES), F32),
        ],
        name="final",
    )(*blocks, cs, *operands)
    return result.reshape(count, 1, size * size)


def swap(x, axis, bit, n):
    return lax.ppermute(x, axis, [(i, i ^ bit) for i in range(n)])


def edges(n):
    cycle = list(range(0, n, 2)) + list(range(n - 1, 0, -2))
    even, odd = [], []
    for i in range(0, n, 2):
        a, b, c = cycle[i], cycle[i + 1], cycle[(i + 2) % n]
        even += [(a, b), (b, a)]
        odd += [(b, c), (c, b)]
    return even, odd


def neighbour_gather(parts, n):
    even, odd = edges(n)
    plans = ((even, odd), (odd, even))
    blocks, sources = [[p[None]] for p in parts], [[np.arange(n)[:, None]] for _ in parts]
    moving = [b[0] for b in blocks]
    held = [s[0] for s in sources]
    for step in range(n // 2):
        arrived = []
        for h, plan in enumerate(plans):
            perm = plan[step % 2]
            arrived.append(lax.ppermute(moving[h], "row", perm))
            source = np.zeros_like(held[h])
            for a, b in perm:
                source[b] = held[h][a]
            blocks[h].append(arrived[h])
            sources[h].append(source)
            if step == 0:
                held[h] = np.concatenate([held[h], source], axis=1)
            else:
                held[h] = source
        for h in range(2):
            moving[h] = (
                jnp.concatenate([moving[h], arrived[h]]) if step == 0 else arrived[h]
            )
    return blocks, [np.concatenate(s, axis=1) for s in sources]


def body(
    constants,
    current_modes,
    owner_id,
    live_count,
    triplets,
    center_point,
    pair_points,
    first_vectors,
    second_vectors,
):
    n_row, n_ba = lax.axis_size("row"), lax.axis_size("ba")
    slots, width, bb = constants.shape
    size = width * n_ba
    bands = current_modes.shape[-1]
    half = size // 2
    total = slots * n_row
    row, ba = lax.axis_index("row"), lax.axis_index("ba")
    ids = jnp.stack([row, ba]).astype(jnp.int32)

    modes = jnp.swapaxes(current_modes[0], 1, 2)
    payload = pack(modes, owner_id, triplets, center_point, ids, bands, slots, total)
    bit = 1
    while bit < n_row:
        other = swap(payload, "row", bit, n_row)
        bit *= 2
        if bit < n_row:
            payload = payload + other
    keep, send = contract(constants, payload, other, live_count, bands)
    geometry = (payload + other)[2 * bands : 2 * bands + total, 0:4].astype(jnp.int32)

    keep = keep.reshape(bands // 2, 2, slots, half, 2 * size)
    send = send.reshape(bands // 2, 2, slots, half, 2 * size)
    got = swap(send, "ba", 1, n_ba)
    far = swap(keep[1] + got[1], "ba", 2, n_ba)
    own = (keep[0] + got[0]) + far
    own = own.swapaxes(0, 1)

    turns = (
        jnp.sum(pair_points[:, :, None] * geometry.T[None, 0:3, :], axis=1)
        - geometry[:, 3][None, :]
    )
    angle = jnp.mod(turns, G).astype(F32) * (FULL_TURN / G)
    table = jnp.stack([jnp.cos(angle), jnp.sin(angle)], axis=-1)

    operands = prep(first_vectors, second_vectors, size)
    if slots == 1 and n_row <= 8:
        parts = (own[0, :, : half // 2], own[0, :, half // 2 :])
        blocks, sources = neighbour_gather(parts, n_row)
        order = jnp.asarray(np.concatenate(sources, axis=1))[row]
        table = table[:, order].reshape(table.shape[0], -1)
        arrays, spec = [], []
        for h in range(2):
            slot = h * n_row
            for b in blocks[h]:
                arrays.append(b)
                spec.append((h * half // 2, half // 2, tuple(range(slot, slot + b.shape[0]))))
                slot += b.shape[0]
    else:
        arrays = [lax.all_gather(own, "row", axis=0, tiled=True)]
        spec = [(0, half, tuple(range(total)))]
        table = table.reshape(table.shape[0], -1)
    return final(arrays, tuple(spec), table, operands, total)


def solution(mesh):
    return jax.shard_map(
        body,
        mesh=mesh,
        in_specs=(
            P("row", "ba", None),
            P("row", None, "ba", None),
            P(),
            P("row"),
            P("row", None),
            P(),
            P("row", None),
            P("row", None, None),
            P("row", None, None),
        ),
        out_specs=P("row", "ba", None),
        check_vma=False,
    )
```

time: 176 us -> 90.4 us (0.51); the launches traced: 173 us -> 89.7 us
  blocking collectives: 43.8 us -> 0 us
  local copies, waits for them, and re-layouts: 40.5 us -> 2.96 us
  Pallas kernels: 0 us -> 33.5 us
  matrix products: 26.4 us -> 0 us
  starting transfers between devices: 0.04 us -> 21.9 us
  between operations: 15.4 us -> 1.43 us
  waiting for transfers between devices: 34.3 us -> 25.7 us
  other arithmetic: 12.4 us -> 4.2 us
    unnamed x3 -> x0, waiting for transfers between devices: 34.3 us -> none
    pallas_call x0 -> x4, Pallas kernels: none -> 33.5 us  [the longest x1 13.9 us: final(): pl.pallas_call(functools.partial(final_kernel, spec, 1.0 / total, size),...]
    dot_general x4 -> x0, matrix products: 26.4 us -> none  [the longest x1 8.12 us: strengths(): jnp.einsum('knibc,koicm->knobm', shaped, complex_block(second_vectors, br...]
    ppermute x0 -> x13, waiting for transfers between devices: none -> 25.7 us  [the longest x5 14 us: swap(): return lax.ppermute(x, axis, [(i, i ^ bit) for i in range(n)])]
    psum x1 -> x0, blocking collectives: 23.1 us -> none  [broadcast(): return lax.psum(jnp.where(mine, shard, jnp.zeros_like(shard)), axis)]
    ppermute x0 -> x13, starting transfers between devices: none -> 21.9 us  [the longest x8 11.9 us: neighbour_gather(): arrived.append(lax.ppermute(moving[h], 'row', perm))]
    all_gather x1 -> x0, blocking collectives: 20.7 us -> none  [body(): shard_geometry = lax.all_gather(geometry, 'row', axis=2, tiled=True)]
    slice x4 -> x3, local copies, waits for them, and re-layouts: 18 us -> 0.29 us  [the longest x1 0.18 us: body(): geometry[:, 3][None, :]]
  transfers between devices with their start and end apart: 2 -> 13, of which waited for: 1 -> 11; matrix products, arithmetic and copies ran while one was open for 24% -> 3% of each run, Pallas kernels for 0% -> 10%
where the time goes in v1:
time: 90.4 us; the launch traced here: 89.7 us
  Pallas kernels  33.5 us (37%)
  waiting for transfers between devices  25.7 us (28%)
  starting transfers between devices  21.9 us (24%)
  other arithmetic  4.2 us (5%)
  local copies, waits for them, and re-layouts  2.96 us (3%)
  between operations  1.43 us (2%)
    ppermute x5, waiting for transfers between devices, swap(): return lax.ppermute(x, axis, [(i, i ^ bit) for i in range(n)])  14 us
    pallas_call x1, Pallas kernels, final(): pl.pallas_call(functools.partial(final_kernel, spec, 1.0 / total, size),...  13.9 us
    ppermute x8, starting transfers between devices, neighbour_gather(): arrived.append(lax.ppermute(moving[h], 'row', perm))  11.9 us
    ppermute x8, waiting for transfers between devices, neighbour_gather(): arrived.append(lax.ppermute(moving[h], 'row', perm))  11.7 us
    ppermute x5, starting transfers between devices, swap(): return lax.ppermute(x, axis, [(i, i ^ bit) for i in range(n)])  10 us
    pallas_call x1, Pallas kernels, contract(): pl.pallas_call(functools.partial(contract_kernel, bands, slots, lines), o...  9.52 us
    pallas_call x1, Pallas kernels, prep(): pl.pallas_call(functools.partial(prep_kernel, size), out_shape=(out,) * 4...  8.78 us
  transfers between devices with their start and end apart: 13, of which 11 were waited for; matrix products, arithmetic and copies ran while one was open for 3% of the time, Pallas kernels for 10%

profile of v1, /device:TPU:0, one launch (start us, length us, event | category | flops | bytes accessed | tf_op | source)
XLA Modules:
  0.0 89.7 jit_solution(1353235505148801832)
XLA Ops:
  0.7 0.6 pad_add_fusion.ids
  1.2 1.3 %pack.1 = f32[16,128]{1,0:T(8,128)} custom-call(s32[2]{0:T(128)} %pad_add_fusion.ids, s32[1]{0:T(128)S(6)} %copy.44.owner, s32[1,6]{1,0:T(1,128)} %trip.1, s32[3]{0:T(128)} %center.1, f32[2,4,48]{2,1,0:T(4,128)} %bitcast.57), custom_call_target="tpu_custom_call" | custom-call | tf_op jit(solution)/shard_map/pack/pallas_call | solution.py:54
  2.6 3.0 %collective-permute-start = (f32[16,128]{1,0:T(8,128)}, f32[16,128]{1,0:T(8,128)S(1)}, u32[]{:S(2)}, u32[]{:S(2)}) collective-permute-start(f32[16,128]{1,0:T(8,128)} %pack.1), channel_id=1, source_target_pairs={{0,4},{4,0},{8,12},{12,8},{16,20},{20,16},{24,28},{28,24},{1,5},{5... | collective-permute-start | bytes 24584 | tf_op jit(solution)/shard_map/ppermute | solution.py:238
  5.5 1.8 %collective-permute-done = f32[16,128]{1,0:T(8,128)S(1)} collective-permute-done((f32[16,128]{1,0:T(8,128)}, f32[16,128]{1,0:T(8,128)S(1)}, u32[]{:S(2)}, u32[]{:S(2)}) %collective-permute-start) | collective-permute-done | bytes 8224 | tf_op jit(solution)/shard_map/ppermute | solution.py:238
  7.4 0.7 add.52
  8.1 2.1 %collective-permute-start.1 = (f32[16,128]{1,0:T(8,128)S(1)}, f32[16,128]{1,0:T(8,128)S(1)}, u32[]{:S(2)}, u32[]{:S(2)}) collective-permute-start(f32[16,128]{1,0:T(8,128)S(1)} %add.52), channel_id=1, source_target_pairs={{0,8},{4,12},{8,0},{12,4},{16,24},{20,28},{24,16},{28,20},{1,9},{5... | collective-permute-start | bytes 24584 | tf_op jit(solution)/shard_map/ppermute | solution.py:238
  10.2 1.6 %collective-permute-done.1 = f32[16,128]{1,0:T(8,128)S(1)} collective-permute-done((f32[16,128]{1,0:T(8,128)S(1)}, f32[16,128]{1,0:T(8,128)S(1)}, u32[]{:S(2)}, u32[]{:S(2)}) %collective-permute-start.1) | collective-permute-done | bytes 8224 | tf_op jit(solution)/shard_map/ppermute | solution.py:238
  11.8 3.0 %collective-permute-start.2 = (f32[16,128]{1,0:T(8,128)S(1)}, f32[16,128]{1,0:T(8,128)S(1)}, u32[]{:S(2)}, u32[]{:S(2)}) collective-permute-start(f32[16,128]{1,0:T(8,128)S(1)} %add.53.e0), channel_id=1, source_target_pairs={{0,16},{4,20},{8,24},{12,28},{16,0},{20,4},{24,8},{28,12},{1,17},{... | collective-permute-start | bytes 24584 | tf_op jit(solution)/shard_map/ppermute | solution.py:238
  15.5 1.0 %collective-permute-done.2.e1 = f32[16,128]{1,0:T(8,128)S(1)} collective-permute-done((f32[16,128]{1,0:T(8,128)S(1)}, f32[16,128]{1,0:T(8,128)S(1)}, u32[]{:S(2)}, u32[]{:S(2)}) %collective-permute-start.2) | collective-permute-done | bytes 8224 | tf_op jit(solution)/shard_map/ppermute | solution.py:238
  16.5 0.6 copy-done.12
  17.1 9.5 %contract.1 = (f32[4,1,96,384]{3,2,1,0:T(8,128)}, f32[4,1,96,384]{3,2,1,0:T(8,128)}) custom-call(s32[1]{0:T(128)S(6)} %copy.45.live, f32[16,128]{1,0:T(8,128)} %copy-done.10, f32[16,128]{1,0:T(8,128)} %copy-done.12, f32[1,48,36864]{2,1,0:T(8,128)} %const.1), custom_call_target="tpu_custom_call" | custom-call | tf_op jit(solution)/shard_map/contract/pallas_call | solution.py:87
  26.6 0.0 collective-permute-start.3
  26.6 2.2 %collective-permute-done.3 = f32[2,2,1,96,384]{4,3,1,2,0:T(8,128)S(1)} collective-permute-done((f32[2,2,1,96,384]{4,3,1,2,0:T(8,128)}, f32[2,2,1,96,384]{4,3,1,2,0:T(8,128)S(1)}, u32[]{:S(2)}, u32[]{:S(2)}) %collective-permute-start.3) | collective-permute-done | bytes 589856 | tf_op jit(solution)/shard_map/ppermute | solution.py:238
  28.8 1.0 %fusion = f32[2,1,96,384]{3,2,0,1:T(8,128)S(1)} fusion(f32[2,2,1,96,384]{4,3,1,2,0:T(8,128)S(1)} %collective-permute-done.3, f32[4,1,96,384]{3,2,0,1:T(8,128)} %bitcast.53), kind=kLoop, calls=%fused_computation.2 | loop fusion | flops 73728 | bytes 884736 | tf_op jit(solution)/shard_map/add | solution.py:312
  29.8 1.9 %collective-permute-start.4 = (f32[2,1,96,384]{3,2,0,1:T(8,128)S(1)}, f32[2,1,96,384]{3,2,0,1:T(8,128)S(1)}, u32[]{:S(2)}, u32[]{:S(2)}) collective-permute-start(f32[2,1,96,384]{3,2,0,1:T(8,128)S(1)} %fusion), channel_id=1, source_target_pairs={{0,2},{1,3},{2,0},{3,1},{4,6},{5,7},{6,4},{7,5},{8,10},{9,11},{10,... | collective-permute-start | bytes 884744 | tf_op jit(solution)/shard_map/ppermute | solution.py:238
  31.7 7.3 %collective-permute-done.4 = f32[2,1,96,384]{3,2,0,1:T(8,128)S(1)} collective-permute-done((f32[2,1,96,384]{3,2,0,1:T(8,128)S(1)}, f32[2,1,96,384]{3,2,0,1:T(8,128)S(1)}, u32[]{:S(2)}, u32[]{:S(2)}) %collective-permute-start.4) | collective-permute-done | bytes 294944 | tf_op jit(solution)/shard_map/ppermute | solution.py:238
  39.0 1.0 %fusion.3 = f32[1,2,96,384]{3,2,1,0:T(8,128)S(1)} fusion(f32[2,1,96,384]{3,2,0,1:T(8,128)S(1)} %collective-permute-done.4, f32[2,2,1,96,384]{4,3,1,2,0:T(8,128)S(1)} %collective-permute-done.3, f32[4,1,96,384]{3,2,0,1:T(8,128)} %bitcast.54), kind=kLoop, calls=%fused_computation.6 | loop fusion | flops 147456 | bytes 1179648 | tf_op jit(solution)/shard_map/transpose | solution.py:314
  40.1 0.0 copy-start
  40.1 0.0 copy-start.1
  40.1 1.8 %collective-permute-start.9 = (f32[1,2,48,384]{3,2,1,0:T(8,128)S(1)}, f32[1,2,48,384]{3,2,1,0:T(8,128)S(1)}, u32[]{:S(2)}, u32[]{:S(2)}) collective-permute-start(f32[1,2,48,384]{3,2,1,0:T(8,128)S(1)} %get-tuple-element.17.refs_5_), channel_id=1, source_target_pairs={{8,16},{16,8},{24,28},{28,24},{20,12},{12,20},{4,0},{0,4},{9,17},{... | collective-permute-start | bytes 442376 | tf_op jit(solution)/shard_map/ppermute | solution.py:261
  41.9 1.7 %collective-permute-start.5 = (f32[1,2,48,384]{3,2,1,0:T(8,128)S(1)}, f32[1,2,48,384]{3,2,1,0:T(8,128)S(1)}, u32[]{:S(2)}, u32[]{:S(2)}) collective-permute-start(f32[1,2,48,384]{3,2,1,0:T(8,128)S(1)} %get-tuple-element.18.refs_0_), channel_id=1, source_target_pairs={{0,8},{8,0},{16,24},{24,16},{28,20},{20,28},{12,4},{4,12},{1,9},{9... | collective-permute-start | bytes 442376 | tf_op jit(solution)/shard_map/ppermute | solution.py:261
  43.5 1.8 %collective-permute-done.9.refs_6_ = f32[1,2,48,384]{3,2,1,0:T(8,128)S(1)} collective-permute-done((f32[1,2,48,384]{3,2,1,0:T(8,128)S(1)}, f32[1,2,48,384]{3,2,1,0:T(8,128)S(1)}, u32[]{:S(2)}, u32[]{:S(2)}) %collective-permute-start.9) | collective-permute-done | bytes 147488 | tf_op jit(solution)/shard_map/ppermute | solution.py:261
  45.3 1.9 %collective-permute-start.10 = (f32[2,2,48,384]{3,2,1,0:T(8,128)S(1)}, f32[2,2,48,384]{3,2,1,0:T(8,128)S(1)}, u32[]{:S(2)}, u32[]{:S(2)}) collective-permute-start(f32[2,2,48,384]{3,2,1,0:T(8,128)S(1)} %pad_maximum_fusion.1), channel_id=1, source_target_pairs={{0,8},{8,0},{16,24},{24,16},{28,20},{20,28},{12,4},{4,12},{1,9},{9... | collective-permute-start | bytes 884744 | tf_op jit(solution)/shard_map/ppermute | solution.py:261
  47.2 0.6 collective-permute-done.5.refs_1_
  47.8 1.0 %collective-permute-start.6 = (f32[2,2,48,384]{3,2,1,0:T(8,128)S(1)}, f32[2,2,48,384]{3,2,1,0:T(8,128)S(1)}, u32[]{:S(2)}, u32[]{:S(2)}) collective-permute-start(f32[2,2,48,384]{3,2,1,0:T(8,128)S(1)} %pad_maximum_fusion), channel_id=1, source_target_pairs={{8,16},{16,8},{24,28},{28,24},{20,12},{12,20},{4,0},{0,4},{9,17},{... | collective-permute-start | bytes 884744 | tf_op jit(solution)/shard_map/ppermute | solution.py:261
  48.8 8.8 %prep.1 = (bf16[8,3,192,192]{3,2,1,0:T(8,128)(2,1)}, bf16[8,3,192,192]{3,2,1,0:T(8,128)(2,1)}, bf16[8,3,192,192]{3,2,1,0:T(8,128)(2,1)}, bf16[8,3,192,192]{3,2,1,0:T(8,128)(2,1)}) custom-call(f32[8,576,128]{2,1,0:T(8,128)} %bitcast.51, f32[8,576,128]{2,1,0:T(8,128)} %bitcast.52), custom_call_target="tpu_custom_call" | custom-call | tf_op jit(solution)/shard_map/prep/pallas_call | solution.py:149
  57.6 0.0 copy-done.2
  57.6 0.0 copy-done.3
  57.6 0.7 fusion.10
  58.3 0.0 collective-permute-done.10.refs_7_
  58.3 1.2 %collective-permute-start.11 = (f32[2,2,48,384]{3,2,1,0:T(8,128)S(1)}, f32[2,2,48,384]{3,2,1,0:T(8,128)S(1)}, u32[]{:S(2)}, u32[]{:S(2)}) collective-permute-start(f32[2,2,48,384]{3,2,1,0:T(8,128)S(1)} %collective-permute-done.10.refs_7_), channel_id=1, source_target_pairs={{8,16},{16,8},{24,28},{28,24},{20,12},{12,20},{4,0},{0,4},{9,17},{... | collective-permute-start | bytes 884744 | tf_op jit(solution)/shard_map/ppermute | solution.py:261
  59.5 0.0 collective-permute-done.6.refs_2_
  59.5 1.6 %collective-permute-start.7 = (f32[2,2,48,384]{3,2,1,0:T(8,128)S(1)}, f32[2,2,48,384]{3,2,1,0:T(8,128)S(1)}, u32[]{:S(2)}, u32[]{:S(2)}) collective-permute-start(f32[2,2,48,384]{3,2,1,0:T(8,128)S(1)} %collective-permute-done.6.refs_2_), channel_id=1, source_target_pairs={{0,8},{8,0},{16,24},{24,16},{28,20},{20,28},{12,4},{4,12},{1,9},{9... | collective-permute-start | bytes 884744 | tf_op jit(solution)/shard_map/ppermute | solution.py:261
  61.2 0.1 copy.38
  61.3 0.2 slice_reduce_fusion
  61.5 0.1 multiply_reduce_fusion
  61.5 3.6 %collective-permute-done.11.refs_8_ = f32[2,2,48,384]{3,2,1,0:T(8,128)S(1)} collective-permute-done((f32[2,2,48,384]{3,2,1,0:T(8,128)S(1)}, f32[2,2,48,384]{3,2,1,0:T(8,128)S(1)}, u32[]{:S(2)}, u32[]{:S(2)}) %collective-permute-start.11) | collective-permute-done | bytes 294944 | tf_op jit(solution)/shard_map/ppermute | solution.py:261
  65.1 2.0 %collective-permute-start.12 = (f32[2,2,48,384]{3,2,1,0:T(8,128)S(1)}, f32[2,2,48,384]{3,2,1,0:T(8,128)S(1)}, u32[]{:S(2)}, u32[]{:S(2)}) collective-permute-start(f32[2,2,48,384]{3,2,1,0:T(8,128)S(1)} %collective-permute-done.11.refs_8_), channel_id=1, source_target_pairs={{0,8},{8,0},{16,24},{24,16},{28,20},{20,28},{12,4},{4,12},{1,9},{9... | collective-permute-start | bytes 884744 | tf_op jit(solution)/shard_map/ppermute | solution.py:261
  67.1 1.3 %collective-permute-done.7.refs_3_ = f32[2,2,48,384]{3,2,1,0:T(8,128)S(1)} collective-permute-done((f32[2,2,48,384]{3,2,1,0:T(8,128)S(1)}, f32[2,2,48,384]{3,2,1,0:T(8,128)S(1)}, u32[]{:S(2)}, u32[]{:S(2)}) %collective-permute-start.7) | collective-permute-done | bytes 294944 | tf_op jit(solution)/shard_map/ppermute | solution.py:261
  68.4 0.8 collective-permute-start.8
  69.2 0.1 fusion.9
  69.2 0.1 copy.39
  69.3 0.6 gather_fusion
  69.9 0.7 copy.42.refs_10_
  70.6 2.0 %collective-permute-done.12.refs_9_ = f32[2,2,48,384]{3,2,1,0:T(8,128)S(1)} collective-permute-done((f32[2,2,48,384]{3,2,1,0:T(8,128)S(1)}, f32[2,2,48,384]{3,2,1,0:T(8,128)S(1)}, u32[]{:S(2)}, u32[]{:S(2)}) %collective-permute-start.12) | collective-permute-done | bytes 294944 | tf_op jit(solution)/shard_map/ppermute | solution.py:261
  72.6 2.5 %collective-permute-done.8.refs_4_ = f32[2,2,48,384]{3,2,1,0:T(8,128)S(1)} collective-permute-done((f32[2,2,48,384]{3,2,1,0:T(8,128)S(1)}, f32[2,2,48,384]{3,2,1,0:T(8,128)S(1)}, u32[]{:S(2)}, u32[]{:S(2)}) %collective-permute-start.8) | collective-permute-done | bytes 294944 | tf_op jit(solution)/shard_map/ppermute | solution.py:261
  75.1 0.7 copy-done.9
  75.8 13.9 %final.1 = f32[8,288,128]{2,1,0:T(8,128)} custom-call(f32[1,2,48,384]{3,2,1,0:T(8,128)} %copy-done.1, f32[1,2,48,384]{3,2,1,0:T(8,128)} %copy-done.3, f32[2,2,48,384]{3,2,1,0:T(8,128)} %copy-done.5, f32[2,2,48,384]{3,2,1,0:T(8,128)} %copy-done.7, f32[2,2,48,384]{3,2,1,0:T(8,128)} %copy-done.9, f32[1,2,48,384]{3,2,1,0:T(8,128)} %copy-done, ...), custom_call_target="tpu_custom_call" | custom-call | tf_op jit(solution)/shard_map/final/pallas_call | solution.py:219
  (31 shorter events, 0.1 us)
Async XLA Ops:
  2.6 4.8 %collective-permute-start = (f32[16,128]{1,0:T(8,128)}, f32[16,128]{1,0:T(8,128)S(1)}, u32[]{:S(2)}, u32[]{:S(2)}) collective-permute-start(f32[16,128]{1,0:T(8,128)} %pack.1), channel_id=1, source_target_pairs={{0,4},{4,0},{8,12},{12,8},{16,20},{20,16},{24,28},{28,24},{1,5},{5... | collective-permute-start | bytes 24584 | tf_op jit(solution)/shard_map/ppermute | solution.py:238
  8.1 3.7 %collective-permute-start.1 = (f32[16,128]{1,0:T(8,128)S(1)}, f32[16,128]{1,0:T(8,128)S(1)}, u32[]{:S(2)}, u32[]{:S(2)}) collective-permute-start(f32[16,128]{1,0:T(8,128)S(1)} %add.52), channel_id=1, source_target_pairs={{0,8},{4,12},{8,0},{12,4},{16,24},{20,28},{24,16},{28,20},{1,9},{5... | collective-permute-start | bytes 24584 | tf_op jit(solution)/shard_map/ppermute | solution.py:238
  11.8 4.7 %copy-start.10 = (f32[16,128]{1,0:T(8,128)}, f32[16,128]{1,0:T(8,128)S(1)}, u32[]{:S(2)}) copy-start(f32[16,128]{1,0:T(8,128)S(1)} %add.53.e0) | copy-start | bytes 24580
  11.8 4.7 %collective-permute-start.2 = (f32[16,128]{1,0:T(8,128)S(1)}, f32[16,128]{1,0:T(8,128)S(1)}, u32[]{:S(2)}, u32[]{:S(2)}) collective-permute-start(f32[16,128]{1,0:T(8,128)S(1)} %add.53.e0), channel_id=1, source_target_pairs={{0,16},{4,20},{8,24},{12,28},{16,0},{20,4},{24,8},{28,12},{1,17},{... | collective-permute-start | bytes 24584 | tf_op jit(solution)/shard_map/ppermute | solution.py:238
  16.5 0.6 copy-start.12
  26.6 2.2 %collective-permute-start.3 = (f32[2,2,1,96,384]{4,3,1,2,0:T(8,128)}, f32[2,2,1,96,384]{4,3,1,2,0:T(8,128)S(1)}, u32[]{:S(2)}, u32[]{:S(2)}) collective-permute-start(f32[2,2,1,96,384]{4,3,1,2,0:T(8,128)} %bitcast.58), channel_id=1, source_target_pairs={{0,1},{1,0},{2,3},{3,2},{4,5},{5,4},{6,7},{7,6},{8,9},{9,8},{10,11... | collective-permute-start | bytes 1769480 | tf_op jit(solution)/shard_map/ppermute | solution.py:238
  29.8 9.2 %collective-permute-start.4 = (f32[2,1,96,384]{3,2,0,1:T(8,128)S(1)}, f32[2,1,96,384]{3,2,0,1:T(8,128)S(1)}, u32[]{:S(2)}, u32[]{:S(2)}) collective-permute-start(f32[2,1,96,384]{3,2,0,1:T(8,128)S(1)} %fusion), channel_id=1, source_target_pairs={{0,2},{1,3},{2,0},{3,1},{4,6},{5,7},{6,4},{7,5},{8,10},{9,11},{10,... | collective-permute-start | bytes 884744 | tf_op jit(solution)/shard_map/ppermute | solution.py:238
  40.1 17.5 %copy-start = (f32[1,2,48,384]{3,2,1,0:T(8,128)}, f32[1,2,48,384]{3,2,1,0:T(8,128)S(1)}, u32[]{:S(2)}) copy-start(f32[1,2,48,384]{3,2,1,0:T(8,128)S(1)} %get-tuple-element.17.refs_5_) | copy-start | bytes 442372
  40.1 17.5 %copy-start.1 = (f32[1,2,48,384]{3,2,1,0:T(8,128)}, f32[1,2,48,384]{3,2,1,0:T(8,128)S(1)}, u32[]{:S(2)}) copy-start(f32[1,2,48,384]{3,2,1,0:T(8,128)S(1)} %get-tuple-element.18.refs_0_) | copy-start | bytes 442372
  40.1 5.2 %collective-permute-start.9 = (f32[1,2,48,384]{3,2,1,0:T(8,128)S(1)}, f32[1,2,48,384]{3,2,1,0:T(8,128)S(1)}, u32[]{:S(2)}, u32[]{:S(2)}) collective-permute-start(f32[1,2,48,384]{3,2,1,0:T(8,128)S(1)} %get-tuple-element.17.refs_5_), channel_id=1, source_target_pairs={{8,16},{16,8},{24,28},{28,24},{20,12},{12,20},{4,0},{0,4},{9,17},{... | collective-permute-start | bytes 442376 | tf_op jit(solution)/shard_map/ppermute | solution.py:261
  41.9 5.9 %collective-permute-start.5 = (f32[1,2,48,384]{3,2,1,0:T(8,128)S(1)}, f32[1,2,48,384]{3,2,1,0:T(8,128)S(1)}, u32[]{:S(2)}, u32[]{:S(2)}) collective-permute-start(f32[1,2,48,384]{3,2,1,0:T(8,128)S(1)} %get-tuple-element.18.refs_0_), channel_id=1, source_target_pairs={{0,8},{8,0},{16,24},{24,16},{28,20},{20,28},{12,4},{4,12},{1,9},{9... | collective-permute-start | bytes 442376 | tf_op jit(solution)/shard_map/ppermute | solution.py:261
  45.3 12.3 %copy-start.2 = (f32[1,2,48,384]{3,2,1,0:T(8,128)}, f32[1,2,48,384]{3,2,1,0:T(8,128)S(1)}, u32[]{:S(2)}) copy-start(f32[1,2,48,384]{3,2,1,0:T(8,128)S(1)} %collective-permute-done.9.refs_6_) | copy-start | bytes 442372
  45.3 13.0 %collective-permute-start.10 = (f32[2,2,48,384]{3,2,1,0:T(8,128)S(1)}, f32[2,2,48,384]{3,2,1,0:T(8,128)S(1)}, u32[]{:S(2)}, u32[]{:S(2)}) collective-permute-start(f32[2,2,48,384]{3,2,1,0:T(8,128)S(1)} %pad_maximum_fusion.1), channel_id=1, source_target_pairs={{0,8},{8,0},{16,24},{24,16},{28,20},{20,28},{12,4},{4,12},{1,9},{9... | collective-permute-start | bytes 884744 | tf_op jit(solution)/shard_map/ppermute | solution.py:261
  47.8 9.8 %copy-start.3 = (f32[1,2,48,384]{3,2,1,0:T(8,128)}, f32[1,2,48,384]{3,2,1,0:T(8,128)S(1)}, u32[]{:S(2)}) copy-start(f32[1,2,48,384]{3,2,1,0:T(8,128)S(1)} %collective-permute-done.5.refs_1_) | copy-start | bytes 442372
  47.8 11.7 %collective-permute-start.6 = (f32[2,2,48,384]{3,2,1,0:T(8,128)S(1)}, f32[2,2,48,384]{3,2,1,0:T(8,128)S(1)}, u32[]{:S(2)}, u32[]{:S(2)}) collective-permute-start(f32[2,2,48,384]{3,2,1,0:T(8,128)S(1)} %pad_maximum_fusion), channel_id=1, source_target_pairs={{8,16},{16,8},{24,28},{28,24},{20,12},{12,20},{4,0},{0,4},{9,17},{... | collective-permute-start | bytes 884744 | tf_op jit(solution)/shard_map/ppermute | solution.py:261
  48.8 12.4 %copy-start.11 = (f32[16,128]{1,0:T(8,128)S(1)}, f32[16,128]{1,0:T(8,128)}, u32[]{:S(2)}) copy-start(f32[16,128]{1,0:T(8,128)} %copy-done.10) | copy-start | bytes 24580
  48.8 12.4 %copy-start.13 = (f32[16,128]{1,0:T(8,128)S(1)}, f32[16,128]{1,0:T(8,128)}, u32[]{:S(2)}) copy-start(f32[16,128]{1,0:T(8,128)} %copy-done.12) | copy-start | bytes 24580
  48.8 12.7 %copy-start.14 = (s32[8,3]{0,1:T(4,128)S(1)}, s32[8,3]{0,1:T(4,128)}, u32[]{:S(2)}) copy-start(s32[8,3]{0,1:T(4,128)} %param.16) | copy-start | bytes 292
  58.3 16.8 %copy-start.4 = (f32[2,2,48,384]{3,2,1,0:T(8,128)}, f32[2,2,48,384]{3,2,1,0:T(8,128)S(1)}, u32[]{:S(2)}) copy-start(f32[2,2,48,384]{3,2,1,0:T(8,128)S(1)} %collective-permute-done.10.refs_7_) | copy-start | bytes 884740
  58.3 6.8 %collective-permute-start.11 = (f32[2,2,48,384]{3,2,1,0:T(8,128)S(1)}, f32[2,2,48,384]{3,2,1,0:T(8,128)S(1)}, u32[]{:S(2)}, u32[]{:S(2)}) collective-permute-start(f32[2,2,48,384]{3,2,1,0:T(8,128)S(1)} %collective-permute-done.10.refs_7_), channel_id=1, source_target_pairs={{8,16},{16,8},{24,28},{28,24},{20,12},{12,20},{4,0},{0,4},{9,17},{... | collective-permute-start | bytes 884744 | tf_op jit(solution)/shard_map/ppermute | solution.py:261
  59.5 15.5 %copy-start.5 = (f32[2,2,48,384]{3,2,1,0:T(8,128)}, f32[2,2,48,384]{3,2,1,0:T(8,128)S(1)}, u32[]{:S(2)}) copy-start(f32[2,2,48,384]{3,2,1,0:T(8,128)S(1)} %collective-permute-done.6.refs_2_) | copy-start | bytes 884740
  59.5 8.8 %collective-permute-start.7 = (f32[2,2,48,384]{3,2,1,0:T(8,128)S(1)}, f32[2,2,48,384]{3,2,1,0:T(8,128)S(1)}, u32[]{:S(2)}, u32[]{:S(2)}) collective-permute-start(f32[2,2,48,384]{3,2,1,0:T(8,128)S(1)} %collective-permute-done.6.refs_2_), channel_id=1, source_target_pairs={{0,8},{8,0},{16,24},{24,16},{28,20},{20,28},{12,4},{4,12},{1,9},{9... | collective-permute-start | bytes 884744 | tf_op jit(solution)/shard_map/ppermute | solution.py:261
  65.1 10.0 %copy-start.6 = (f32[2,2,48,384]{3,2,1,0:T(8,128)}, f32[2,2,48,384]{3,2,1,0:T(8,128)S(1)}, u32[]{:S(2)}) copy-start(f32[2,2,48,384]{3,2,1,0:T(8,128)S(1)} %collective-permute-done.11.refs_8_) | copy-start | bytes 884740
  65.1 7.5 %collective-permute-start.12 = (f32[2,2,48,384]{3,2,1,0:T(8,128)S(1)}, f32[2,2,48,384]{3,2,1,0:T(8,128)S(1)}, u32[]{:S(2)}, u32[]{:S(2)}) collective-permute-start(f32[2,2,48,384]{3,2,1,0:T(8,128)S(1)} %collective-permute-done.11.refs_8_), channel_id=1, source_target_pairs={{0,8},{8,0},{16,24},{24,16},{28,20},{20,28},{12,4},{4,12},{1,9},{9... | collective-permute-start | bytes 884744 | tf_op jit(solution)/shard_map/ppermute | solution.py:261
  68.3 6.7 %copy-start.7 = (f32[2,2,48,384]{3,2,1,0:T(8,128)}, f32[2,2,48,384]{3,2,1,0:T(8,128)S(1)}, u32[]{:S(2)}) copy-start(f32[2,2,48,384]{3,2,1,0:T(8,128)S(1)} %collective-permute-done.7.refs_3_) | copy-start | bytes 884740
  68.4 6.7 %collective-permute-start.8 = (f32[2,2,48,384]{3,2,1,0:T(8,128)S(1)}, f32[2,2,48,384]{3,2,1,0:T(8,128)S(1)}, u32[]{:S(2)}, u32[]{:S(2)}) collective-permute-start(f32[2,2,48,384]{3,2,1,0:T(8,128)S(1)} %collective-permute-done.7.refs_3_), channel_id=1, source_target_pairs={{8,16},{16,8},{24,28},{28,24},{20,12},{12,20},{4,0},{0,4},{9,17},{... | collective-permute-start | bytes 884744 | tf_op jit(solution)/shard_map/ppermute | solution.py:261
  72.6 2.5 %copy-start.8 = (f32[2,2,48,384]{3,2,1,0:T(8,128)}, f32[2,2,48,384]{3,2,1,0:T(8,128)S(1)}, u32[]{:S(2)}) copy-start(f32[2,2,48,384]{3,2,1,0:T(8,128)S(1)} %collective-permute-done.12.refs_9_) | copy-start | bytes 884740
  75.1 0.7 copy-start.9

commit v2 on v0

v2 whole, which is shorter than its diff:
```python
import functools
import math

import jax
import jax.numpy as jnp
import numpy as np
from jax import lax
from jax.experimental import pallas as pl
from jax.experimental.pallas import tpu as pltpu
from jax.sharding import PartitionSpec as P

G = 32
FULL_TURN = 2.0 * math.pi
LANES = 128
F32 = jnp.float32
BF16 = jnp.bfloat16
VMEM = pltpu.VMEM
SMEM = pltpu.SMEM


def split(x):
    hi = x.astype(BF16)
    lo = (x - hi.astype(F32)).astype(BF16)
    return hi, lo


def dot(a, b):
    return jnp.dot(a, b, preferred_element_type=F32)


def in_vmem(*xs):
    return [pltpu.with_memory_space_constraint(x, VMEM) for x in xs]


def kept(shape, dtype=F32):
    return VMEM(shape, dtype)


WHOLE = pl.BlockSpec(memory_space=VMEM)
SCALARS = pl.BlockSpec(memory_space=SMEM)
RAW = pl.BlockSpec(memory_space=pltpu.HBM)


def limit(mib):
    return pltpu.CompilerParams(vmem_limit_bytes=mib << 20)


def pack_kernel(bands, slots, *refs):
    raw, out, (owner, trip, center, live, modes, sem) = refs[:5], refs[5], refs[6:]
    copies = [
        pltpu.make_async_copy(src, dst, sem.at[i])
        for i, (src, dst) in enumerate(zip(raw, (owner, trip, center, live, modes)))
    ]
    for c in copies:
        c.start()
    out[...] = jnp.zeros_like(out)
    for c in copies:
        c.wait()
    row, ba = lax.axis_index("row"), lax.axis_index("ba")
    mine = (owner[0] == row).astype(F32)
    width = modes.shape[-1]
    order = [j for j in range(bands) if j % 2 == 0] + [j for j in range(bands) if j % 2]
    for place, j in enumerate(order):
        for s in range(2):
            line = modes[s, pl.ds(lax.bitwise_xor(ba, j), 1), :]
            out[pl.ds(place * 2 + s, 1), 0:width] = line * mine
    lane = lax.broadcasted_iota(jnp.int32, (1, LANES), 1)
    for r in range(slots):
        shift = 0
        entry = jnp.where(lane == 4, (r < live[0]).astype(jnp.int32), 0)
        for d in range(3):
            entry = jnp.where(lane == d, trip[r, d] - trip[r, 3 + d], entry)
            shift = shift + trip[r, 3 + d] * center[d]
        entry = jnp.where(lane == 3, shift, entry)
        out[pl.ds(2 * bands + row * slots + r, 1), :] = entry.astype(F32)


def pack(modes, owner, trip, center, live, bands, slots, total):
    rows = 2 * bands + -(-total // 8) * 8
    ints = (owner, trip, center, live)
    return pl.pallas_call(
        functools.partial(pack_kernel, bands, slots),
        out_shape=kept((rows, LANES)),
        in_specs=[RAW] * 5,
        out_specs=WHOLE,
        scratch_shapes=[SMEM(x.shape, x.dtype) for x in ints]
        + [VMEM(modes.shape, F32), pltpu.SemaphoreType.DMA((5,))],
        compiler_params=limit(4),
        name="pack",
    )(*ints, modes)


def fetch_kernel(slots, first, rows, parts, const, hi, lo, buf, sem):
    width = const.shape[2] // parts
    copies = []
    for r in range(slots):
        for i in range(parts):
            lanes = pl.ds(i * width, width)
            copies.append(
                pltpu.make_async_copy(
                    const.at[r, pl.ds(first, rows), lanes], buf.at[r, :, lanes], sem.at[r, i]
                )
            )
    for c in copies:
        c.start()
    for n, c in enumerate(copies):
        c.wait()
        r, i = n // parts, n % parts
        lanes = slice(i * width, (i + 1) * width)
        hi[r, :, lanes], lo[r, :, lanes] = split(buf[r, :, lanes])


def fetch(constants, first, rows):
    slots, _, bb = constants.shape
    parts = 6
    return pl.pallas_call(
        functools.partial(fetch_kernel, slots, first, rows, parts),
        out_shape=(kept((slots, rows, bb), BF16),) * 2,
        in_specs=[RAW],
        out_specs=[WHOLE] * 2,
        scratch_shapes=[
            VMEM((slots, rows, bb), F32),
            pltpu.SemaphoreType.DMA((slots, parts)),
        ],
        compiler_params=limit(8),
        name="fetch",
    )(constants)


def contract_kernel(bands, slots, lines, e0, e1, *refs):
    pieces, (keep, send) = refs[:-2], refs[-2:]
    his, los = pieces[0::2], pieces[1::2]
    width = sum(h.shape[1] for h in his)
    total = e0[...] + e1[...]
    eigen = total[0 : 2 * bands, 0:width]
    pairs, chunk = keep.shape[2], keep.shape[3]
    low = lax.broadcasted_iota(jnp.int32, (2 * bands, LANES), 1) < 64
    for r in range(slots):
        own = pl.ds(2 * bands + lax.axis_index("row") * slots + r, 1)
        weight = e0[own, 4:5] + e1[own, 4:5]
        eh, el = split(eigen * weight)
        left = jnp.concatenate(
            [
                jnp.concatenate([eh, eh], axis=1),
                jnp.concatenate([el, jnp.zeros_like(el)], axis=1),
            ],
            axis=0,
        )
        for base in range(0, pairs, lines):
            lanes = slice(base * chunk, (base + lines) * chunk)
            right = jnp.concatenate(
                [h[r, :, lanes] for h in his] + [m[r, :, lanes] for m in los], axis=0
            )
            both = dot(left, right)
            res = both[0 : 2 * bands] + both[2 * bands :]
            for q in range(lines):
                j0, j1, j2 = (
                    res[:, q * chunk + j * LANES : q * chunk + (j + 1) * LANES]
                    for j in range(3)
                )
                t1 = jnp.where(low, j1, j2)
                t2 = jnp.where(low, pltpu.roll(j1, 64, 1), pltpu.roll(j2, 64, 1))
                for j, t in enumerate((j0, t1, t2)):
                    spot = slice(j * LANES, (j + 1) * LANES)
                    keep[:, r, base + q, spot] = t[0:bands]
                    send[:, r, base + q, spot] = t[bands:]


def contract(pieces, e0, e1, bands):
    slots, _, bb = pieces[0].shape
    chunk = 3 * LANES
    return pl.pallas_call(
        functools.partial(contract_kernel, bands, slots, 8),
        out_shape=(kept((bands, slots, bb // chunk, chunk)),) * 2,
        in_specs=[WHOLE] * (2 + len(pieces)),
        out_specs=[WHOLE] * 2,
        compiler_params=limit(8),
        name="contract",
    )(*in_vmem(e0, e1, *pieces))


def unpack_matrix(ref, k, s, size):
    half = size // 2
    j0, j1, j2 = (ref[k, pl.ds(2 * j + s, half, stride=6), :] for j in range(3))
    lane = lax.broadcasted_iota(jnp.int32, j0.shape, 1)
    r1 = pltpu.roll(j1, 64, 1)
    r2 = pltpu.roll(j2, 64, 1)
    return (j0, j1), (jnp.where(lane < 64, r1, r2), r2)


def join(a, b, size):
    return jnp.concatenate([a, b[:, 0 : size - LANES]], axis=1)


def prep_kernel(size, turn, raw, hi, lo, buf, sem, left, right):
    half = size // 2
    count = raw.shape[0]
    copies = [
        pltpu.make_async_copy(raw.at[k], buf.at[k], sem.at[k]) for k in range(count)
    ]
    for c in copies:
        c.start()
    for k in range(count):
        copies[k].wait()
        mats = []
        for s in range(2):
            even, odd = unpack_matrix(buf, k, s, size)
            if turn:
                turned = jnp.concatenate([join(*even, size), join(*odd, size)], axis=0).T
                left[...] = turned[:, 0:LANES]
                right[:, 0 : size - LANES] = turned[:, LANES:size]
                rows = [
                    join(
                        left[pl.ds(p, half, stride=2), :],
                        right[pl.ds(p, half, stride=2), :],
                        size,
                    )
                    for p in range(2)
                ]
                mats.append(jnp.concatenate(rows, axis=0))
            else:
                for p, (a, b) in enumerate((even, odd)):
                    left[pl.ds(p, half, stride=2), :] = a
                    right[pl.ds(p, half, stride=2), :] = b
                mats.append(join(left[...], right[...], size))
        re, im = mats
        three = (re + im, re, im) if turn else (re, im - re, re + im)
        for i, m in enumerate(three):
            hi[k, i], lo[k, i] = split(m)


def prep(vectors, size, turn):
    count, _, bb = vectors.shape
    tiles = bb // LANES
    view = vectors.reshape(count, 2, tiles, LANES).swapaxes(1, 2)
    view = view.reshape(count, 2 * tiles, LANES)
    return pl.pallas_call(
        functools.partial(prep_kernel, size, turn),
        out_shape=(kept((count, 3, size, size), BF16),) * 2,
        in_specs=[RAW],
        out_specs=[WHOLE] * 2,
        scratch_shapes=[
            VMEM(view.shape, F32),
            pltpu.SemaphoreType.DMA((count,)),
            VMEM((size, LANES), F32),
            VMEM((size, LANES), F32),
        ],
        compiler_params=limit(8),
        name="prep",
    )(view)


def angle_kernel(first, order, e0, e1, points, out):
    count, width = points.shape[1], len(order[0])
    row = lax.axis_index("row")
    lines = []
    for choice in zip(*order):
        if len(set(choice)) == 1:
            slot = choice[0]
        else:
            slot = sum(jnp.where(row == i, c, 0) for i, c in enumerate(choice))
        spot = pl.ds(first + slot, 1)
        lines.append(e0[spot, :] + e1[spot, :])
    lines = jnp.concatenate(lines, axis=0)
    cell = [jnp.broadcast_to(lines[:, d : d + 1], (width, LANES)) for d in range(4)]
    for k in range(count):
        turns = -cell[3]
        for d in range(3):
            turns = turns + cell[d] * points[d : d + 1, k : k + 1].astype(F32)
        turns = lax.rem(turns.astype(jnp.int32), G)
        turns = jnp.where(turns < 0, turns + G, turns)
        angle = turns.astype(F32) * (FULL_TURN / G)
        out[0, k * width : (k + 1) * width, :] = jnp.cos(angle)
        out[1, k * width : (k + 1) * width, :] = jnp.sin(angle)


def angles(e0, e1, points, first, order):
    lines = points.shape[0] * len(order[0])
    return pl.pallas_call(
        functools.partial(angle_kernel, first, order),
        out_shape=kept((2, lines, LANES)),
        in_specs=[WHOLE] * 3,
        out_specs=WHOLE,
        compiler_params=limit(4),
        name="angles",
    )(*in_vmem(e0, e1), points.T)


def rotated(refs, spec, cs, width, k, q0, group, re, im):
    for ref, (base, lines, slots) in zip(refs, spec):
        if not base <= q0 < base + lines:
            continue
        local = pl.ds(q0 - base, group)

        def turn(t, slot):
            spot = pl.ds(k * width + slot, 1)
            c, s = cs[0, spot, :], cs[1, spot, :]
            a, b = ref[t, 0, local, :], ref[t, 1, local, :]
            c, s = (jnp.concatenate([x] * 3, axis=1) for x in (c, s))
            return a * c - b * s, a * s + b * c

        if len(slots) <= 8:
            for t, slot in enumerate(slots):
                a, b = turn(t, slot)
                re = a if re is None else re + a
                im = b if im is None else im + b
        else:
            zero = jnp.zeros((group, 3 * LANES), F32)

            def step(t, carry):
                a, b = turn(t, t)
                return carry[0] + a, carry[1] + b

            start = (zero if re is None else re, zero if im is None else im)
            re, im = lax.fori_loop(0, len(slots), step, start)
    return re, im


def early_kernel(spec, width, group, *refs):
    blocks, cs, out = refs[: len(spec)], refs[-2], refs[-1]

    def one(k, carry):
        for q0 in range(0, out.shape[2], group):
            re, im = rotated(blocks, spec, cs, width, k, q0, group, None, None)
            out[k, 0, pl.ds(q0, group), :] = re
            out[k, 1, pl.ds(q0, group), :] = im
        return carry

    lax.fori_loop(0, out.shape[0], one, 0)


def early(blocks, spec, cs, count, half):
    width = cs.shape[1] // count
    return pl.pallas_call(
        functools.partial(early_kernel, spec, width, 8),
        out_shape=kept((count, 2, half, 3 * LANES)),
        in_specs=[WHOLE] * (len(blocks) + 1),
        out_specs=WHOLE,
        compiler_params=limit(4),
        name="early",
    )(*in_vmem(*blocks, cs))


def final_kernel(spec, width, scale, size, unroll, partial, *refs):
    blocks = refs[: len(spec)]
    cs, gh, gl, wh, wl, out, ph, plo = refs[len(spec) :]
    half = size // 2
    group = 16
    first = pl.program_id(0) * unroll

    def load(u):
        k = first + u
        for q0 in range(0, half, group):
            re, im = partial[k, 0, pl.ds(q0, group), :], partial[k, 1, pl.ds(q0, group), :]
            re, im = rotated(blocks, spec, cs, width, k, q0, group, re, im)
            for i, m in enumerate((re + im, re, im)):
                t0, t1, t2 = (m[:, j * LANES : (j + 1) * LANES] for j in range(3))
                for base, a, b in ((0, t0, t1), (half, t2, pltpu.roll(t1, 64, 1))):
                    spot = pl.ds(base + q0, group)
                    for dst, x, y in zip((ph, plo), split(a), split(b)):
                        dst[u, i, spot, 0:LANES] = x
                        dst[u, i, spot, LANES : 2 * LANES] = y

    def triple(xh, xl, yh, yl):
        both = dot(jnp.concatenate([xh, xl], axis=0), yh)
        return both[0:size] + both[size:] + dot(xh, yl)

    def inner(u):
        k = first + u
        k1, k2, k3 = (
            triple(ph[u, i][:, 0:size], plo[u, i][:, 0:size], wh[k, i], wl[k, i])
            for i in range(3)
        )
        return k1 - k3, k1 + k2

    def outer(u, re, im):
        k = first + u
        k1, k2, k3 = (
            triple(gh[k, i], gl[k, i], *split(m))
            for i, m in enumerate((re, im - re, re + im))
        )
        re, im = k1 - k3, k1 + k2
        return (re * re + im * im) * scale

    def store(u, value):
        tail = value[:, LANES:size]
        tail = jnp.concatenate([tail, tail], axis=1)
        turned = pltpu.roll(value[half:, 0:LANES], 64, 1)
        low = lax.broadcasted_iota(jnp.int32, turned.shape, 1) < 64
        out[u, pl.ds(0, half, stride=3), :] = value[0:half, 0:LANES]
        out[u, pl.ds(1, half, stride=3), :] = jnp.where(low, tail[0:half], turned)
        out[u, pl.ds(2, half, stride=3), :] = jnp.where(low, turned, tail[half:])

    for u in range(unroll):
        load(u)
    sums = [inner(u) for u in range(unroll)]
    for u in range(unroll):
        store(u, outer(u, *sums[u]))


def final(partial, blocks, spec, cs, operands, total):
    count, _, size, _ = operands[0].shape
    tiles = size * size // LANES
    unroll = 2 if count % 2 == 0 else 1
    result = pl.pallas_call(
        functools.partial(final_kernel, spec, cs.shape[1] // count, 1.0 / total, size, unroll),
        out_shape=jax.ShapeDtypeStruct((count, tiles, LANES), F32),
        grid=(count // unroll,),
        in_specs=[WHOLE] * (6 + len(blocks)),
        out_specs=pl.BlockSpec((unroll, tiles, LANES), lambda k: (k, 0, 0)),
        scratch_shapes=[VMEM((unroll, 3, size, 2 * LANES), BF16)] * 2,
        compiler_params=limit(16),
        name="final",
    )(*in_vmem(partial, *blocks, cs, *operands))
    return result.reshape(count, 1, size * size)


def swap(x, axis, bit, n):
    return lax.ppermute(x, axis, [(i, i ^ bit) for i in range(n)])


def edges(n):
    cycle = list(range(0, n, 2)) + list(range(n - 1, 0, -2))
    even, odd = [], []
    for i in range(0, n, 2):
        a, b, c = cycle[i], cycle[i + 1], cycle[(i + 2) % n]
        even += [(a, b), (b, a)]
        odd += [(b, c), (c, b)]
    return even, odd


def neighbour_gather(parts, n):
    even, odd = edges(n)
    plans = ((even, odd), (odd, even))
    moving = [p[None] for p in parts]
    held = [np.arange(n)[:, None] for _ in parts]
    blocks, sources = [[], []], [[], []]
    for step in range(n // 2):
        arrived = []
        for h, plan in enumerate(plans):
            perm = plan[step % 2]
            with jax.named_scope(f"ring{step}{'ab'[h]}"):
                arrived.append(lax.ppermute(moving[h], "row", perm))
            source = np.zeros_like(held[h])
            for a, b in perm:
                source[b] = held[h][a]
            if step == 0:
                source = np.concatenate([held[h], source], axis=1)
            held[h] = source
            sources[h].append(source)
        for h in range(2):
            if step == 0:
                arrived[h] = jnp.concatenate([moving[h], arrived[h]])
            moving[h] = arrived[h]
            blocks[h].append(moving[h])
    return blocks, [np.concatenate(s, axis=1) for s in sources]


def body(
    constants,
    current_modes,
    owner_id,
    live_count,
    triplets,
    center_point,
    pair_points,
    first_vectors,
    second_vectors,
):
    n_row, n_ba = lax.axis_size("row"), lax.axis_size("ba")
    slots, width, bb = constants.shape
    size = width * n_ba
    bands = current_modes.shape[-1]
    half = size // 2
    total = slots * n_row
    scope = jax.named_scope
    modes = jnp.swapaxes(current_modes[0], 1, 2)
    payload = pack(
        modes, owner_id, triplets, center_point, live_count, bands, slots, total
    )
    bit, hop = 1, 0
    while bit < n_row:
        with scope(f"hop{hop}"):
            other = swap(payload, "row", bit, n_row)
        bit, hop = bit * 2, hop + 1
        if bit < n_row:
            payload = payload + other
    cuts = 3 if width % 48 == 0 else 1
    pieces = []
    for i in range(cuts):
        with scope(f"fetch{i}"):
            pieces += fetch(constants, i * width // cuts, width // cuts)
    keep, send = contract(pieces, payload, other, bands)

    keep = keep.reshape(bands // 2, 2, slots, half, 2 * size)
    send = send.reshape(bands // 2, 2, slots, half, 2 * size)
    with scope("core"):
        got = swap(send, "ba", 1, n_ba)
    with scope("far"):
        far = swap(keep[1] + got[1], "ba", 2, n_ba)
    own = (keep[0] + got[0]) + far
    own = own.swapaxes(0, 1)

    with scope("weights"):
        weights = prep(second_vectors, size, False)
    with scope("lefts"):
        lefts = prep(first_vectors, size, True)
    operands = (*lefts, *weights)
    if slots == 1 and n_row <= 8:
        parts = (own[0, :, : half // 2], own[0, :, half // 2 :])
        blocks, sources = neighbour_gather(parts, n_row)
        order = np.concatenate(sources, axis=1)
        ahead, behind = [], []
        for h in range(2):
            slot = h * n_row
            for n, b in enumerate(blocks[h]):
                here = range(slot, slot + b.shape[0])
                entry = (b, (h * half // 2, half // 2, tuple(here)))
                (behind if n == len(blocks[h]) - 1 else ahead).append(entry)
                slot += b.shape[0]
    else:
        gathered = lax.all_gather(own, "row", axis=0, tiled=True)
        ahead, behind = [(gathered, (0, half, tuple(range(total))))], []
        order = np.broadcast_to(np.arange(total), (n_row, total))
    order = tuple(tuple(int(x) for x in line) for line in order)
    with scope("angles"):
        table = angles(payload, other, pair_points, 2 * bands, order)
    arrays, spec = zip(*ahead)
    with scope("early"):
        partial = early(arrays, spec, table, pair_points.shape[0], half)
    arrays, spec = zip(*behind) if behind else ((), ())
    return final(partial, arrays, spec, table, operands, total)


def solution(mesh):
    return jax.shard_map(
        body,
        mesh=mesh,
        in_specs=(
            P("row", "ba", None),
            P("row", None, "ba", None),
            P(),
            P("row"),
            P("row", None),
            P(),
            P("row", None),
            P("row", None, None),
            P("row", None, None),
        ),
        out_specs=P("row", "ba", None),
        check_vma=False,
    )
```

time: 176 us -> 70.4 us (0.40); the launches traced: 173 us -> 70.1 us
  blocking collectives: 43.8 us -> 0 us
  local copies, waits for them, and re-layouts: 40.5 us -> 5.04 us
  matrix products: 26.4 us -> 0 us
  starting transfers between devices: 0.04 us -> 18.7 us
  Pallas kernels: 0 us -> 18.3 us
  between operations: 15.4 us -> 1.47 us
  other arithmetic: 12.4 us -> 0.12 us
  waiting for transfers between devices: 34.3 us -> 26.5 us
    unnamed x3 -> x0, waiting for transfers between devices: 34.3 us -> none
    ppermute x0 -> x13, waiting for transfers between devices: none -> 26.5 us  [the longest x8 13.7 us: neighbour_gather(): arrived.append(lax.ppermute(moving[h], 'row', perm))]
    dot_general x4 -> x0, matrix products: 26.4 us -> none  [the longest x1 8.12 us: strengths(): jnp.einsum('knibc,koicm->knobm', shaped, complex_block(second_vectors, br...]
    psum x1 -> x0, blocking collectives: 23.1 us -> none  [broadcast(): return lax.psum(jnp.where(mine, shard, jnp.zeros_like(shard)), axis)]
    all_gather x1 -> x0, blocking collectives: 20.7 us -> none  [body(): shard_geometry = lax.all_gather(geometry, 'row', axis=2, tiled=True)]
    ppermute x0 -> x13, starting transfers between devices: none -> 18.7 us  [the longest x5 9.83 us: swap(): return lax.ppermute(x, axis, [(i, i ^ bit) for i in range(n)])]
    pallas_call x0 -> x10, Pallas kernels: none -> 18.3 us  [the longest x1 5.61 us: final(): pl.pallas_call(functools.partial(final_kernel, spec, cs.shape[1] // count...]
    slice x4 -> x1, local copies, waits for them, and re-layouts: 18 us -> 0.02 us  [body(): parts = (own[0, :, :half // 2], own[0, :, half // 2:])]
  transfers between devices with their start and end apart: 2 -> 13, of which waited for: 1 -> 10; matrix products, arithmetic and copies ran while one was open for 24% -> 0% of each run, Pallas kernels for 0% -> 15%
where the time goes in v2:
time: 70.4 us; the launch traced here: 70.1 us
  waiting for transfers between devices  26.5 us (38%)
  starting transfers between devices  18.7 us (27%)
  Pallas kernels  18.3 us (26%)
  local copies, waits for them, and re-layouts  5.04 us (7%)
  between operations  1.47 us (2%)
    ppermute x8, waiting for transfers between devices, neighbour_gather(): arrived.append(lax.ppermute(moving[h], 'row', perm))  13.7 us
    ppermute x5, waiting for transfers between devices, swap(): return lax.ppermute(x, axis, [(i, i ^ bit) for i in range(n)])  12.8 us
    ppermute x5, starting transfers between devices, swap(): return lax.ppermute(x, axis, [(i, i ^ bit) for i in range(n)])  9.83 us
    ppermute x8, starting transfers between devices, neighbour_gather(): arrived.append(lax.ppermute(moving[h], 'row', perm))  8.91 us
    pallas_call x1, Pallas kernels, final(): pl.pallas_call(functools.partial(final_kernel, spec, cs.shape[1] // count...  5.61 us
    pallas_call x2, Pallas kernels, prep(): pl.pallas_call(functools.partial(prep_kernel, size, turn), out_shape=(kep...  5.07 us
    unnamed x14, local copies, waits for them, and re-layouts  5.01 us
    pallas_call x3, Pallas kernels, fetch(): pl.pallas_call(functools.partial(fetch_kernel, slots, first, rows, parts)...  3.32 us
  transfers between devices with their start and end apart: 13, of which 10 were waited for; matrix products, arithmetic and copies ran while one was open for 0% of the time, Pallas kernels for 15%

profile of v2, /device:TPU:0, one launch (start us, length us, event | category | flops | bytes accessed | tf_op | source)
XLA Modules:
  0.0 70.1 jit_solution(898446734160004059)
XLA Ops:
  1.3 0.0 copy-start.3
  1.3 0.7 copy-done.3
  2.0 0.0 copy-start.5
  2.0 0.7 copy-done.5
  2.6 0.0 copy-start.6
  2.6 0.7 copy-done.6
  3.3 0.6 pack.1
  3.9 3.0 %collective-permute-start = (f32[16,128]{1,0:T(8,128)S(1)}, f32[16,128]{1,0:T(8,128)S(1)}, u32[]{:S(2)}, u32[]{:S(2)}) collective-permute-start(f32[16,128]{1,0:T(8,128)S(1)} %pack.1), channel_id=1, source_target_pairs={{0,4},{4,0},{8,12},{12,8},{16,20},{20,16},{24,28},{28,24},{1,5},{5... | collective-permute-start | bytes 24584 | tf_op jit(solution)/shard_map/hop0/ppermute | solution.py:419
  7.0 1.6 %collective-permute-done = f32[16,128]{1,0:T(8,128)S(1)} collective-permute-done((f32[16,128]{1,0:T(8,128)S(1)}, f32[16,128]{1,0:T(8,128)S(1)}, u32[]{:S(2)}, u32[]{:S(2)}) %collective-permute-start) | collective-permute-done | bytes 8224 | tf_op jit(solution)/shard_map/hop0/ppermute | solution.py:419
  8.6 2.1 %collective-permute-start.1 = (f32[16,128]{1,0:T(8,128)S(1)}, f32[16,128]{1,0:T(8,128)S(1)}, u32[]{:S(2)}, u32[]{:S(2)}) collective-permute-start(f32[16,128]{1,0:T(8,128)S(1)} %add.19), channel_id=1, source_target_pairs={{0,8},{4,12},{8,0},{12,4},{16,24},{20,28},{24,16},{28,20},{1,9},{5... | collective-permute-start | bytes 24584 | tf_op jit(solution)/shard_map/hop1/ppermute | solution.py:419
  10.7 1.6 %collective-permute-done.1 = f32[16,128]{1,0:T(8,128)S(1)} collective-permute-done((f32[16,128]{1,0:T(8,128)S(1)}, f32[16,128]{1,0:T(8,128)S(1)}, u32[]{:S(2)}, u32[]{:S(2)}) %collective-permute-start.1) | collective-permute-done | bytes 8224 | tf_op jit(solution)/shard_map/hop1/ppermute | solution.py:419
  12.3 3.0 %collective-permute-start.2 = (f32[16,128]{1,0:T(8,128)S(1)}, f32[16,128]{1,0:T(8,128)S(1)}, u32[]{:S(2)}, u32[]{:S(2)}) collective-permute-start(f32[16,128]{1,0:T(8,128)S(1)} %add.20.e0), channel_id=1, source_target_pairs={{0,16},{4,20},{8,24},{12,28},{16,0},{20,4},{24,8},{28,12},{1,17},{... | collective-permute-start | bytes 24584 | tf_op jit(solution)/shard_map/hop2/ppermute | solution.py:419
  15.4 3.0 %copy-done = f32[1,48,36864]{2,1,0:T(8,128)S(1)} copy-done((f32[1,48,36864]{2,1,0:T(8,128)S(1)}, f32[1,48,36864]{2,1,0:T(8,128)}, u32[]{:S(2)}) %copy-start) | copy-done | bytes 7077912
  18.4 1.1 %fetch.3 = (bf16[1,16,36864]{2,1,0:T(8,128)(2,1)S(1)}, bf16[1,16,36864]{2,1,0:T(8,128)(2,1)S(1)}) custom-call(f32[1,48,36864]{2,1,0:T(8,128)S(1)} %copy-done), custom_call_target="tpu_custom_call" | custom-call | tf_op jit(solution)/shard_map/fetch0/fetch/pallas_call | solution.py:116
  19.5 1.1 %fetch.5 = (bf16[1,16,36864]{2,1,0:T(8,128)(2,1)S(1)}, bf16[1,16,36864]{2,1,0:T(8,128)(2,1)S(1)}) custom-call(f32[1,48,36864]{2,1,0:T(8,128)S(1)} %copy-done), custom_call_target="tpu_custom_call" | custom-call | tf_op jit(solution)/shard_map/fetch2/fetch/pallas_call | solution.py:116
  20.6 1.1 %fetch.4 = (bf16[1,16,36864]{2,1,0:T(8,128)(2,1)S(1)}, bf16[1,16,36864]{2,1,0:T(8,128)(2,1)S(1)}) custom-call(f32[1,48,36864]{2,1,0:T(8,128)S(1)} %copy-done), custom_call_target="tpu_custom_call" | custom-call | tf_op jit(solution)/shard_map/fetch1/fetch/pallas_call | solution.py:116
  21.7 0.0 collective-permute-done.2.e1
  21.7 1.4 %contract.1 = (f32[4,1,96,384]{3,2,1,0:T(8,128)S(1)}, f32[4,1,96,384]{3,2,1,0:T(8,128)S(1)}) custom-call(f32[16,128]{1,0:T(8,128)S(1)} %add.20.e0, f32[16,128]{1,0:T(8,128)S(1)} %collective-permute-done.2.e1, bf16[1,16,36864]{2,1,0:T(8,128)(2,1)S(1)} %get-tuple-element.17.refs_0_, bf16[1,16,36864]{2,1,0:T(8,128)(2,1)S(1)} %get-tuple-element.18.refs_1_, ...), custom_call_target="tpu_custom_call" | custom-call | tf_op jit(solution)/shard_map/contract/pallas_call | solution.py:172
  23.1 0.0 copy-start.1
  23.1 0.1 collective-permute-start.3
  23.2 2.0 %collective-permute-done.3 = f32[2,2,1,96,384]{4,3,1,2,0:T(8,128)S(1)} collective-permute-done((f32[2,2,1,96,384]{4,3,1,2,0:T(8,128)S(1)}, f32[2,2,1,96,384]{4,3,1,2,0:T(8,128)S(1)}, u32[]{:S(2)}, u32[]{:S(2)}) %collective-permute-start.3) | collective-permute-done | bytes 589856 | tf_op jit(solution)/shard_map/core/ppermute | solution.py:419
  25.2 1.6 %collective-permute-start.4 = (f32[2,1,96,384]{3,2,0,1:T(8,128)S(1)}, f32[2,1,96,384]{3,2,0,1:T(8,128)S(1)}, u32[]{:S(2)}, u32[]{:S(2)}) collective-permute-start(f32[2,1,96,384]{3,2,0,1:T(8,128)S(1)} %fusion), channel_id=1, source_target_pairs={{0,2},{1,3},{2,0},{3,1},{4,6},{5,7},{6,4},{7,5},{8,10},{9,11},{10,... | collective-permute-start | bytes 884744 | tf_op jit(solution)/shard_map/far/ppermute | solution.py:419
  26.8 7.5 %collective-permute-done.4 = f32[2,1,96,384]{3,2,0,1:T(8,128)S(1)} collective-permute-done((f32[2,1,96,384]{3,2,0,1:T(8,128)S(1)}, f32[2,1,96,384]{3,2,0,1:T(8,128)S(1)}, u32[]{:S(2)}, u32[]{:S(2)}) %collective-permute-start.4) | collective-permute-done | bytes 294944 | tf_op jit(solution)/shard_map/far/ppermute | solution.py:419
  34.4 0.0 copy-start.2
  34.4 1.6 %collective-permute-start.5 = (f32[1,2,48,384]{3,2,1,0:T(8,128)S(1)}, f32[1,2,48,384]{3,2,1,0:T(8,128)S(1)}, u32[]{:S(2)}, u32[]{:S(2)}) collective-permute-start(f32[1,2,48,384]{3,2,1,0:T(8,128)S(1)} %get-tuple-element.30), channel_id=1, source_target_pairs={{0,8},{8,0},{16,24},{24,16},{28,20},{20,28},{12,4},{4,12},{1,9},{9... | collective-permute-start | bytes 442376 | tf_op jit(solution)/shard_map/ring0a/ppermute | solution.py:443
  36.1 1.5 %collective-permute-start.8 = (f32[1,2,48,384]{3,2,1,0:T(8,128)S(1)}, f32[1,2,48,384]{3,2,1,0:T(8,128)S(1)}, u32[]{:S(2)}, u32[]{:S(2)}) collective-permute-start(f32[1,2,48,384]{3,2,1,0:T(8,128)S(1)} %get-tuple-element.29), channel_id=1, source_target_pairs={{8,16},{16,8},{24,28},{28,24},{20,12},{12,20},{4,0},{0,4},{9,17},{... | collective-permute-start | bytes 442376 | tf_op jit(solution)/shard_map/ring0b/ppermute | solution.py:443
  37.6 2.1 %collective-permute-done.5 = f32[1,2,48,384]{3,2,1,0:T(8,128)S(1)} collective-permute-done((f32[1,2,48,384]{3,2,1,0:T(8,128)S(1)}, f32[1,2,48,384]{3,2,1,0:T(8,128)S(1)}, u32[]{:S(2)}, u32[]{:S(2)}) %collective-permute-start.5) | collective-permute-done | bytes 147488 | tf_op jit(solution)/shard_map/ring0a/ppermute | solution.py:443
  39.7 1.6 %collective-permute-start.6 = (f32[2,2,48,384]{3,2,1,0:T(8,128)S(1)}, f32[2,2,48,384]{3,2,1,0:T(8,128)S(1)}, u32[]{:S(2)}, u32[]{:S(2)}) collective-permute-start(f32[2,2,48,384]{3,2,1,0:T(8,128)S(1)} %pad_maximum_fusion.refs_0_), channel_id=1, source_target_pairs={{8,16},{16,8},{24,28},{28,24},{20,12},{12,20},{4,0},{0,4},{9,17},{... | collective-permute-start | bytes 884744 | tf_op jit(solution)/shard_map/ring1a/ppermute | solution.py:443
  41.2 0.8 %collective-permute-done.8 = f32[1,2,48,384]{3,2,1,0:T(8,128)S(1)} collective-permute-done((f32[1,2,48,384]{3,2,1,0:T(8,128)S(1)}, f32[1,2,48,384]{3,2,1,0:T(8,128)S(1)}, u32[]{:S(2)}, u32[]{:S(2)}) %collective-permute-start.8) | collective-permute-done | bytes 147488 | tf_op jit(solution)/shard_map/ring0b/ppermute | solution.py:443
  42.0 0.1 collective-permute-start.9
  42.1 5.5 %collective-permute-done.6.refs_1_ = f32[2,2,48,384]{3,2,1,0:T(8,128)S(1)} collective-permute-done((f32[2,2,48,384]{3,2,1,0:T(8,128)S(1)}, f32[2,2,48,384]{3,2,1,0:T(8,128)S(1)}, u32[]{:S(2)}, u32[]{:S(2)}) %collective-permute-start.6) | collective-permute-done | bytes 294944 | tf_op jit(solution)/shard_map/ring1a/ppermute | solution.py:443
  47.5 0.8 %collective-permute-start.7 = (f32[2,2,48,384]{3,2,1,0:T(8,128)S(1)}, f32[2,2,48,384]{3,2,1,0:T(8,128)S(1)}, u32[]{:S(2)}, u32[]{:S(2)}) collective-permute-start(f32[2,2,48,384]{3,2,1,0:T(8,128)S(1)} %collective-permute-done.6.refs_1_), channel_id=1, source_target_pairs={{0,8},{8,0},{16,24},{24,16},{28,20},{20,28},{12,4},{4,12},{1,9},{9... | collective-permute-start | bytes 884744 | tf_op jit(solution)/shard_map/ring2a/ppermute | solution.py:443
  48.4 1.1 %collective-permute-done.9.refs_4_ = f32[2,2,48,384]{3,2,1,0:T(8,128)S(1)} collective-permute-done((f32[2,2,48,384]{3,2,1,0:T(8,128)S(1)}, f32[2,2,48,384]{3,2,1,0:T(8,128)S(1)}, u32[]{:S(2)}, u32[]{:S(2)}) %collective-permute-start.9) | collective-permute-done | bytes 294944 | tf_op jit(solution)/shard_map/ring1b/ppermute | solution.py:443
  49.4 1.5 %collective-permute-start.10 = (f32[2,2,48,384]{3,2,1,0:T(8,128)S(1)}, f32[2,2,48,384]{3,2,1,0:T(8,128)S(1)}, u32[]{:S(2)}, u32[]{:S(2)}) collective-permute-start(f32[2,2,48,384]{3,2,1,0:T(8,128)S(1)} %collective-permute-done.9.refs_4_), channel_id=1, source_target_pairs={{8,16},{16,8},{24,28},{28,24},{20,12},{12,20},{4,0},{0,4},{9,17},{... | collective-permute-start | bytes 884744 | tf_op jit(solution)/shard_map/ring2b/ppermute | solution.py:443
  50.9 4.2 %collective-permute-done.7.refs_2_ = f32[2,2,48,384]{3,2,1,0:T(8,128)S(1)} collective-permute-done((f32[2,2,48,384]{3,2,1,0:T(8,128)S(1)}, f32[2,2,48,384]{3,2,1,0:T(8,128)S(1)}, u32[]{:S(2)}, u32[]{:S(2)}) %collective-permute-start.7) | collective-permute-done | bytes 294944 | tf_op jit(solution)/shard_map/ring2a/ppermute | solution.py:443
  55.1 1.5 %collective-permute-start.11 = (f32[2,2,48,384]{3,2,1,0:T(8,128)S(1)}, f32[2,2,48,384]{3,2,1,0:T(8,128)S(1)}, u32[]{:S(2)}, u32[]{:S(2)}) collective-permute-start(f32[2,2,48,384]{3,2,1,0:T(8,128)S(1)} %collective-permute-done.7.refs_2_), channel_id=1, source_target_pairs={{8,16},{16,8},{24,28},{28,24},{20,12},{12,20},{4,0},{0,4},{9,17},{... | collective-permute-start | bytes 884744 | tf_op jit(solution)/shard_map/ring3a/ppermute | solution.py:443
  56.6 0.2 collective-permute-done.10.refs_5_
  56.8 0.4 collective-permute-start.12
  57.1 0.0 copy-done.1
  57.1 2.9 %prep.2 = (bf16[8,3,192,192]{3,2,1,0:T(8,128)(2,1)S(1)}, bf16[8,3,192,192]{3,2,1,0:T(8,128)(2,1)S(1)}) custom-call(f32[8,576,128]{2,1,0:T(8,128)S(1)} %bitcast.31), custom_call_target="tpu_custom_call" | custom-call | tf_op jit(solution)/shard_map/lefts/prep/pallas_call | solution.py:237
  60.1 0.0 copy-done.2
  60.1 2.2 %prep.3 = (bf16[8,3,192,192]{3,2,1,0:T(8,128)(2,1)S(1)}, bf16[8,3,192,192]{3,2,1,0:T(8,128)(2,1)S(1)}) custom-call(f32[8,576,128]{2,1,0:T(8,128)S(1)} %bitcast.32), custom_call_target="tpu_custom_call" | custom-call | tf_op jit(solution)/shard_map/weights/prep/pallas_call | solution.py:237
  62.2 0.0 copy-done.4
  62.3 0.4 angles.1.refs_6_.refs_2_
  62.7 1.8 %early.1.partial = f32[8,2,96,384]{3,2,1,0:T(8,128)S(1)} custom-call(f32[2,2,48,384]{3,2,1,0:T(8,128)S(1)} %pad_maximum_fusion.refs_0_, f32[2,2,48,384]{3,2,1,0:T(8,128)S(1)} %collective-permute-done.6.refs_1_, f32[2,2,48,384]{3,2,1,0:T(8,128)S(1)} %collective-permute-done.7.refs_2_, f32[2,2,48,384]{3,2,1,0:T(8,128)S(1)} %pad_maximum_fusion.1.refs_3_, ...), custom_call_target="tpu_custom_call" | custom-call | tf_op jit(solution)/shard_map/early/early/pallas_call | solution.py:334
  64.5 0.0 collective-permute-done.11.refs_0_
  64.5 0.0 collective-permute-done.12.refs_1_
  64.5 5.6 %final.1 = f32[8,288,128]{2,1,0:T(8,128)} custom-call(f32[8,2,96,384]{3,2,1,0:T(8,128)S(1)} %early.1.partial, f32[2,2,48,384]{3,2,1,0:T(8,128)S(1)} %collective-permute-done.11.refs_0_, f32[2,2,48,384]{3,2,1,0:T(8,128)S(1)} %collective-permute-done.12.refs_1_, f32[2,128,128]{2,1,0:T(8,128)S(1)} %angles.1.refs_6_.refs_2_, ...), custom_call_target="tpu_custom_call" | custom-call | tf_op jit(solution)/shard_map/final/pallas_call | solution.py:405
  (9 shorter events, 0.1 us)
Async XLA Ops:
  1.3 0.7 copy-start.3
  2.0 0.7 copy-start.5
  2.6 0.7 copy-start.6
  3.9 4.7 %collective-permute-start = (f32[16,128]{1,0:T(8,128)S(1)}, f32[16,128]{1,0:T(8,128)S(1)}, u32[]{:S(2)}, u32[]{:S(2)}) collective-permute-start(f32[16,128]{1,0:T(8,128)S(1)} %pack.1), channel_id=1, source_target_pairs={{0,4},{4,0},{8,12},{12,8},{16,20},{20,16},{24,28},{28,24},{1,5},{5... | collective-permute-start | bytes 24584 | tf_op jit(solution)/shard_map/hop0/ppermute | solution.py:419
  8.6 3.7 %collective-permute-start.1 = (f32[16,128]{1,0:T(8,128)S(1)}, f32[16,128]{1,0:T(8,128)S(1)}, u32[]{:S(2)}, u32[]{:S(2)}) collective-permute-start(f32[16,128]{1,0:T(8,128)S(1)} %add.19), channel_id=1, source_target_pairs={{0,8},{4,12},{8,0},{12,4},{16,24},{20,28},{24,16},{28,20},{1,9},{5... | collective-permute-start | bytes 24584 | tf_op jit(solution)/shard_map/hop1/ppermute | solution.py:419
  12.3 9.4 %collective-permute-start.2 = (f32[16,128]{1,0:T(8,128)S(1)}, f32[16,128]{1,0:T(8,128)S(1)}, u32[]{:S(2)}, u32[]{:S(2)}) collective-permute-start(f32[16,128]{1,0:T(8,128)S(1)} %add.20.e0), channel_id=1, source_target_pairs={{0,16},{4,20},{8,24},{12,28},{16,0},{20,4},{24,8},{28,12},{1,17},{... | collective-permute-start | bytes 24584 | tf_op jit(solution)/shard_map/hop2/ppermute | solution.py:419
  15.4 3.0 %copy-start = (f32[1,48,36864]{2,1,0:T(8,128)S(1)}, f32[1,48,36864]{2,1,0:T(8,128)}, u32[]{:S(2)}) copy-start(f32[1,48,36864]{2,1,0:T(8,128)} %const.5) | copy-start | bytes 21233668
  23.1 34.0 %copy-start.1 = (f32[8,2,36864]{2,1,0:T(2,128)S(1)}, f32[8,2,36864]{2,1,0:T(2,128)}, u32[]{:S(2)}) copy-start(f32[8,2,36864]{2,1,0:T(2,128)} %param.16) | copy-start | bytes 7077892
  23.1 2.1 %collective-permute-start.3 = (f32[2,2,1,96,384]{4,3,1,2,0:T(8,128)S(1)}, f32[2,2,1,96,384]{4,3,1,2,0:T(8,128)S(1)}, u32[]{:S(2)}, u32[]{:S(2)}) collective-permute-start(f32[2,2,1,96,384]{4,3,1,2,0:T(8,128)S(1)} %bitcast.37), channel_id=1, source_target_pairs={{0,1},{1,0},{2,3},{3,2},{4,5},{5,4},{6,7},{7,6},{8,9},{9,8},{10,11... | collective-permute-start | bytes 1769480 | tf_op jit(solution)/shard_map/core/ppermute | solution.py:419
  25.2 9.1 %collective-permute-start.4 = (f32[2,1,96,384]{3,2,0,1:T(8,128)S(1)}, f32[2,1,96,384]{3,2,0,1:T(8,128)S(1)}, u32[]{:S(2)}, u32[]{:S(2)}) collective-permute-start(f32[2,1,96,384]{3,2,0,1:T(8,128)S(1)} %fusion), channel_id=1, source_target_pairs={{0,2},{1,3},{2,0},{3,1},{4,6},{5,7},{6,4},{7,5},{8,10},{9,11},{10,... | collective-permute-start | bytes 884744 | tf_op jit(solution)/shard_map/far/ppermute | solution.py:419
  34.4 25.7 %copy-start.2 = (f32[8,2,36864]{2,1,0:T(2,128)S(1)}, f32[8,2,36864]{2,1,0:T(2,128)}, u32[]{:S(2)}) copy-start(f32[8,2,36864]{2,1,0:T(2,128)} %param.17) | copy-start | bytes 7077892
  34.4 5.2 %collective-permute-start.5 = (f32[1,2,48,384]{3,2,1,0:T(8,128)S(1)}, f32[1,2,48,384]{3,2,1,0:T(8,128)S(1)}, u32[]{:S(2)}, u32[]{:S(2)}) collective-permute-start(f32[1,2,48,384]{3,2,1,0:T(8,128)S(1)} %get-tuple-element.30), channel_id=1, source_target_pairs={{0,8},{8,0},{16,24},{24,16},{28,20},{20,28},{12,4},{4,12},{1,9},{9... | collective-permute-start | bytes 442376 | tf_op jit(solution)/shard_map/ring0a/ppermute | solution.py:443
  36.1 5.9 %collective-permute-start.8 = (f32[1,2,48,384]{3,2,1,0:T(8,128)S(1)}, f32[1,2,48,384]{3,2,1,0:T(8,128)S(1)}, u32[]{:S(2)}, u32[]{:S(2)}) collective-permute-start(f32[1,2,48,384]{3,2,1,0:T(8,128)S(1)} %get-tuple-element.29), channel_id=1, source_target_pairs={{8,16},{16,8},{24,28},{28,24},{20,12},{12,20},{4,0},{0,4},{9,17},{... | collective-permute-start | bytes 442376 | tf_op jit(solution)/shard_map/ring0b/ppermute | solution.py:443
  39.7 7.9 %collective-permute-start.6 = (f32[2,2,48,384]{3,2,1,0:T(8,128)S(1)}, f32[2,2,48,384]{3,2,1,0:T(8,128)S(1)}, u32[]{:S(2)}, u32[]{:S(2)}) collective-permute-start(f32[2,2,48,384]{3,2,1,0:T(8,128)S(1)} %pad_maximum_fusion.refs_0_), channel_id=1, source_target_pairs={{8,16},{16,8},{24,28},{28,24},{20,12},{12,20},{4,0},{0,4},{9,17},{... | collective-permute-start | bytes 884744 | tf_op jit(solution)/shard_map/ring1a/ppermute | solution.py:443
  42.0 7.4 %collective-permute-start.9 = (f32[2,2,48,384]{3,2,1,0:T(8,128)S(1)}, f32[2,2,48,384]{3,2,1,0:T(8,128)S(1)}, u32[]{:S(2)}, u32[]{:S(2)}) collective-permute-start(f32[2,2,48,384]{3,2,1,0:T(8,128)S(1)} %pad_maximum_fusion.1.refs_3_), channel_id=1, source_target_pairs={{0,8},{8,0},{16,24},{24,16},{28,20},{20,28},{12,4},{4,12},{1,9},{9... | collective-permute-start | bytes 884744 | tf_op jit(solution)/shard_map/ring1b/ppermute | solution.py:443
  47.5 7.6 %collective-permute-start.7 = (f32[2,2,48,384]{3,2,1,0:T(8,128)S(1)}, f32[2,2,48,384]{3,2,1,0:T(8,128)S(1)}, u32[]{:S(2)}, u32[]{:S(2)}) collective-permute-start(f32[2,2,48,384]{3,2,1,0:T(8,128)S(1)} %collective-permute-done.6.refs_1_), channel_id=1, source_target_pairs={{0,8},{8,0},{16,24},{24,16},{28,20},{20,28},{12,4},{4,12},{1,9},{9... | collective-permute-start | bytes 884744 | tf_op jit(solution)/shard_map/ring2a/ppermute | solution.py:443
  49.4 7.3 %collective-permute-start.10 = (f32[2,2,48,384]{3,2,1,0:T(8,128)S(1)}, f32[2,2,48,384]{3,2,1,0:T(8,128)S(1)}, u32[]{:S(2)}, u32[]{:S(2)}) collective-permute-start(f32[2,2,48,384]{3,2,1,0:T(8,128)S(1)} %collective-permute-done.9.refs_4_), channel_id=1, source_target_pairs={{8,16},{16,8},{24,28},{28,24},{20,12},{12,20},{4,0},{0,4},{9,17},{... | collective-permute-start | bytes 884744 | tf_op jit(solution)/shard_map/ring2b/ppermute | solution.py:443
  55.1 9.4 %collective-permute-start.11 = (f32[2,2,48,384]{3,2,1,0:T(8,128)S(1)}, f32[2,2,48,384]{3,2,1,0:T(8,128)S(1)}, u32[]{:S(2)}, u32[]{:S(2)}) collective-permute-start(f32[2,2,48,384]{3,2,1,0:T(8,128)S(1)} %collective-permute-done.7.refs_2_), channel_id=1, source_target_pairs={{8,16},{16,8},{24,28},{28,24},{20,12},{12,20},{4,0},{0,4},{9,17},{... | collective-permute-start | bytes 884744 | tf_op jit(solution)/shard_map/ring3a/ppermute | solution.py:443
  56.8 7.8 %collective-permute-start.12 = (f32[2,2,48,384]{3,2,1,0:T(8,128)S(1)}, f32[2,2,48,384]{3,2,1,0:T(8,128)S(1)}, u32[]{:S(2)}, u32[]{:S(2)}) collective-permute-start(f32[2,2,48,384]{3,2,1,0:T(8,128)S(1)} %collective-permute-done.10.refs_5_), channel_id=1, source_target_pairs={{0,8},{8,0},{16,24},{24,16},{28,20},{20,28},{12,4},{4,12},{1,9},{9... | collective-permute-start | bytes 884744 | tf_op jit(solution)/shard_map/ring3b/ppermute | solution.py:443
  57.1 5.1 %copy-start.4 = (s32[8,3]{0,1:T(4,128)S(1)}, s32[8,3]{0,1:T(4,128)}, u32[]{:S(2)}) copy-start(s32[8,3]{0,1:T(4,128)} %param.15) | copy-start | bytes 292

commit v3 on v2

--- a/solution.py
+++ b/solution.py
@@ -32,6 +32,10 @@
     return [pltpu.with_memory_space_constraint(x, VMEM) for x in xs]
 
 
+def in_hbm(*xs):
+    return [pltpu.with_memory_space_constraint(x, pltpu.HBM) for x in xs]
+
+
 def kept(shape, dtype=F32):
     return VMEM(shape, dtype)
 
@@ -46,10 +50,11 @@
 
 
 def pack_kernel(bands, slots, *refs):
-    raw, out, (owner, trip, center, live, modes, sem) = refs[:5], refs[5], refs[6:]
+    owner, live, raw, out, held = refs[0], refs[1], refs[2:5], refs[5], refs[6:]
+    trip, center, modes, sem = held
     copies = [
         pltpu.make_async_copy(src, dst, sem.at[i])
-        for i, (src, dst) in enumerate(zip(raw, (owner, trip, center, live, modes)))
+        for i, (src, dst) in enumerate(zip(raw, (trip, center, modes)))
     ]
     for c in copies:
         c.start()
@@ -77,17 +82,16 @@
 
 def pack(modes, owner, trip, center, live, bands, slots, total):
     rows = 2 * bands + -(-total // 8) * 8
-    ints = (owner, trip, center, live)
     return pl.pallas_call(
         functools.partial(pack_kernel, bands, slots),
         out_shape=kept((rows, LANES)),
-        in_specs=[RAW] * 5,
+        in_specs=[SCALARS] * 2 + [RAW] * 3,
         out_specs=WHOLE,
-        scratch_shapes=[SMEM(x.shape, x.dtype) for x in ints]
-        + [VMEM(modes.shape, F32), pltpu.SemaphoreType.DMA((5,))],
+        scratch_shapes=[SMEM(x.shape, x.dtype) for x in (trip, center)]
+        + [VMEM(modes.shape, F32), pltpu.SemaphoreType.DMA((3,))],
         compiler_params=limit(4),
         name="pack",
-    )(*ints, modes)
+    )(owner, live, *in_hbm(trip, center, modes))
 
 
 def fetch_kernel(slots, first, rows, parts, const, hi, lo, buf, sem):
@@ -124,7 +128,7 @@
         ],
         compiler_params=limit(8),
         name="fetch",
-    )(constants)
+    )(*in_hbm(constants))
 
 
 def contract_kernel(bands, slots, lines, e0, e1, *refs):
@@ -247,7 +251,7 @@
         ],
         compiler_params=limit(8),
         name="prep",
-    )(view)
+    )(*in_hbm(view))
 
 
 def angle_kernel(first, order, e0, e1, points, out):
@@ -439,8 +443,7 @@
         arrived = []
         for h, plan in enumerate(plans):
             perm = plan[step % 2]
-            with jax.named_scope(f"ring{step}{'ab'[h]}"):
-                arrived.append(lax.ppermute(moving[h], "row", perm))
+            arrived.append(lax.ppermute(moving[h], "row", perm))
             source = np.zeros_like(held[h])
             for a, b in perm:
                 source[b] = held[h][a]
@@ -468,43 +471,36 @@
     second_vectors,
 ):
     n_row, n_ba = lax.axis_size("row"), lax.axis_size("ba")
-    slots, width, bb = constants.shape
+    slots, width, _ = constants.shape
     size = width * n_ba
     bands = current_modes.shape[-1]
     half = size // 2
     total = slots * n_row
-    scope = jax.named_scope
     modes = jnp.swapaxes(current_modes[0], 1, 2)
     payload = pack(
         modes, owner_id, triplets, center_point, live_count, bands, slots, total
     )
-    bit, hop = 1, 0
+    bit = 1
     while bit < n_row:
-        with scope(f"hop{hop}"):
-            other = swap(payload, "row", bit, n_row)
-        bit, hop = bit * 2, hop + 1
+        other = swap(payload, "row", bit, n_row)
+        bit = bit * 2
         if bit < n_row:
             payload = payload + other
     cuts = 3 if width % 48 == 0 else 1
     pieces = []
     for i in range(cuts):
-        with scope(f"fetch{i}"):
-            pieces += fetch(constants, i * width // cuts, width // cuts)
+        pieces += fetch(constants, i * width // cuts, width // cuts)
     keep, send = contract(pieces, payload, other, bands)
 
     keep = keep.reshape(bands // 2, 2, slots, half, 2 * size)
     send = send.reshape(bands // 2, 2, slots, half, 2 * size)
-    with scope("core"):
-        got = swap(send, "ba", 1, n_ba)
-    with scope("far"):
-        far = swap(keep[1] + got[1], "ba", 2, n_ba)
+    got = swap(send, "ba", 1, n_ba)
+    far = swap(keep[1] + got[1], "ba", 2, n_ba)
     own = (keep[0] + got[0]) + far
     own = own.swapaxes(0, 1)
 
-    with scope("weights"):
-        weights = prep(second_vectors, size, False)
-    with scope("lefts"):
-        lefts = prep(first_vectors, size, True)
+    weights = prep(second_vectors, size, False)
+    lefts = prep(first_vectors, size, True)
     operands = (*lefts, *weights)
     if slots == 1 and n_row <= 8:
         parts = (own[0, :, : half // 2], own[0, :, half // 2 :])
@@ -523,11 +519,9 @@
         ahead, behind = [(gathered, (0, half, tuple(range(total))))], []
         order = np.broadcast_to(np.arange(total), (n_row, total))
     order = tuple(tuple(int(x) for x in line) for line in order)
-    with scope("angles"):
-        table = angles(payload, other, pair_points, 2 * bands, order)
+    table = angles(payload, other, pair_points, 2 * bands, order)
     arrays, spec = zip(*ahead)
-    with scope("early"):
-        partial = early(arrays, spec, table, pair_points.shape[0], half)
+    partial = early(arrays, spec, table, pair_points.shape[0], half)
     arrays, spec = zip(*behind) if behind else ((), ())
     return final(partial, arrays, spec, table, operands, total)
 

time: 70.4 us -> 68.4 us (0.972)
  local copies, waits for them, and re-layouts: 5.04 us -> 0.03 us
  Pallas kernels: 18.3 us -> 21.3 us
    unnamed x14 -> x2, local copies, waits for them, and re-layouts: 5.01 us -> 0.01 us
    pallas_call x3, Pallas kernels: 3.32 us -> 5.14 us  [fetch(): pl.pallas_call(functools.partial(fetch_kernel, slots, first, rows, parts)...]
    pallas_call x2, Pallas kernels: 5.07 us -> 6.05 us  [prep(): pl.pallas_call(functools.partial(prep_kernel, size, turn), out_shape=(kep...]
  transfers between devices with their start and end apart: 13 -> 13, of which waited for: 10 -> 10; matrix products, arithmetic and copies ran while one was open for 0% -> 0% of each run, Pallas kernels for 15% -> 20%
where the time goes in v3:
time: 68.4 us; the launch traced here: 68.1 us
  waiting for transfers between devices  26.5 us (39%)
  Pallas kernels  21.3 us (31%)
  starting transfers between devices  18.7 us (27%)
  between operations  1.43 us (2%)
    ppermute x8, waiting for transfers between devices, neighbour_gather(): arrived.append(lax.ppermute(moving[h], 'row', perm))  13.7 us
    ppermute x5, waiting for transfers between devices, swap(): return lax.ppermute(x, axis, [(i, i ^ bit) for i in range(n)])  12.8 us
    ppermute x5, starting transfers between devices, swap(): return lax.ppermute(x, axis, [(i, i ^ bit) for i in range(n)])  9.83 us
    ppermute x8, starting transfers between devices, neighbour_gather(): arrived.append(lax.ppermute(moving[h], 'row', perm))  8.92 us
    pallas_call x2, Pallas kernels, prep(): pl.pallas_call(functools.partial(prep_kernel, size, turn), out_shape=(kep...  6.05 us
    pallas_call x1, Pallas kernels, final(): pl.pallas_call(functools.partial(final_kernel, spec, cs.shape[1] // count...  5.61 us
    pallas_call x3, Pallas kernels, fetch(): pl.pallas_call(functools.partial(fetch_kernel, slots, first, rows, parts)...  5.14 us
    pallas_call x1, Pallas kernels, early(): pl.pallas_call(functools.partial(early_kernel, spec, width, 8), out_shape...  1.98 us
  transfers between devices with their start and end apart: 13, of which 10 were waited for; matrix products, arithmetic and copies ran while one was open for 0% of the time, Pallas kernels for 20%

profile of v3, /device:TPU:0, one launch (start us, length us, event | category | flops | bytes accessed | tf_op | source)
XLA Modules:
  0.0 68.1 jit_solution(2365018005417496072)
XLA Ops:
  1.3 0.7 %pack.1 = f32[16,128]{1,0:T(8,128)S(1)} custom-call(s32[1]{0:T(128)S(6)} %copy.15.refs_0_, s32[1]{0:T(128)S(6)} %copy.16.refs_1_, s32[1,6]{1,0:T(1,128)} %refs_2_.1, s32[3]{0:T(128)} %refs_3_.1, f32[2,4,48]{2,1,0:T(4,128)} %bitcast.37), custom_call_target="tpu_custom_call" | custom-call | tf_op jit(solution)/shard_map/pack/pallas_call | solution.py:85
  2.0 3.0 %collective-permute-start = (f32[16,128]{1,0:T(8,128)S(1)}, f32[16,128]{1,0:T(8,128)S(1)}, u32[]{:S(2)}, u32[]{:S(2)}) collective-permute-start(f32[16,128]{1,0:T(8,128)S(1)} %pack.1), channel_id=1, source_target_pairs={{0,4},{4,0},{8,12},{12,8},{16,20},{20,16},{24,28},{28,24},{1,5},{5... | collective-permute-start | bytes 24584 | tf_op jit(solution)/shard_map/ppermute | solution.py:423
  5.1 1.6 %collective-permute-done = f32[16,128]{1,0:T(8,128)S(1)} collective-permute-done((f32[16,128]{1,0:T(8,128)S(1)}, f32[16,128]{1,0:T(8,128)S(1)}, u32[]{:S(2)}, u32[]{:S(2)}) %collective-permute-start) | collective-permute-done | bytes 8224 | tf_op jit(solution)/shard_map/ppermute | solution.py:423
  6.7 2.1 %collective-permute-start.1 = (f32[16,128]{1,0:T(8,128)S(1)}, f32[16,128]{1,0:T(8,128)S(1)}, u32[]{:S(2)}, u32[]{:S(2)}) collective-permute-start(f32[16,128]{1,0:T(8,128)S(1)} %add.19), channel_id=1, source_target_pairs={{0,8},{4,12},{8,0},{12,4},{16,24},{20,28},{24,16},{28,20},{1,9},{5... | collective-permute-start | bytes 24584 | tf_op jit(solution)/shard_map/ppermute | solution.py:423
  8.8 1.6 %collective-permute-done.1 = f32[16,128]{1,0:T(8,128)S(1)} collective-permute-done((f32[16,128]{1,0:T(8,128)S(1)}, f32[16,128]{1,0:T(8,128)S(1)}, u32[]{:S(2)}, u32[]{:S(2)}) %collective-permute-start.1) | collective-permute-done | bytes 8224 | tf_op jit(solution)/shard_map/ppermute | solution.py:423
  10.4 3.0 %collective-permute-start.2 = (f32[16,128]{1,0:T(8,128)S(1)}, f32[16,128]{1,0:T(8,128)S(1)}, u32[]{:S(2)}, u32[]{:S(2)}) collective-permute-start(f32[16,128]{1,0:T(8,128)S(1)} %add.20.e0), channel_id=1, source_target_pairs={{0,16},{4,20},{8,24},{12,28},{16,0},{20,4},{24,8},{28,12},{1,17},{... | collective-permute-start | bytes 24584 | tf_op jit(solution)/shard_map/ppermute | solution.py:423
  13.5 1.7 %fetch.3 = (bf16[1,16,36864]{2,1,0:T(8,128)(2,1)S(1)}, bf16[1,16,36864]{2,1,0:T(8,128)(2,1)S(1)}) custom-call(f32[1,48,36864]{2,1,0:T(8,128)} %const.5), custom_call_target="tpu_custom_call" | custom-call | tf_op jit(solution)/shard_map/fetch/pallas_call | solution.py:120
  15.2 1.7 %fetch.5 = (bf16[1,16,36864]{2,1,0:T(8,128)(2,1)S(1)}, bf16[1,16,36864]{2,1,0:T(8,128)(2,1)S(1)}) custom-call(f32[1,48,36864]{2,1,0:T(8,128)} %const.5), custom_call_target="tpu_custom_call" | custom-call | tf_op jit(solution)/shard_map/fetch/pallas_call | solution.py:120
  16.9 1.7 %fetch.4 = (bf16[1,16,36864]{2,1,0:T(8,128)(2,1)S(1)}, bf16[1,16,36864]{2,1,0:T(8,128)(2,1)S(1)}) custom-call(f32[1,48,36864]{2,1,0:T(8,128)} %const.5), custom_call_target="tpu_custom_call" | custom-call | tf_op jit(solution)/shard_map/fetch/pallas_call | solution.py:120
  18.6 0.0 collective-permute-done.2.e1
  18.6 1.4 %contract.1 = (f32[4,1,96,384]{3,2,1,0:T(8,128)S(1)}, f32[4,1,96,384]{3,2,1,0:T(8,128)S(1)}) custom-call(f32[16,128]{1,0:T(8,128)S(1)} %add.20.e0, f32[16,128]{1,0:T(8,128)S(1)} %collective-permute-done.2.e1, bf16[1,16,36864]{2,1,0:T(8,128)(2,1)S(1)} %get-tuple-element.17.refs_0_, bf16[1,16,36864]{2,1,0:T(8,128)(2,1)S(1)} %get-tuple-element.18.refs_1_, ...), custom_call_target="tpu_custom_call" | custom-call | tf_op jit(solution)/shard_map/contract/pallas_call | solution.py:176
  20.0 0.1 collective-permute-start.3
  20.1 2.0 %collective-permute-done.3 = f32[2,2,1,96,384]{4,3,1,2,0:T(8,128)S(1)} collective-permute-done((f32[2,2,1,96,384]{4,3,1,2,0:T(8,128)S(1)}, f32[2,2,1,96,384]{4,3,1,2,0:T(8,128)S(1)}, u32[]{:S(2)}, u32[]{:S(2)}) %collective-permute-start.3) | collective-permute-done | bytes 589856 | tf_op jit(solution)/shard_map/ppermute | solution.py:423
  22.1 1.6 %collective-permute-start.4 = (f32[2,1,96,384]{3,2,0,1:T(8,128)S(1)}, f32[2,1,96,384]{3,2,0,1:T(8,128)S(1)}, u32[]{:S(2)}, u32[]{:S(2)}) collective-permute-start(f32[2,1,96,384]{3,2,0,1:T(8,128)S(1)} %fusion), channel_id=1, source_target_pairs={{0,2},{1,3},{2,0},{3,1},{4,6},{5,7},{6,4},{7,5},{8,10},{9,11},{10,... | collective-permute-start | bytes 884744 | tf_op jit(solution)/shard_map/ppermute | solution.py:423
  23.7 7.5 %collective-permute-done.4 = f32[2,1,96,384]{3,2,0,1:T(8,128)S(1)} collective-permute-done((f32[2,1,96,384]{3,2,0,1:T(8,128)S(1)}, f32[2,1,96,384]{3,2,0,1:T(8,128)S(1)}, u32[]{:S(2)}, u32[]{:S(2)}) %collective-permute-start.4) | collective-permute-done | bytes 294944 | tf_op jit(solution)/shard_map/ppermute | solution.py:423
  31.3 1.6 %collective-permute-start.5 = (f32[1,2,48,384]{3,2,1,0:T(8,128)S(1)}, f32[1,2,48,384]{3,2,1,0:T(8,128)S(1)}, u32[]{:S(2)}, u32[]{:S(2)}) collective-permute-start(f32[1,2,48,384]{3,2,1,0:T(8,128)S(1)} %get-tuple-element.30), channel_id=1, source_target_pairs={{0,8},{8,0},{16,24},{24,16},{28,20},{20,28},{12,4},{4,12},{1,9},{9... | collective-permute-start | bytes 442376 | tf_op jit(solution)/shard_map/ppermute | solution.py:446
  33.0 1.5 %collective-permute-start.8 = (f32[1,2,48,384]{3,2,1,0:T(8,128)S(1)}, f32[1,2,48,384]{3,2,1,0:T(8,128)S(1)}, u32[]{:S(2)}, u32[]{:S(2)}) collective-permute-start(f32[1,2,48,384]{3,2,1,0:T(8,128)S(1)} %get-tuple-element.29), channel_id=1, source_target_pairs={{8,16},{16,8},{24,28},{28,24},{20,12},{12,20},{4,0},{0,4},{9,17},{... | collective-permute-start | bytes 442376 | tf_op jit(solution)/shard_map/ppermute | solution.py:446
  34.5 2.1 %collective-permute-done.5 = f32[1,2,48,384]{3,2,1,0:T(8,128)S(1)} collective-permute-done((f32[1,2,48,384]{3,2,1,0:T(8,128)S(1)}, f32[1,2,48,384]{3,2,1,0:T(8,128)S(1)}, u32[]{:S(2)}, u32[]{:S(2)}) %collective-permute-start.5) | collective-permute-done | bytes 147488 | tf_op jit(solution)/shard_map/ppermute | solution.py:446
  36.6 1.6 %collective-permute-start.6 = (f32[2,2,48,384]{3,2,1,0:T(8,128)S(1)}, f32[2,2,48,384]{3,2,1,0:T(8,128)S(1)}, u32[]{:S(2)}, u32[]{:S(2)}) collective-permute-start(f32[2,2,48,384]{3,2,1,0:T(8,128)S(1)} %pad_maximum_fusion.refs_0_), channel_id=1, source_target_pairs={{8,16},{16,8},{24,28},{28,24},{20,12},{12,20},{4,0},{0,4},{9,17},{... | collective-permute-start | bytes 884744 | tf_op jit(solution)/shard_map/ppermute | solution.py:446
  38.1 0.8 %collective-permute-done.8 = f32[1,2,48,384]{3,2,1,0:T(8,128)S(1)} collective-permute-done((f32[1,2,48,384]{3,2,1,0:T(8,128)S(1)}, f32[1,2,48,384]{3,2,1,0:T(8,128)S(1)}, u32[]{:S(2)}, u32[]{:S(2)}) %collective-permute-start.8) | collective-permute-done | bytes 147488 | tf_op jit(solution)/shard_map/ppermute | solution.py:446
  38.9 0.1 collective-permute-start.9
  39.0 5.5 %collective-permute-done.6.refs_1_ = f32[2,2,48,384]{3,2,1,0:T(8,128)S(1)} collective-permute-done((f32[2,2,48,384]{3,2,1,0:T(8,128)S(1)}, f32[2,2,48,384]{3,2,1,0:T(8,128)S(1)}, u32[]{:S(2)}, u32[]{:S(2)}) %collective-permute-start.6) | collective-permute-done | bytes 294944 | tf_op jit(solution)/shard_map/ppermute | solution.py:446
  44.4 0.8 %collective-permute-start.7 = (f32[2,2,48,384]{3,2,1,0:T(8,128)S(1)}, f32[2,2,48,384]{3,2,1,0:T(8,128)S(1)}, u32[]{:S(2)}, u32[]{:S(2)}) collective-permute-start(f32[2,2,48,384]{3,2,1,0:T(8,128)S(1)} %collective-permute-done.6.refs_1_), channel_id=1, source_target_pairs={{0,8},{8,0},{16,24},{24,16},{28,20},{20,28},{12,4},{4,12},{1,9},{9... | collective-permute-start | bytes 884744 | tf_op jit(solution)/shard_map/ppermute | solution.py:446
  45.2 1.1 %collective-permute-done.9.refs_4_ = f32[2,2,48,384]{3,2,1,0:T(8,128)S(1)} collective-permute-done((f32[2,2,48,384]{3,2,1,0:T(8,128)S(1)}, f32[2,2,48,384]{3,2,1,0:T(8,128)S(1)}, u32[]{:S(2)}, u32[]{:S(2)}) %collective-permute-start.9) | collective-permute-done | bytes 294944 | tf_op jit(solution)/shard_map/ppermute | solution.py:446
  46.3 1.5 %collective-permute-start.10 = (f32[2,2,48,384]{3,2,1,0:T(8,128)S(1)}, f32[2,2,48,384]{3,2,1,0:T(8,128)S(1)}, u32[]{:S(2)}, u32[]{:S(2)}) collective-permute-start(f32[2,2,48,384]{3,2,1,0:T(8,128)S(1)} %collective-permute-done.9.refs_4_), channel_id=1, source_target_pairs={{8,16},{16,8},{24,28},{28,24},{20,12},{12,20},{4,0},{0,4},{9,17},{... | collective-permute-start | bytes 884744 | tf_op jit(solution)/shard_map/ppermute | solution.py:446
  47.8 4.2 %collective-permute-done.7.refs_2_ = f32[2,2,48,384]{3,2,1,0:T(8,128)S(1)} collective-permute-done((f32[2,2,48,384]{3,2,1,0:T(8,128)S(1)}, f32[2,2,48,384]{3,2,1,0:T(8,128)S(1)}, u32[]{:S(2)}, u32[]{:S(2)}) %collective-permute-start.7) | collective-permute-done | bytes 294944 | tf_op jit(solution)/shard_map/ppermute | solution.py:446
  52.0 1.5 %collective-permute-start.11 = (f32[2,2,48,384]{3,2,1,0:T(8,128)S(1)}, f32[2,2,48,384]{3,2,1,0:T(8,128)S(1)}, u32[]{:S(2)}, u32[]{:S(2)}) collective-permute-start(f32[2,2,48,384]{3,2,1,0:T(8,128)S(1)} %collective-permute-done.7.refs_2_), channel_id=1, source_target_pairs={{8,16},{16,8},{24,28},{28,24},{20,12},{12,20},{4,0},{0,4},{9,17},{... | collective-permute-start | bytes 884744 | tf_op jit(solution)/shard_map/ppermute | solution.py:446
  53.5 0.2 collective-permute-done.10.refs_5_
  53.7 0.4 collective-permute-start.12
  54.0 0.0 copy-start
  54.0 3.4 %prep.2 = (bf16[8,3,192,192]{3,2,1,0:T(8,128)(2,1)S(1)}, bf16[8,3,192,192]{3,2,1,0:T(8,128)(2,1)S(1)}) custom-call(f32[8,576,128]{2,1,0:T(8,128)} %bitcast.35), custom_call_target="tpu_custom_call" | custom-call | tf_op jit(solution)/shard_map/prep/pallas_call | solution.py:241
  57.4 2.6 %prep.3 = (bf16[8,3,192,192]{3,2,1,0:T(8,128)(2,1)S(1)}, bf16[8,3,192,192]{3,2,1,0:T(8,128)(2,1)S(1)}) custom-call(f32[8,576,128]{2,1,0:T(8,128)} %bitcast.36), custom_call_target="tpu_custom_call" | custom-call | tf_op jit(solution)/shard_map/prep/pallas_call | solution.py:241
  60.1 0.0 copy-done
  60.1 0.4 angles.1.refs_6_.refs_2_
  60.5 2.0 %early.1.partial = f32[8,2,96,384]{3,2,1,0:T(8,128)S(1)} custom-call(f32[2,2,48,384]{3,2,1,0:T(8,128)S(1)} %pad_maximum_fusion.refs_0_, f32[2,2,48,384]{3,2,1,0:T(8,128)S(1)} %collective-permute-done.6.refs_1_, f32[2,2,48,384]{3,2,1,0:T(8,128)S(1)} %collective-permute-done.7.refs_2_, f32[2,2,48,384]{3,2,1,0:T(8,128)S(1)} %pad_maximum_fusion.1.refs_3_, ...), custom_call_target="tpu_custom_call" | custom-call | tf_op jit(solution)/shard_map/early/pallas_call | solution.py:338
  62.5 0.0 collective-permute-done.11.refs_0_
  62.5 0.0 collective-permute-done.12.refs_1_
  62.5 5.6 %final.1 = f32[8,288,128]{2,1,0:T(8,128)} custom-call(f32[8,2,96,384]{3,2,1,0:T(8,128)S(1)} %early.1.partial, f32[2,2,48,384]{3,2,1,0:T(8,128)S(1)} %collective-permute-done.11.refs_0_, f32[2,2,48,384]{3,2,1,0:T(8,128)S(1)} %collective-permute-done.12.refs_1_, f32[2,128,128]{2,1,0:T(8,128)S(1)} %angles.1.refs_6_.refs_2_, ...), custom_call_target="tpu_custom_call" | custom-call | tf_op jit(solution)/shard_map/final/pallas_call | solution.py:409
  (7 shorter events, 0.1 us)
Async XLA Ops:
  2.0 4.7 %collective-permute-start = (f32[16,128]{1,0:T(8,128)S(1)}, f32[16,128]{1,0:T(8,128)S(1)}, u32[]{:S(2)}, u32[]{:S(2)}) collective-permute-start(f32[16,128]{1,0:T(8,128)S(1)} %pack.1), channel_id=1, source_target_pairs={{0,4},{4,0},{8,12},{12,8},{16,20},{20,16},{24,28},{28,24},{1,5},{5... | collective-permute-start | bytes 24584 | tf_op jit(solution)/shard_map/ppermute | solution.py:423
  6.7 3.7 %collective-permute-start.1 = (f32[16,128]{1,0:T(8,128)S(1)}, f32[16,128]{1,0:T(8,128)S(1)}, u32[]{:S(2)}, u32[]{:S(2)}) collective-permute-start(f32[16,128]{1,0:T(8,128)S(1)} %add.19), channel_id=1, source_target_pairs={{0,8},{4,12},{8,0},{12,4},{16,24},{20,28},{24,16},{28,20},{1,9},{5... | collective-permute-start | bytes 24584 | tf_op jit(solution)/shard_map/ppermute | solution.py:423
  10.4 8.2 %collective-permute-start.2 = (f32[16,128]{1,0:T(8,128)S(1)}, f32[16,128]{1,0:T(8,128)S(1)}, u32[]{:S(2)}, u32[]{:S(2)}) collective-permute-start(f32[16,128]{1,0:T(8,128)S(1)} %add.20.e0), channel_id=1, source_target_pairs={{0,16},{4,20},{8,24},{12,28},{16,0},{20,4},{24,8},{28,12},{1,17},{... | collective-permute-start | bytes 24584 | tf_op jit(solution)/shard_map/ppermute | solution.py:423
  20.0 2.1 %collective-permute-start.3 = (f32[2,2,1,96,384]{4,3,1,2,0:T(8,128)S(1)}, f32[2,2,1,96,384]{4,3,1,2,0:T(8,128)S(1)}, u32[]{:S(2)}, u32[]{:S(2)}) collective-permute-start(f32[2,2,1,96,384]{4,3,1,2,0:T(8,128)S(1)} %bitcast.34), channel_id=1, source_target_pairs={{0,1},{1,0},{2,3},{3,2},{4,5},{5,4},{6,7},{7,6},{8,9},{9,8},{10,11... | collective-permute-start | bytes 1769480 | tf_op jit(solution)/shard_map/ppermute | solution.py:423
  22.1 9.1 %collective-permute-start.4 = (f32[2,1,96,384]{3,2,0,1:T(8,128)S(1)}, f32[2,1,96,384]{3,2,0,1:T(8,128)S(1)}, u32[]{:S(2)}, u32[]{:S(2)}) collective-permute-start(f32[2,1,96,384]{3,2,0,1:T(8,128)S(1)} %fusion), channel_id=1, source_target_pairs={{0,2},{1,3},{2,0},{3,1},{4,6},{5,7},{6,4},{7,5},{8,10},{9,11},{10,... | collective-permute-start | bytes 884744 | tf_op jit(solution)/shard_map/ppermute | solution.py:423
  31.3 5.2 %collective-permute-start.5 = (f32[1,2,48,384]{3,2,1,0:T(8,128)S(1)}, f32[1,2,48,384]{3,2,1,0:T(8,128)S(1)}, u32[]{:S(2)}, u32[]{:S(2)}) collective-permute-start(f32[1,2,48,384]{3,2,1,0:T(8,128)S(1)} %get-tuple-element.30), channel_id=1, source_target_pairs={{0,8},{8,0},{16,24},{24,16},{28,20},{20,28},{12,4},{4,12},{1,9},{9... | collective-permute-start | bytes 442376 | tf_op jit(solution)/shard_map/ppermute | solution.py:446
  33.0 5.9 %collective-permute-start.8 = (f32[1,2,48,384]{3,2,1,0:T(8,128)S(1)}, f32[1,2,48,384]{3,2,1,0:T(8,128)S(1)}, u32[]{:S(2)}, u32[]{:S(2)}) collective-permute-start(f32[1,2,48,384]{3,2,1,0:T(8,128)S(1)} %get-tuple-element.29), channel_id=1, source_target_pairs={{8,16},{16,8},{24,28},{28,24},{20,12},{12,20},{4,0},{0,4},{9,17},{... | collective-permute-start | bytes 442376 | tf_op jit(solution)/shard_map/ppermute | solution.py:446
  36.6 7.9 %collective-permute-start.6 = (f32[2,2,48,384]{3,2,1,0:T(8,128)S(1)}, f32[2,2,48,384]{3,2,1,0:T(8,128)S(1)}, u32[]{:S(2)}, u32[]{:S(2)}) collective-permute-start(f32[2,2,48,384]{3,2,1,0:T(8,128)S(1)} %pad_maximum_fusion.refs_0_), channel_id=1, source_target_pairs={{8,16},{16,8},{24,28},{28,24},{20,12},{12,20},{4,0},{0,4},{9,17},{... | collective-permute-start | bytes 884744 | tf_op jit(solution)/shard_map/ppermute | solution.py:446
  38.9 7.4 %collective-permute-start.9 = (f32[2,2,48,384]{3,2,1,0:T(8,128)S(1)}, f32[2,2,48,384]{3,2,1,0:T(8,128)S(1)}, u32[]{:S(2)}, u32[]{:S(2)}) collective-permute-start(f32[2,2,48,384]{3,2,1,0:T(8,128)S(1)} %pad_maximum_fusion.1.refs_3_), channel_id=1, source_target_pairs={{0,8},{8,0},{16,24},{24,16},{28,20},{20,28},{12,4},{4,12},{1,9},{9... | collective-permute-start | bytes 884744 | tf_op jit(solution)/shard_map/ppermute | solution.py:446
  44.4 7.6 %collective-permute-start.7 = (f32[2,2,48,384]{3,2,1,0:T(8,128)S(1)}, f32[2,2,48,384]{3,2,1,0:T(8,128)S(1)}, u32[]{:S(2)}, u32[]{:S(2)}) collective-permute-start(f32[2,2,48,384]{3,2,1,0:T(8,128)S(1)} %collective-permute-done.6.refs_1_), channel_id=1, source_target_pairs={{0,8},{8,0},{16,24},{24,16},{28,20},{20,28},{12,4},{4,12},{1,9},{9... | collective-permute-start | bytes 884744 | tf_op jit(solution)/shard_map/ppermute | solution.py:446
  46.3 7.3 %collective-permute-start.10 = (f32[2,2,48,384]{3,2,1,0:T(8,128)S(1)}, f32[2,2,48,384]{3,2,1,0:T(8,128)S(1)}, u32[]{:S(2)}, u32[]{:S(2)}) collective-permute-start(f32[2,2,48,384]{3,2,1,0:T(8,128)S(1)} %collective-permute-done.9.refs_4_), channel_id=1, source_target_pairs={{8,16},{16,8},{24,28},{28,24},{20,12},{12,20},{4,0},{0,4},{9,17},{... | collective-permute-start | bytes 884744 | tf_op jit(solution)/shard_map/ppermute | solution.py:446
  52.0 10.5 %collective-permute-start.11 = (f32[2,2,48,384]{3,2,1,0:T(8,128)S(1)}, f32[2,2,48,384]{3,2,1,0:T(8,128)S(1)}, u32[]{:S(2)}, u32[]{:S(2)}) collective-permute-start(f32[2,2,48,384]{3,2,1,0:T(8,128)S(1)} %collective-permute-done.7.refs_2_), channel_id=1, source_target_pairs={{8,16},{16,8},{24,28},{28,24},{20,12},{12,20},{4,0},{0,4},{9,17},{... | collective-permute-start | bytes 884744 | tf_op jit(solution)/shard_map/ppermute | solution.py:446
  53.7 8.9 %collective-permute-start.12 = (f32[2,2,48,384]{3,2,1,0:T(8,128)S(1)}, f32[2,2,48,384]{3,2,1,0:T(8,128)S(1)}, u32[]{:S(2)}, u32[]{:S(2)}) collective-permute-start(f32[2,2,48,384]{3,2,1,0:T(8,128)S(1)} %collective-permute-done.10.refs_5_), channel_id=1, source_target_pairs={{0,8},{8,0},{16,24},{24,16},{28,20},{20,28},{12,4},{4,12},{1,9},{9... | collective-permute-start | bytes 884744 | tf_op jit(solution)/shard_map/ppermute | solution.py:446
  54.0 6.1 %copy-start = (s32[8,3]{0,1:T(4,128)S(1)}, s32[8,3]{0,1:T(4,128)}, u32[]{:S(2)}) copy-start(s32[8,3]{0,1:T(4,128)} %param.15) | copy-start | bytes 292

commit v4 on v3

--- a/solution.py
+++ b/solution.py
@@ -50,8 +50,7 @@
 
 
 def pack_kernel(bands, slots, *refs):
-    owner, live, raw, out, held = refs[0], refs[1], refs[2:5], refs[5], refs[6:]
-    trip, center, modes, sem = held
+    owner, raw, out, (trip, center, modes, sem) = refs[0], refs[1:4], refs[4], refs[5:]
     copies = [
         pltpu.make_async_copy(src, dst, sem.at[i])
         for i, (src, dst) in enumerate(zip(raw, (trip, center, modes)))
@@ -72,7 +71,7 @@
     lane = lax.broadcasted_iota(jnp.int32, (1, LANES), 1)
     for r in range(slots):
         shift = 0
-        entry = jnp.where(lane == 4, (r < live[0]).astype(jnp.int32), 0)
+        entry = jnp.zeros((1, LANES), jnp.int32)
         for d in range(3):
             entry = jnp.where(lane == d, trip[r, d] - trip[r, 3 + d], entry)
             shift = shift + trip[r, 3 + d] * center[d]
@@ -80,18 +79,18 @@
         out[pl.ds(2 * bands + row * slots + r, 1), :] = entry.astype(F32)
 
 
-def pack(modes, owner, trip, center, live, bands, slots, total):
+def pack(modes, owner, trip, center, bands, slots, total):
     rows = 2 * bands + -(-total // 8) * 8
     return pl.pallas_call(
         functools.partial(pack_kernel, bands, slots),
         out_shape=kept((rows, LANES)),
-        in_specs=[SCALARS] * 2 + [RAW] * 3,
+        in_specs=[SCALARS] + [RAW] * 3,
         out_specs=WHOLE,
         scratch_shapes=[SMEM(x.shape, x.dtype) for x in (trip, center)]
         + [VMEM(modes.shape, F32), pltpu.SemaphoreType.DMA((3,))],
         compiler_params=limit(4),
         name="pack",
-    )(owner, live, *in_hbm(trip, center, modes))
+    )(owner, *in_hbm(trip, center, modes))
 
 
 def fetch_kernel(slots, first, rows, parts, const, hi, lo, buf, sem):
@@ -131,7 +130,7 @@
     )(*in_hbm(constants))
 
 
-def contract_kernel(bands, slots, lines, e0, e1, *refs):
+def contract_kernel(bands, slots, first, lines, e0, e1, *refs):
     pieces, (keep, send) = refs[:-2], refs[-2:]
     his, los = pieces[0::2], pieces[1::2]
     width = sum(h.shape[1] for h in his)
@@ -140,9 +139,7 @@
     pairs, chunk = keep.shape[2], keep.shape[3]
     low = lax.broadcasted_iota(jnp.int32, (2 * bands, LANES), 1) < 64
     for r in range(slots):
-        own = pl.ds(2 * bands + lax.axis_index("row") * slots + r, 1)
-        weight = e0[own, 4:5] + e1[own, 4:5]
-        eh, el = split(eigen * weight)
+        eh, el = split(eigen)
         left = jnp.concatenate(
             [
                 jnp.concatenate([eh, eh], axis=1),
@@ -151,7 +148,7 @@
             axis=0,
         )
         for base in range(0, pairs, lines):
-            lanes = slice(base * chunk, (base + lines) * chunk)
+            lanes = slice((first + base) * chunk, (first + base + lines) * chunk)
             right = jnp.concatenate(
                 [h[r, :, lanes] for h in his] + [m[r, :, lanes] for m in los], axis=0
             )
@@ -170,12 +167,11 @@
                     send[:, r, base + q, spot] = t[bands:]
 
 
-def contract(pieces, e0, e1, bands):
-    slots, _, bb = pieces[0].shape
-    chunk = 3 * LANES
-    return pl.pallas_call(
-        functools.partial(contract_kernel, bands, slots, 8),
-        out_shape=(kept((bands, slots, bb // chunk, chunk)),) * 2,
+def contract(pieces, e0, e1, bands, first, count):
+    slots = pieces[0].shape[0]
+    return pl.pallas_call(
+        functools.partial(contract_kernel, bands, slots, first, 8),
+        out_shape=(kept((bands, slots, count, 3 * LANES)),) * 2,
         in_specs=[WHOLE] * (2 + len(pieces)),
         out_specs=[WHOLE] * 2,
         compiler_params=limit(8),
@@ -196,7 +192,7 @@
     return jnp.concatenate([a, b[:, 0 : size - LANES]], axis=1)
 
 
-def prep_kernel(size, turn, raw, hi, lo, buf, sem, left, right):
+def prep_kernel(size, turn, spans, raw, hi, lo, buf, sem, left, right):
     half = size // 2
     count = raw.shape[0]
     copies = [
@@ -210,7 +206,9 @@
         for s in range(2):
             even, odd = unpack_matrix(buf, k, s, size)
             if turn:
-                turned = jnp.concatenate([join(*even, size), join(*odd, size)], axis=0).T
+                both = join(*even, size), join(*odd, size)
+                rows = [x[a : a + n] for a, n in spans for x in both]
+                turned = jnp.concatenate(rows, axis=0).T
                 left[...] = turned[:, 0:LANES]
                 right[:, 0 : size - LANES] = turned[:, LANES:size]
                 rows = [
@@ -233,13 +231,13 @@
             hi[k, i], lo[k, i] = split(m)
 
 
-def prep(vectors, size, turn):
+def prep(vectors, size, turn, spans):
     count, _, bb = vectors.shape
     tiles = bb // LANES
     view = vectors.reshape(count, 2, tiles, LANES).swapaxes(1, 2)
     view = view.reshape(count, 2 * tiles, LANES)
     return pl.pallas_call(
-        functools.partial(prep_kernel, size, turn),
+        functools.partial(prep_kernel, size, turn, spans),
         out_shape=(kept((count, 3, size, size), BF16),) * 2,
         in_specs=[RAW],
         out_specs=[WHOLE] * 2,
@@ -345,40 +343,74 @@
     )(*in_vmem(*blocks, cs))
 
 
-def final_kernel(spec, width, scale, size, unroll, partial, *refs):
+def triple(xh, xl, yh, yl):
+    rows = xh.shape[0]
+    both = dot(jnp.concatenate([xh, xl], axis=0), yh)
+    return both[0:rows] + both[rows:] + dot(xh, yl)
+
+
+def load(span, width, spec, k, u, partial, blocks, cs, ph, plo):
+    first, lines = span
+    group = 16
+    for q0 in range(first, first + lines, group):
+        re, im = partial[k, 0, pl.ds(q0, group), :], partial[k, 1, pl.ds(q0, group), :]
+        re, im = rotated(blocks, spec, cs, width, k, q0, group, re, im)
+        for i, m in enumerate((re + im, re, im)):
+            t0, t1, t2 = (m[:, j * LANES : (j + 1) * LANES] for j in range(3))
+            for base, a, b in ((0, t0, t1), (lines, t2, pltpu.roll(t1, 64, 1))):
+                spot = pl.ds(base + q0 - first, group)
+                for dst, x, y in zip((ph, plo), split(a), split(b)):
+                    dst[u, i, spot, 0:LANES] = x
+                    dst[u, i, spot, LANES : 2 * LANES] = y
+
+
+def product(size, k, u, ph, plo, wh, wl):
+    k1, k2, k3 = (
+        triple(ph[u, i][:, 0:size], plo[u, i][:, 0:size], wh[k, i], wl[k, i])
+        for i in range(3)
+    )
+    return k1 - k3, k1 + k2
+
+
+def inner_kernel(span, width, spec, size, unroll, partial, *refs):
+    blocks = refs[: len(spec)]
+    cs, wh, wl, out, ph, plo = refs[len(spec) :]
+    first = pl.program_id(0) * unroll
+    for u in range(unroll):
+        load(span, width, spec, first + u, u, partial, blocks, cs, ph, plo)
+    for u in range(unroll):
+        k = first + u
+        out[k, 0], out[k, 1] = product(size, k, u, ph, plo, wh, wl)
+
+
+def halves(unroll, span):
+    return [VMEM((unroll, 3, 2 * span[1], 2 * LANES), BF16)] * 2
+
+
+def inner(span, partial, blocks, spec, cs, weights):
+    count, _, size, _ = weights[0].shape
+    unroll = 2 if count % 2 == 0 else 1
+    return pl.pallas_call(
+        functools.partial(inner_kernel, span, cs.shape[1] // count, spec, size, unroll),
+        out_shape=kept((count, 2, 2 * span[1], size)),
+        grid=(count // unroll,),
+        in_specs=[WHOLE] * (4 + len(blocks)),
+        out_specs=WHOLE,
+        scratch_shapes=halves(unroll, span),
+        compiler_params=limit(8),
+        name="inner",
+    )(*in_vmem(partial, *blocks, cs, *weights))
+
+
+def final_kernel(span, width, spec, scale, size, unroll, done, partial, *refs):
     blocks = refs[: len(spec)]
     cs, gh, gl, wh, wl, out, ph, plo = refs[len(spec) :]
     half = size // 2
-    group = 16
     first = pl.program_id(0) * unroll
 
-    def load(u):
+    def outer(u, sums):
         k = first + u
-        for q0 in range(0, half, group):
-            re, im = partial[k, 0, pl.ds(q0, group), :], partial[k, 1, pl.ds(q0, group), :]
-            re, im = rotated(blocks, spec, cs, width, k, q0, group, re, im)
-            for i, m in enumerate((re + im, re, im)):
-                t0, t1, t2 = (m[:, j * LANES : (j + 1) * LANES] for j in range(3))
-                for base, a, b in ((0, t0, t1), (half, t2, pltpu.roll(t1, 64, 1))):
-                    spot = pl.ds(base + q0, group)
-                    for dst, x, y in zip((ph, plo), split(a), split(b)):
-                        dst[u, i, spot, 0:LANES] = x
-                        dst[u, i, spot, LANES : 2 * LANES] = y
-
-    def triple(xh, xl, yh, yl):
-        both = dot(jnp.concatenate([xh, xl], axis=0), yh)
-        return both[0:size] + both[size:] + dot(xh, yl)
-
-    def inner(u):
-        k = first + u
-        k1, k2, k3 = (
-            triple(ph[u, i][:, 0:size], plo[u, i][:, 0:size], wh[k, i], wl[k, i])
-            for i in range(3)
-        )
-        return k1 - k3, k1 + k2
-
-    def outer(u, re, im):
-        k = first + u
+        re, im = (jnp.concatenate([done[k, i], x], axis=0) for i, x in enumerate(sums))
         k1, k2, k3 = (
             triple(gh[k, i], gl[k, i], *split(m))
             for i, m in enumerate((re, im - re, re + im))
@@ -396,26 +428,27 @@
         out[u, pl.ds(2, half, stride=3), :] = jnp.where(low, turned, tail[half:])
 
     for u in range(unroll):
-        load(u)
-    sums = [inner(u) for u in range(unroll)]
+        load(span, width, spec, first + u, u, partial, blocks, cs, ph, plo)
+    sums = [product(size, first + u, u, ph, plo, wh, wl) for u in range(unroll)]
     for u in range(unroll):
-        store(u, outer(u, *sums[u]))
-
-
-def final(partial, blocks, spec, cs, operands, total):
-    count, _, size, _ = operands[0].shape
+        store(u, outer(u, sums[u]))
+
+
+def final(span, done, partial, blocks, spec, cs, lefts, weights, total):
+    count, _, size, _ = weights[0].shape
     tiles = size * size // LANES
     unroll = 2 if count % 2 == 0 else 1
+    width = cs.shape[1] // count
     result = pl.pallas_call(
-        functools.partial(final_kernel, spec, cs.shape[1] // count, 1.0 / total, size, unroll),
+        functools.partial(final_kernel, span, width, spec, 1.0 / total, size, unroll),
         out_shape=jax.ShapeDtypeStruct((count, tiles, LANES), F32),
         grid=(count // unroll,),
-        in_specs=[WHOLE] * (6 + len(blocks)),
+        in_specs=[WHOLE] * (7 + len(blocks)),
         out_specs=pl.BlockSpec((unroll, tiles, LANES), lambda k: (k, 0, 0)),
-        scratch_shapes=[VMEM((unroll, 3, size, 2 * LANES), BF16)] * 2,
-        compiler_params=limit(16),
+        scratch_shapes=halves(unroll, span),
+        compiler_params=limit(12),
         name="final",
-    )(*in_vmem(partial, *blocks, cs, *operands))
+    )(*in_vmem(done, partial, *blocks, cs, *lefts, *weights))
     return result.reshape(count, 1, size * size)
 
 
@@ -433,16 +466,19 @@
     return even, odd
 
 
+def chunks(lines):
+    return ((0, 2 * lines // 3), (2 * lines // 3, lines // 3))
+
+
 def neighbour_gather(parts, n):
     even, odd = edges(n)
-    plans = ((even, odd), (odd, even))
     moving = [p[None] for p in parts]
     held = [np.arange(n)[:, None] for _ in parts]
-    blocks, sources = [[], []], [[], []]
+    blocks, sources = [[] for _ in parts], [[] for _ in parts]
     for step in range(n // 2):
         arrived = []
-        for h, plan in enumerate(plans):
-            perm = plan[step % 2]
+        for h in range(len(parts)):
+            perm = (even, odd)[(step + h) % 2]
             arrived.append(lax.ppermute(moving[h], "row", perm))
             source = np.zeros_like(held[h])
             for a, b in perm:
@@ -451,7 +487,7 @@
                 source = np.concatenate([held[h], source], axis=1)
             held[h] = source
             sources[h].append(source)
-        for h in range(2):
+        for h in range(len(parts)):
             if step == 0:
                 arrived[h] = jnp.concatenate([moving[h], arrived[h]])
             moving[h] = arrived[h]
@@ -477,9 +513,7 @@
     half = size // 2
     total = slots * n_row
     modes = jnp.swapaxes(current_modes[0], 1, 2)
-    payload = pack(
-        modes, owner_id, triplets, center_point, live_count, bands, slots, total
-    )
+    payload = pack(modes, owner_id, triplets, center_point, bands, slots, total)
     bit = 1
     while bit < n_row:
         other = swap(payload, "row", bit, n_row)
@@ -490,40 +524,49 @@
     pieces = []
     for i in range(cuts):
         pieces += fetch(constants, i * width // cuts, width // cuts)
-    keep, send = contract(pieces, payload, other, bands)
-
-    keep = keep.reshape(bands // 2, 2, slots, half, 2 * size)
-    send = send.reshape(bands // 2, 2, slots, half, 2 * size)
-    got = swap(send, "ba", 1, n_ba)
-    far = swap(keep[1] + got[1], "ba", 2, n_ba)
-    own = (keep[0] + got[0]) + far
-    own = own.swapaxes(0, 1)
-
-    weights = prep(second_vectors, size, False)
-    lefts = prep(first_vectors, size, True)
-    operands = (*lefts, *weights)
+    spans = chunks(half)
+    weight = (jnp.arange(slots, dtype=jnp.int32) < live_count[0]).astype(F32)
+    owns = []
+    for base, lines in spans:
+        keep, send = contract(pieces, payload, other, bands, base, lines)
+        keep = keep.reshape(bands // 2, 2, slots, lines, 2 * size)
+        send = send.reshape(bands // 2, 2, slots, lines, 2 * size)
+        got = swap(send, "ba", 1, n_ba)
+        far = swap(keep[1] + got[1], "ba", 2, n_ba)
+        own = ((keep[0] + got[0]) + far) * weight[None, :, None, None]
+        owns.append(own.swapaxes(0, 1))
+
+    weights = prep(second_vectors, size, False, spans)
+    lefts = prep(first_vectors, size, True, spans)
     if slots == 1 and n_row <= 8:
-        parts = (own[0, :, : half // 2], own[0, :, half // 2 :])
+        parts, places = [], []
+        for own, (base, lines) in zip(owns, spans):
+            for start in (0, lines // 2):
+                parts.append(own[0, :, start : start + lines // 2])
+                places.append((base + start, lines // 2))
         blocks, sources = neighbour_gather(parts, n_row)
         order = np.concatenate(sources, axis=1)
-        ahead, behind = [], []
-        for h in range(2):
+        ahead, behind = [], [[] for _ in spans]
+        for h, (base, lines) in enumerate(places):
             slot = h * n_row
             for n, b in enumerate(blocks[h]):
                 here = range(slot, slot + b.shape[0])
-                entry = (b, (h * half // 2, half // 2, tuple(here)))
-                (behind if n == len(blocks[h]) - 1 else ahead).append(entry)
+                entry = (b, (base, lines, tuple(here)))
+                (behind[h // 2] if n == len(blocks[h]) - 1 else ahead).append(entry)
                 slot += b.shape[0]
     else:
-        gathered = lax.all_gather(own, "row", axis=0, tiled=True)
-        ahead, behind = [(gathered, (0, half, tuple(range(total))))], []
+        slots_all = tuple(range(total))
+        ahead, behind = [], [[] for _ in spans]
+        for own, (base, lines) in zip(owns, spans):
+            gathered = lax.all_gather(own, "row", axis=0, tiled=True)
+            ahead.append((gathered, (base, lines, slots_all)))
         order = np.broadcast_to(np.arange(total), (n_row, total))
     order = tuple(tuple(int(x) for x in line) for line in order)
     table = angles(payload, other, pair_points, 2 * bands, order)
-    arrays, spec = zip(*ahead)
-    partial = early(arrays, spec, table, pair_points.shape[0], half)
-    arrays, spec = zip(*behind) if behind else ((), ())
-    return final(partial, arrays, spec, table, operands, total)
+    partial = early(*zip(*ahead), table, pair_points.shape[0], half)
+    late = [tuple(zip(*b)) if b else ((), ()) for b in behind]
+    done = inner(spans[0], partial, *late[0], table, weights)
+    return final(spans[1], done, partial, *late[1], table, lefts, weights, total)
 
 
 def solution(mesh):

time: 68.4 us -> 78.5 us (1.15)
  starting transfers between devices: 18.7 us -> 30.4 us
  waiting for transfers between devices: 26.5 us -> 23.4 us
  Pallas kernels: 21.3 us -> 22.8 us
    ppermute x8 -> x16, starting transfers between devices: 8.92 us -> 19 us  [neighbour_gather(): arrived.append(lax.ppermute(moving[h], 'row', perm))]
    ppermute x5 -> x7, waiting for transfers between devices: 12.8 us -> 8.47 us  [swap(): return lax.ppermute(x, axis, [(i, i ^ bit) for i in range(n)])]
    ppermute x5 -> x7, starting transfers between devices: 9.83 us -> 11.4 us  [swap(): return lax.ppermute(x, axis, [(i, i ^ bit) for i in range(n)])]
    pallas_call x4 -> x6, Pallas kernels: 13 us -> 14.5 us  [the longest x2 6.09 us: prep(): pl.pallas_call(functools.partial(prep_kernel, size, turn, spans), out_sha...]
    ppermute x8 -> x16, waiting for transfers between devices: 13.7 us -> 14.9 us  [neighbour_gather(): arrived.append(lax.ppermute(moving[h], 'row', perm))]
  transfers between devices with their start and end apart: 13 -> 23, of which waited for: 10 -> 8; matrix products, arithmetic and copies ran while one was open for 0% -> 0% of each run, Pallas kernels for 20% -> 21%
where the time goes in v4:
time: 78.5 us; the launch traced here: 78.2 us
  starting transfers between devices  30.4 us (39%)
  waiting for transfers between devices  23.4 us (30%)
  Pallas kernels  22.8 us (29%)
  between operations  1.48 us (2%)
    ppermute x16, starting transfers between devices, neighbour_gather(): arrived.append(lax.ppermute(moving[h], 'row', perm))  19 us
    ppermute x16, waiting for transfers between devices, neighbour_gather(): arrived.append(lax.ppermute(moving[h], 'row', perm))  14.9 us
    ppermute x7, starting transfers between devices, swap(): return lax.ppermute(x, axis, [(i, i ^ bit) for i in range(n)])  11.4 us
    ppermute x7, waiting for transfers between devices, swap(): return lax.ppermute(x, axis, [(i, i ^ bit) for i in range(n)])  8.47 us
    pallas_call x2, Pallas kernels, prep(): pl.pallas_call(functools.partial(prep_kernel, size, turn, spans), out_sha...  6.09 us
    pallas_call x3, Pallas kernels, fetch(): pl.pallas_call(functools.partial(fetch_kernel, slots, first, rows, parts)...  5.14 us
    pallas_call x1, Pallas kernels, final(): pl.pallas_call(functools.partial(final_kernel, span, width, spec, 1.0 / t...  4.8 us
    pallas_call x1, Pallas kernels, inner(): pl.pallas_call(functools.partial(inner_kernel, span, cs.shape[1] // count...  2.12 us
  transfers between devices with their start and end apart: 23, of which 8 were waited for; matrix products, arithmetic and copies ran while one was open for 0% of the time, Pallas kernels for 21%

profile of v4, /device:TPU:0, one launch (start us, length us, event | category | flops | bytes accessed | tf_op | source)
XLA Modules:
  0.0 78.2 jit_solution(15023868368333926921)
XLA Ops:
  0.7 0.7 pack.1
  1.4 3.0 %collective-permute-start = (f32[16,128]{1,0:T(8,128)S(1)}, f32[16,128]{1,0:T(8,128)S(1)}, u32[]{:S(2)}, u32[]{:S(2)}) collective-permute-start(f32[16,128]{1,0:T(8,128)S(1)} %pack.1), channel_id=1, source_target_pairs={{0,4},{4,0},{8,12},{12,8},{16,20},{20,16},{24,28},{28,24},{1,5},{5... | collective-permute-start | bytes 24584 | tf_op jit(solution)/shard_map/ppermute | solution.py:456
  4.4 1.6 %collective-permute-done = f32[16,128]{1,0:T(8,128)S(1)} collective-permute-done((f32[16,128]{1,0:T(8,128)S(1)}, f32[16,128]{1,0:T(8,128)S(1)}, u32[]{:S(2)}, u32[]{:S(2)}) %collective-permute-start) | collective-permute-done | bytes 8224 | tf_op jit(solution)/shard_map/ppermute | solution.py:456
  6.1 2.1 %collective-permute-start.1 = (f32[16,128]{1,0:T(8,128)S(1)}, f32[16,128]{1,0:T(8,128)S(1)}, u32[]{:S(2)}, u32[]{:S(2)}) collective-permute-start(f32[16,128]{1,0:T(8,128)S(1)} %add.32), channel_id=1, source_target_pairs={{0,8},{4,12},{8,0},{12,4},{16,24},{20,28},{24,16},{28,20},{1,9},{5... | collective-permute-start | bytes 24584 | tf_op jit(solution)/shard_map/ppermute | solution.py:456
  8.2 1.6 %collective-permute-done.1 = f32[16,128]{1,0:T(8,128)S(1)} collective-permute-done((f32[16,128]{1,0:T(8,128)S(1)}, f32[16,128]{1,0:T(8,128)S(1)}, u32[]{:S(2)}, u32[]{:S(2)}) %collective-permute-start.1) | collective-permute-done | bytes 8224 | tf_op jit(solution)/shard_map/ppermute | solution.py:456
  9.8 3.0 %collective-permute-start.2 = (f32[16,128]{1,0:T(8,128)S(1)}, f32[16,128]{1,0:T(8,128)S(1)}, u32[]{:S(2)}, u32[]{:S(2)}) collective-permute-start(f32[16,128]{1,0:T(8,128)S(1)} %add.33.e0), channel_id=1, source_target_pairs={{0,16},{4,20},{8,24},{12,28},{16,0},{20,4},{24,8},{28,12},{1,17},{... | collective-permute-start | bytes 24584 | tf_op jit(solution)/shard_map/ppermute | solution.py:456
  12.8 1.7 %fetch.3 = (bf16[1,16,36864]{2,1,0:T(8,128)(2,1)S(1)}, bf16[1,16,36864]{2,1,0:T(8,128)(2,1)S(1)}) custom-call(f32[1,48,36864]{2,1,0:T(8,128)} %const.5), custom_call_target="tpu_custom_call" | custom-call | tf_op jit(solution)/shard_map/fetch/pallas_call | solution.py:119
  14.5 1.7 %fetch.5 = (bf16[1,16,36864]{2,1,0:T(8,128)(2,1)S(1)}, bf16[1,16,36864]{2,1,0:T(8,128)(2,1)S(1)}) custom-call(f32[1,48,36864]{2,1,0:T(8,128)} %const.5), custom_call_target="tpu_custom_call" | custom-call | tf_op jit(solution)/shard_map/fetch/pallas_call | solution.py:119
  16.3 1.7 %fetch.4 = (bf16[1,16,36864]{2,1,0:T(8,128)(2,1)S(1)}, bf16[1,16,36864]{2,1,0:T(8,128)(2,1)S(1)}) custom-call(f32[1,48,36864]{2,1,0:T(8,128)} %const.5), custom_call_target="tpu_custom_call" | custom-call | tf_op jit(solution)/shard_map/fetch/pallas_call | solution.py:119
  18.0 0.9 %contract.2 = (f32[4,1,64,384]{3,2,1,0:T(8,128)S(1)}, f32[4,1,64,384]{3,2,1,0:T(8,128)S(1)}) custom-call(f32[16,128]{1,0:T(8,128)S(1)} %add.33.e0, f32[16,128]{1,0:T(8,128)S(1)} %collective-permute-done.2.e1, bf16[1,16,36864]{2,1,0:T(8,128)(2,1)S(1)} %get-tuple-element.19.refs_0_, bf16[1,16,36864]{2,1,0:T(8,128)(2,1)S(1)} %get-tuple-element.20.refs_1_, ...), custom_call_target="tpu_custom_call" | custom-call | tf_op jit(solution)/shard_map/contract/pallas_call | solution.py:172
  18.9 0.1 collective-permute-start.3
  19.7 0.6 contract.3
  20.2 0.6 collective-permute-start.11
  20.8 1.6 %collective-permute-start.4 = (f32[2,1,64,384]{3,2,0,1:T(8,128)S(1)}, f32[2,1,64,384]{3,2,0,1:T(8,128)S(1)}, u32[]{:S(2)}, u32[]{:S(2)}) collective-permute-start(f32[2,1,64,384]{3,2,0,1:T(8,128)S(1)} %fusion), channel_id=1, source_target_pairs={{0,2},{1,3},{2,0},{3,1},{4,6},{5,7},{6,4},{7,5},{8,10},{9,11},{10,... | collective-permute-start | bytes 589832 | tf_op jit(solution)/shard_map/ppermute | solution.py:456
  22.4 0.0 collective-permute-done.11
  22.4 1.0 %collective-permute-start.12 = (f32[2,1,32,384]{3,2,0,1:T(8,128)S(1)}, f32[2,1,32,384]{3,2,0,1:T(8,128)S(1)}, u32[]{:S(2)}, u32[]{:S(2)}) collective-permute-start(f32[2,1,32,384]{3,2,0,1:T(8,128)S(1)} %fusion.5), channel_id=1, source_target_pairs={{0,2},{1,3},{2,0},{3,1},{4,6},{5,7},{6,4},{7,5},{8,10},{9,11},{10,... | collective-permute-start | bytes 294920 | tf_op jit(solution)/shard_map/ppermute | solution.py:456
  23.5 5.2 %collective-permute-done.4 = f32[2,1,64,384]{3,2,0,1:T(8,128)S(1)} collective-permute-done((f32[2,1,64,384]{3,2,0,1:T(8,128)S(1)}, f32[2,1,64,384]{3,2,0,1:T(8,128)S(1)}, u32[]{:S(2)}, u32[]{:S(2)}) %collective-permute-start.4) | collective-permute-done | bytes 196640 | tf_op jit(solution)/shard_map/ppermute | solution.py:456
  28.7 1.6 %collective-permute-start.5 = (f32[1,2,32,384]{3,2,1,0:T(8,128)S(1)}, f32[1,2,32,384]{3,2,1,0:T(8,128)S(1)}, u32[]{:S(2)}, u32[]{:S(2)}) collective-permute-start(f32[1,2,32,384]{3,2,1,0:T(8,128)S(1)} %get-tuple-element.34), channel_id=1, source_target_pairs={{0,8},{8,0},{16,24},{24,16},{28,20},{20,28},{12,4},{4,12},{1,9},{9... | collective-permute-start | bytes 294920 | tf_op jit(solution)/shard_map/ppermute | solution.py:482
  30.4 1.6 %collective-permute-start.8 = (f32[1,2,32,384]{3,2,1,0:T(8,128)S(1)}, f32[1,2,32,384]{3,2,1,0:T(8,128)S(1)}, u32[]{:S(2)}, u32[]{:S(2)}) collective-permute-start(f32[1,2,32,384]{3,2,1,0:T(8,128)S(1)} %get-tuple-element.33), channel_id=1, source_target_pairs={{8,16},{16,8},{24,28},{28,24},{20,12},{12,20},{4,0},{0,4},{9,17},{... | collective-permute-start | bytes 294920 | tf_op jit(solution)/shard_map/ppermute | solution.py:482
  32.0 1.5 %collective-permute-done.5 = f32[1,2,32,384]{3,2,1,0:T(8,128)S(1)} collective-permute-done((f32[1,2,32,384]{3,2,1,0:T(8,128)S(1)}, f32[1,2,32,384]{3,2,1,0:T(8,128)S(1)}, u32[]{:S(2)}, u32[]{:S(2)}) %collective-permute-start.5) | collective-permute-done | bytes 98336 | tf_op jit(solution)/shard_map/ppermute | solution.py:482
  33.4 1.6 %collective-permute-start.6 = (f32[2,2,32,384]{3,2,1,0:T(8,128)S(1)}, f32[2,2,32,384]{3,2,1,0:T(8,128)S(1)}, u32[]{:S(2)}, u32[]{:S(2)}) collective-permute-start(f32[2,2,32,384]{3,2,1,0:T(8,128)S(1)} %pad_maximum_fusion.refs_0_), channel_id=1, source_target_pairs={{8,16},{16,8},{24,28},{28,24},{20,12},{12,20},{4,0},{0,4},{9,17},{... | collective-permute-start | bytes 589832 | tf_op jit(solution)/shard_map/ppermute | solution.py:482
  35.0 1.1 %collective-permute-done.8 = f32[1,2,32,384]{3,2,1,0:T(8,128)S(1)} collective-permute-done((f32[1,2,32,384]{3,2,1,0:T(8,128)S(1)}, f32[1,2,32,384]{3,2,1,0:T(8,128)S(1)}, u32[]{:S(2)}, u32[]{:S(2)}) %collective-permute-start.8) | collective-permute-done | bytes 98336 | tf_op jit(solution)/shard_map/ppermute | solution.py:482
  36.1 1.1 %collective-permute-start.9 = (f32[2,2,32,384]{3,2,1,0:T(8,128)S(1)}, f32[2,2,32,384]{3,2,1,0:T(8,128)S(1)}, u32[]{:S(2)}, u32[]{:S(2)}) collective-permute-start(f32[2,2,32,384]{3,2,1,0:T(8,128)S(1)} %pad_maximum_fusion.1.refs_3_), channel_id=1, source_target_pairs={{0,8},{8,0},{16,24},{24,16},{28,20},{20,28},{12,4},{4,12},{1,9},{9... | collective-permute-start | bytes 589832 | tf_op jit(solution)/shard_map/ppermute | solution.py:482
  37.3 1.0 %collective-permute-start.13 = (f32[1,2,16,384]{3,2,1,0:T(8,128)S(1)}, f32[1,2,16,384]{3,2,1,0:T(8,128)S(1)}, u32[]{:S(2)}, u32[]{:S(2)}) collective-permute-start(f32[1,2,16,384]{3,2,1,0:T(8,128)S(1)} %get-tuple-element.36), channel_id=1, source_target_pairs={{0,8},{8,0},{16,24},{24,16},{28,20},{20,28},{12,4},{4,12},{1,9},{9... | collective-permute-start | bytes 147464 | tf_op jit(solution)/shard_map/ppermute | solution.py:482
  38.3 1.5 %collective-permute-start.16 = (f32[1,2,16,384]{3,2,1,0:T(8,128)S(1)}, f32[1,2,16,384]{3,2,1,0:T(8,128)S(1)}, u32[]{:S(2)}, u32[]{:S(2)}) collective-permute-start(f32[1,2,16,384]{3,2,1,0:T(8,128)S(1)} %get-tuple-element.35), channel_id=1, source_target_pairs={{8,16},{16,8},{24,28},{28,24},{20,12},{12,20},{4,0},{0,4},{9,17},{... | collective-permute-start | bytes 147464 | tf_op jit(solution)/shard_map/ppermute | solution.py:482
  39.8 2.8 %collective-permute-done.13 = f32[1,2,16,384]{3,2,1,0:T(8,128)S(1)} collective-permute-done((f32[1,2,16,384]{3,2,1,0:T(8,128)S(1)}, f32[1,2,16,384]{3,2,1,0:T(8,128)S(1)}, u32[]{:S(2)}, u32[]{:S(2)}) %collective-permute-start.13) | collective-permute-done | bytes 49184 | tf_op jit(solution)/shard_map/ppermute | solution.py:482
  42.6 2.5 %collective-permute-start.14 = (f32[2,2,16,384]{3,2,1,0:T(8,128)S(1)}, f32[2,2,16,384]{3,2,1,0:T(8,128)S(1)}, u32[]{:S(2)}, u32[]{:S(2)}) collective-permute-start(f32[2,2,16,384]{3,2,1,0:T(8,128)S(1)} %pad_maximum_fusion.2.refs_6_), channel_id=1, source_target_pairs={{8,16},{16,8},{24,28},{28,24},{20,12},{12,20},{4,0},{0,4},{9,17},{... | collective-permute-start | bytes 294920 | tf_op jit(solution)/shard_map/ppermute | solution.py:482
  45.1 0.0 collective-permute-done.6.refs_1_
  45.1 0.0 collective-permute-start.7
  45.1 0.8 %collective-permute-start.10 = (f32[2,2,32,384]{3,2,1,0:T(8,128)S(1)}, f32[2,2,32,384]{3,2,1,0:T(8,128)S(1)}, u32[]{:S(2)}, u32[]{:S(2)}) collective-permute-start(f32[2,2,32,384]{3,2,1,0:T(8,128)S(1)} %collective-permute-done.9.refs_4_), channel_id=1, source_target_pairs={{8,16},{16,8},{24,28},{28,24},{20,12},{12,20},{4,0},{0,4},{9,17},{... | collective-permute-start | bytes 589832 | tf_op jit(solution)/shard_map/ppermute | solution.py:482
  45.9 0.0 collective-permute-done.16
  46.0 1.3 %collective-permute-start.17 = (f32[2,2,16,384]{3,2,1,0:T(8,128)S(1)}, f32[2,2,16,384]{3,2,1,0:T(8,128)S(1)}, u32[]{:S(2)}, u32[]{:S(2)}) collective-permute-start(f32[2,2,16,384]{3,2,1,0:T(8,128)S(1)} %pad_maximum_fusion.3.refs_9_), channel_id=1, source_target_pairs={{0,8},{8,0},{16,24},{24,16},{28,20},{20,28},{12,4},{4,12},{1,9},{9... | collective-permute-start | bytes 294920 | tf_op jit(solution)/shard_map/ppermute | solution.py:482
  47.3 5.7 %collective-permute-done.7.refs_2_ = f32[2,2,32,384]{3,2,1,0:T(8,128)S(1)} collective-permute-done((f32[2,2,32,384]{3,2,1,0:T(8,128)S(1)}, f32[2,2,32,384]{3,2,1,0:T(8,128)S(1)}, u32[]{:S(2)}, u32[]{:S(2)}) %collective-permute-start.7) | collective-permute-done | bytes 196640 | tf_op jit(solution)/shard_map/ppermute | solution.py:482
  52.9 0.1 collective-permute-start.19
  53.0 1.2 %collective-permute-start.20 = (f32[2,2,32,384]{3,2,1,0:T(8,128)S(1)}, f32[2,2,32,384]{3,2,1,0:T(8,128)S(1)}, u32[]{:S(2)}, u32[]{:S(2)}) collective-permute-start(f32[2,2,32,384]{3,2,1,0:T(8,128)S(1)} %collective-permute-done.10.refs_5_), channel_id=1, source_target_pairs={{0,8},{8,0},{16,24},{24,16},{28,20},{20,28},{12,4},{4,12},{1,9},{9... | collective-permute-start | bytes 589832 | tf_op jit(solution)/shard_map/ppermute | solution.py:482
  54.2 0.8 %collective-permute-start.15 = (f32[2,2,16,384]{3,2,1,0:T(8,128)S(1)}, f32[2,2,16,384]{3,2,1,0:T(8,128)S(1)}, u32[]{:S(2)}, u32[]{:S(2)}) collective-permute-start(f32[2,2,16,384]{3,2,1,0:T(8,128)S(1)} %collective-permute-done.14.refs_7_), channel_id=1, source_target_pairs={{0,8},{8,0},{16,24},{24,16},{28,20},{20,28},{12,4},{4,12},{1,9},{9... | collective-permute-start | bytes 294920 | tf_op jit(solution)/shard_map/ppermute | solution.py:482
  55.0 0.0 collective-permute-done.17.refs_10_
  55.0 1.9 %collective-permute-start.18 = (f32[2,2,16,384]{3,2,1,0:T(8,128)S(1)}, f32[2,2,16,384]{3,2,1,0:T(8,128)S(1)}, u32[]{:S(2)}, u32[]{:S(2)}) collective-permute-start(f32[2,2,16,384]{3,2,1,0:T(8,128)S(1)} %collective-permute-done.17.refs_10_), channel_id=1, source_target_pairs={{8,16},{16,8},{24,28},{28,24},{20,12},{12,20},{4,0},{0,4},{9,17},{... | collective-permute-start | bytes 294920 | tf_op jit(solution)/shard_map/ppermute | solution.py:482
  57.0 3.8 %collective-permute-done.15.refs_8_ = f32[2,2,16,384]{3,2,1,0:T(8,128)S(1)} collective-permute-done((f32[2,2,16,384]{3,2,1,0:T(8,128)S(1)}, f32[2,2,16,384]{3,2,1,0:T(8,128)S(1)}, u32[]{:S(2)}, u32[]{:S(2)}) %collective-permute-start.15) | collective-permute-done | bytes 98336 | tf_op jit(solution)/shard_map/ppermute | solution.py:482
  60.8 1.8 %collective-permute-start.21 = (f32[2,2,16,384]{3,2,1,0:T(8,128)S(1)}, f32[2,2,16,384]{3,2,1,0:T(8,128)S(1)}, u32[]{:S(2)}, u32[]{:S(2)}) collective-permute-start(f32[2,2,16,384]{3,2,1,0:T(8,128)S(1)} %collective-permute-done.15.refs_8_), channel_id=1, source_target_pairs={{8,16},{16,8},{24,28},{28,24},{20,12},{12,20},{4,0},{0,4},{9,17},{... | collective-permute-start | bytes 294920 | tf_op jit(solution)/shard_map/ppermute | solution.py:482
  62.6 0.1 collective-permute-start.22
  62.7 3.4 %prep.3 = (bf16[8,3,192,192]{3,2,1,0:T(8,128)(2,1)S(1)}, bf16[8,3,192,192]{3,2,1,0:T(8,128)(2,1)S(1)}) custom-call(f32[8,576,128]{2,1,0:T(8,128)} %bitcast.59), custom_call_target="tpu_custom_call" | custom-call | tf_op jit(solution)/shard_map/prep/pallas_call | solution.py:239
  66.2 2.6 %prep.2 = (bf16[8,3,192,192]{3,2,1,0:T(8,128)(2,1)S(1)}, bf16[8,3,192,192]{3,2,1,0:T(8,128)(2,1)S(1)}) custom-call(f32[8,576,128]{2,1,0:T(8,128)} %bitcast.60), custom_call_target="tpu_custom_call" | custom-call | tf_op jit(solution)/shard_map/prep/pallas_call | solution.py:239
  68.8 0.4 angles.1.refs_12_.refs_2_
  69.3 2.0 %early.1.partial = f32[8,2,96,384]{3,2,1,0:T(8,128)S(1)} custom-call(f32[2,2,32,384]{3,2,1,0:T(8,128)S(1)} %pad_maximum_fusion.refs_0_, f32[2,2,32,384]{3,2,1,0:T(8,128)S(1)} %collective-permute-done.6.refs_1_, f32[2,2,32,384]{3,2,1,0:T(8,128)S(1)} %collective-permute-done.7.refs_2_, f32[2,2,32,384]{3,2,1,0:T(8,128)S(1)} %pad_maximum_fusion.1.refs_3_, ...), custom_call_target="tpu_custom_call" | custom-call | tf_op jit(solution)/shard_map/early/pallas_call | solution.py:336
  71.2 0.0 collective-permute-done.20.refs_1_
  71.2 2.1 %inner.1.done = f32[8,2,128,192]{3,2,1,0:T(8,128)S(1)} custom-call(f32[8,2,96,384]{3,2,1,0:T(8,128)S(1)} %early.1.partial, f32[2,2,32,384]{3,2,1,0:T(8,128)S(1)} %collective-permute-done.19.refs_0_, f32[2,2,32,384]{3,2,1,0:T(8,128)S(1)} %collective-permute-done.20.refs_1_, f32[2,256,128]{2,1,0:T(8,128)S(1)} %angles.1.refs_12_.refs_2_, ...), custom_call_target="tpu_custom_call" | custom-call | tf_op jit(solution)/shard_map/inner/pallas_call | solution.py:393
  73.4 4.8 %final.1 = f32[8,288,128]{2,1,0:T(8,128)} custom-call(f32[8,2,128,192]{3,2,1,0:T(8,128)S(1)} %inner.1.done, f32[8,2,96,384]{3,2,1,0:T(8,128)S(1)} %early.1.partial, f32[2,2,16,384]{3,2,1,0:T(8,128)S(1)} %collective-permute-done.21.refs_0_, f32[2,2,16,384]{3,2,1,0:T(8,128)S(1)} %collective-permute-done.22.refs_1_, f32[2,256,128]{2,1,0:T(8,128)S(1)} %angles.1.refs_12_.refs_2_, ...), custom_call_target="tpu_custom_call" | custom-call | tf_op jit(solution)/shard_map/final/pallas_call | solution.py:442
  (24 shorter events, 0.2 us)
Async XLA Ops:
  1.4 4.7 %collective-permute-start = (f32[16,128]{1,0:T(8,128)S(1)}, f32[16,128]{1,0:T(8,128)S(1)}, u32[]{:S(2)}, u32[]{:S(2)}) collective-permute-start(f32[16,128]{1,0:T(8,128)S(1)} %pack.1), channel_id=1, source_target_pairs={{0,4},{4,0},{8,12},{12,8},{16,20},{20,16},{24,28},{28,24},{1,5},{5... | collective-permute-start | bytes 24584 | tf_op jit(solution)/shard_map/ppermute | solution.py:456
  6.1 3.7 %collective-permute-start.1 = (f32[16,128]{1,0:T(8,128)S(1)}, f32[16,128]{1,0:T(8,128)S(1)}, u32[]{:S(2)}, u32[]{:S(2)}) collective-permute-start(f32[16,128]{1,0:T(8,128)S(1)} %add.32), channel_id=1, source_target_pairs={{0,8},{4,12},{8,0},{12,4},{16,24},{20,28},{24,16},{28,20},{1,9},{5... | collective-permute-start | bytes 24584 | tf_op jit(solution)/shard_map/ppermute | solution.py:456
  9.8 8.2 %collective-permute-start.2 = (f32[16,128]{1,0:T(8,128)S(1)}, f32[16,128]{1,0:T(8,128)S(1)}, u32[]{:S(2)}, u32[]{:S(2)}) collective-permute-start(f32[16,128]{1,0:T(8,128)S(1)} %add.33.e0), channel_id=1, source_target_pairs={{0,16},{4,20},{8,24},{12,28},{16,0},{20,4},{24,8},{28,12},{1,17},{... | collective-permute-start | bytes 24584 | tf_op jit(solution)/shard_map/ppermute | solution.py:456
  18.9 1.9 %collective-permute-start.3 = (f32[2,2,1,64,384]{4,3,1,2,0:T(8,128)S(1)}, f32[2,2,1,64,384]{4,3,1,2,0:T(8,128)S(1)}, u32[]{:S(2)}, u32[]{:S(2)}) collective-permute-start(f32[2,2,1,64,384]{4,3,1,2,0:T(8,128)S(1)} %bitcast.57), channel_id=1, source_target_pairs={{0,1},{1,0},{2,3},{3,2},{4,5},{5,4},{6,7},{7,6},{8,9},{9,8},{10,11... | collective-permute-start | bytes 1179656 | tf_op jit(solution)/shard_map/ppermute | solution.py:456
  20.2 2.2 %collective-permute-start.11 = (f32[2,2,1,32,384]{4,3,1,2,0:T(8,128)S(1)}, f32[2,2,1,32,384]{4,3,1,2,0:T(8,128)S(1)}, u32[]{:S(2)}, u32[]{:S(2)}) collective-permute-start(f32[2,2,1,32,384]{4,3,1,2,0:T(8,128)S(1)} %bitcast.58), channel_id=1, source_target_pairs={{0,1},{1,0},{2,3},{3,2},{4,5},{5,4},{6,7},{7,6},{8,9},{9,8},{10,11... | collective-permute-start | bytes 589832 | tf_op jit(solution)/shard_map/ppermute | solution.py:456
  20.8 7.8 %collective-permute-start.4 = (f32[2,1,64,384]{3,2,0,1:T(8,128)S(1)}, f32[2,1,64,384]{3,2,0,1:T(8,128)S(1)}, u32[]{:S(2)}, u32[]{:S(2)}) collective-permute-start(f32[2,1,64,384]{3,2,0,1:T(8,128)S(1)} %fusion), channel_id=1, source_target_pairs={{0,2},{1,3},{2,0},{3,1},{4,6},{5,7},{6,4},{7,5},{8,10},{9,11},{10,... | collective-permute-start | bytes 589832 | tf_op jit(solution)/shard_map/ppermute | solution.py:456
  22.4 7.9 %collective-permute-start.12 = (f32[2,1,32,384]{3,2,0,1:T(8,128)S(1)}, f32[2,1,32,384]{3,2,0,1:T(8,128)S(1)}, u32[]{:S(2)}, u32[]{:S(2)}) collective-permute-start(f32[2,1,32,384]{3,2,0,1:T(8,128)S(1)} %fusion.5), channel_id=1, source_target_pairs={{0,2},{1,3},{2,0},{3,1},{4,6},{5,7},{6,4},{7,5},{8,10},{9,11},{10,... | collective-permute-start | bytes 294920 | tf_op jit(solution)/shard_map/ppermute | solution.py:456
  28.7 4.7 %collective-permute-start.5 = (f32[1,2,32,384]{3,2,1,0:T(8,128)S(1)}, f32[1,2,32,384]{3,2,1,0:T(8,128)S(1)}, u32[]{:S(2)}, u32[]{:S(2)}) collective-permute-start(f32[1,2,32,384]{3,2,1,0:T(8,128)S(1)} %get-tuple-element.34), channel_id=1, source_target_pairs={{0,8},{8,0},{16,24},{24,16},{28,20},{20,28},{12,4},{4,12},{1,9},{9... | collective-permute-start | bytes 294920 | tf_op jit(solution)/shard_map/ppermute | solution.py:482
  30.4 5.7 %collective-permute-start.8 = (f32[1,2,32,384]{3,2,1,0:T(8,128)S(1)}, f32[1,2,32,384]{3,2,1,0:T(8,128)S(1)}, u32[]{:S(2)}, u32[]{:S(2)}) collective-permute-start(f32[1,2,32,384]{3,2,1,0:T(8,128)S(1)} %get-tuple-element.33), channel_id=1, source_target_pairs={{8,16},{16,8},{24,28},{28,24},{20,12},{12,20},{4,0},{0,4},{9,17},{... | collective-permute-start | bytes 294920 | tf_op jit(solution)/shard_map/ppermute | solution.py:482
  33.4 11.7 %collective-permute-start.6 = (f32[2,2,32,384]{3,2,1,0:T(8,128)S(1)}, f32[2,2,32,384]{3,2,1,0:T(8,128)S(1)}, u32[]{:S(2)}, u32[]{:S(2)}) collective-permute-start(f32[2,2,32,384]{3,2,1,0:T(8,128)S(1)} %pad_maximum_fusion.refs_0_), channel_id=1, source_target_pairs={{8,16},{16,8},{24,28},{28,24},{20,12},{12,20},{4,0},{0,4},{9,17},{... | collective-permute-start | bytes 589832 | tf_op jit(solution)/shard_map/ppermute | solution.py:482
  36.1 9.0 %collective-permute-start.9 = (f32[2,2,32,384]{3,2,1,0:T(8,128)S(1)}, f32[2,2,32,384]{3,2,1,0:T(8,128)S(1)}, u32[]{:S(2)}, u32[]{:S(2)}) collective-permute-start(f32[2,2,32,384]{3,2,1,0:T(8,128)S(1)} %pad_maximum_fusion.1.refs_3_), channel_id=1, source_target_pairs={{0,8},{8,0},{16,24},{24,16},{28,20},{20,28},{12,4},{4,12},{1,9},{9... | collective-permute-start | bytes 589832 | tf_op jit(solution)/shard_map/ppermute | solution.py:482
  37.3 5.3 %collective-permute-start.13 = (f32[1,2,16,384]{3,2,1,0:T(8,128)S(1)}, f32[1,2,16,384]{3,2,1,0:T(8,128)S(1)}, u32[]{:S(2)}, u32[]{:S(2)}) collective-permute-start(f32[1,2,16,384]{3,2,1,0:T(8,128)S(1)} %get-tuple-element.36), channel_id=1, source_target_pairs={{0,8},{8,0},{16,24},{24,16},{28,20},{20,28},{12,4},{4,12},{1,9},{9... | collective-permute-start | bytes 147464 | tf_op jit(solution)/shard_map/ppermute | solution.py:482
  38.3 7.6 %collective-permute-start.16 = (f32[1,2,16,384]{3,2,1,0:T(8,128)S(1)}, f32[1,2,16,384]{3,2,1,0:T(8,128)S(1)}, u32[]{:S(2)}, u32[]{:S(2)}) collective-permute-start(f32[1,2,16,384]{3,2,1,0:T(8,128)S(1)} %get-tuple-element.35), channel_id=1, source_target_pairs={{8,16},{16,8},{24,28},{28,24},{20,12},{12,20},{4,0},{0,4},{9,17},{... | collective-permute-start | bytes 147464 | tf_op jit(solution)/shard_map/ppermute | solution.py:482
  42.6 11.6 %collective-permute-start.14 = (f32[2,2,16,384]{3,2,1,0:T(8,128)S(1)}, f32[2,2,16,384]{3,2,1,0:T(8,128)S(1)}, u32[]{:S(2)}, u32[]{:S(2)}) collective-permute-start(f32[2,2,16,384]{3,2,1,0:T(8,128)S(1)} %pad_maximum_fusion.2.refs_6_), channel_id=1, source_target_pairs={{8,16},{16,8},{24,28},{28,24},{20,12},{12,20},{4,0},{0,4},{9,17},{... | collective-permute-start | bytes 294920 | tf_op jit(solution)/shard_map/ppermute | solution.py:482
  45.1 7.8 %collective-permute-start.7 = (f32[2,2,32,384]{3,2,1,0:T(8,128)S(1)}, f32[2,2,32,384]{3,2,1,0:T(8,128)S(1)}, u32[]{:S(2)}, u32[]{:S(2)}) collective-permute-start(f32[2,2,32,384]{3,2,1,0:T(8,128)S(1)} %collective-permute-done.6.refs_1_), channel_id=1, source_target_pairs={{0,8},{8,0},{16,24},{24,16},{28,20},{20,28},{12,4},{4,12},{1,9},{9... | collective-permute-start | bytes 589832 | tf_op jit(solution)/shard_map/ppermute | solution.py:482
  45.1 7.9 %collective-permute-start.10 = (f32[2,2,32,384]{3,2,1,0:T(8,128)S(1)}, f32[2,2,32,384]{3,2,1,0:T(8,128)S(1)}, u32[]{:S(2)}, u32[]{:S(2)}) collective-permute-start(f32[2,2,32,384]{3,2,1,0:T(8,128)S(1)} %collective-permute-done.9.refs_4_), channel_id=1, source_target_pairs={{8,16},{16,8},{24,28},{28,24},{20,12},{12,20},{4,0},{0,4},{9,17},{... | collective-permute-start | bytes 589832 | tf_op jit(solution)/shard_map/ppermute | solution.py:482
  46.0 9.1 %collective-permute-start.17 = (f32[2,2,16,384]{3,2,1,0:T(8,128)S(1)}, f32[2,2,16,384]{3,2,1,0:T(8,128)S(1)}, u32[]{:S(2)}, u32[]{:S(2)}) collective-permute-start(f32[2,2,16,384]{3,2,1,0:T(8,128)S(1)} %pad_maximum_fusion.3.refs_9_), channel_id=1, source_target_pairs={{0,8},{8,0},{16,24},{24,16},{28,20},{20,28},{12,4},{4,12},{1,9},{9... | collective-permute-start | bytes 294920 | tf_op jit(solution)/shard_map/ppermute | solution.py:482
  52.9 18.3 %collective-permute-start.19 = (f32[2,2,32,384]{3,2,1,0:T(8,128)S(1)}, f32[2,2,32,384]{3,2,1,0:T(8,128)S(1)}, u32[]{:S(2)}, u32[]{:S(2)}) collective-permute-start(f32[2,2,32,384]{3,2,1,0:T(8,128)S(1)} %collective-permute-done.7.refs_2_), channel_id=1, source_target_pairs={{8,16},{16,8},{24,28},{28,24},{20,12},{12,20},{4,0},{0,4},{9,17},{... | collective-permute-start | bytes 589832 | tf_op jit(solution)/shard_map/ppermute | solution.py:482
  53.0 18.2 %collective-permute-start.20 = (f32[2,2,32,384]{3,2,1,0:T(8,128)S(1)}, f32[2,2,32,384]{3,2,1,0:T(8,128)S(1)}, u32[]{:S(2)}, u32[]{:S(2)}) collective-permute-start(f32[2,2,32,384]{3,2,1,0:T(8,128)S(1)} %collective-permute-done.10.refs_5_), channel_id=1, source_target_pairs={{0,8},{8,0},{16,24},{24,16},{28,20},{20,28},{12,4},{4,12},{1,9},{9... | collective-permute-start | bytes 589832 | tf_op jit(solution)/shard_map/ppermute | solution.py:482
  54.2 6.5 %collective-permute-start.15 = (f32[2,2,16,384]{3,2,1,0:T(8,128)S(1)}, f32[2,2,16,384]{3,2,1,0:T(8,128)S(1)}, u32[]{:S(2)}, u32[]{:S(2)}) collective-permute-start(f32[2,2,16,384]{3,2,1,0:T(8,128)S(1)} %collective-permute-done.14.refs_7_), channel_id=1, source_target_pairs={{0,8},{8,0},{16,24},{24,16},{28,20},{20,28},{12,4},{4,12},{1,9},{9... | collective-permute-start | bytes 294920 | tf_op jit(solution)/shard_map/ppermute | solution.py:482
  55.0 7.5 %collective-permute-start.18 = (f32[2,2,16,384]{3,2,1,0:T(8,128)S(1)}, f32[2,2,16,384]{3,2,1,0:T(8,128)S(1)}, u32[]{:S(2)}, u32[]{:S(2)}) collective-permute-start(f32[2,2,16,384]{3,2,1,0:T(8,128)S(1)} %collective-permute-done.17.refs_10_), channel_id=1, source_target_pairs={{8,16},{16,8},{24,28},{28,24},{20,12},{12,20},{4,0},{0,4},{9,17},{... | collective-permute-start | bytes 294920 | tf_op jit(solution)/shard_map/ppermute | solution.py:482
  60.8 12.6 %collective-permute-start.21 = (f32[2,2,16,384]{3,2,1,0:T(8,128)S(1)}, f32[2,2,16,384]{3,2,1,0:T(8,128)S(1)}, u32[]{:S(2)}, u32[]{:S(2)}) collective-permute-start(f32[2,2,16,384]{3,2,1,0:T(8,128)S(1)} %collective-permute-done.15.refs_8_), channel_id=1, source_target_pairs={{8,16},{16,8},{24,28},{28,24},{20,12},{12,20},{4,0},{0,4},{9,17},{... | collective-permute-start | bytes 294920 | tf_op jit(solution)/shard_map/ppermute | solution.py:482
  62.6 10.8 %collective-permute-start.22 = (f32[2,2,16,384]{3,2,1,0:T(8,128)S(1)}, f32[2,2,16,384]{3,2,1,0:T(8,128)S(1)}, u32[]{:S(2)}, u32[]{:S(2)}) collective-permute-start(f32[2,2,16,384]{3,2,1,0:T(8,128)S(1)} %collective-permute-done.18.refs_11_), channel_id=1, source_target_pairs={{0,8},{8,0},{16,24},{24,16},{28,20},{20,28},{12,4},{4,12},{1,9},{9... | collective-permute-start | bytes 294920 | tf_op jit(solution)/shard_map/ppermute | solution.py:482
  62.7 6.1 %copy-start = (s32[8,3]{0,1:T(4,128)S(1)}, s32[8,3]{0,1:T(4,128)}, u32[]{:S(2)}) copy-start(s32[8,3]{0,1:T(4,128)} %param.15) | copy-start | bytes 292

commit v5 on v4

--- a/solution.py
+++ b/solution.py
@@ -10,6 +10,7 @@
 from jax.sharding import PartitionSpec as P
 
 G = 32
+FIRST = 1
 FULL_TURN = 2.0 * math.pi
 LANES = 128
 F32 = jnp.float32
@@ -389,7 +390,7 @@
 
 def inner(span, partial, blocks, spec, cs, weights):
     count, _, size, _ = weights[0].shape
-    unroll = 2 if count % 2 == 0 else 1
+    unroll = 4 if count % 4 == 0 else 1
     return pl.pallas_call(
         functools.partial(inner_kernel, span, cs.shape[1] // count, spec, size, unroll),
         out_shape=kept((count, 2, 2 * span[1], size)),
@@ -397,7 +398,7 @@
         in_specs=[WHOLE] * (4 + len(blocks)),
         out_specs=WHOLE,
         scratch_shapes=halves(unroll, span),
-        compiler_params=limit(8),
+        compiler_params=limit(12),
         name="inner",
     )(*in_vmem(partial, *blocks, cs, *weights))
 
@@ -437,7 +438,7 @@
 def final(span, done, partial, blocks, spec, cs, lefts, weights, total):
     count, _, size, _ = weights[0].shape
     tiles = size * size // LANES
-    unroll = 2 if count % 2 == 0 else 1
+    unroll = 4 if count % 4 == 0 else 1
     width = cs.shape[1] // count
     result = pl.pallas_call(
         functools.partial(final_kernel, span, width, spec, 1.0 / total, size, unroll),
@@ -446,7 +447,7 @@
         in_specs=[WHOLE] * (7 + len(blocks)),
         out_specs=pl.BlockSpec((unroll, tiles, LANES), lambda k: (k, 0, 0)),
         scratch_shapes=halves(unroll, span),
-        compiler_params=limit(12),
+        compiler_params=limit(20),
         name="final",
     )(*in_vmem(done, partial, *blocks, cs, *lefts, *weights))
     return result.reshape(count, 1, size * size)
@@ -514,12 +515,20 @@
     total = slots * n_row
     modes = jnp.swapaxes(current_modes[0], 1, 2)
     payload = pack(modes, owner_id, triplets, center_point, bands, slots, total)
-    bit = 1
+    bit, hop = 1, 0
     while bit < n_row:
-        other = swap(payload, "row", bit, n_row)
-        bit = bit * 2
-        if bit < n_row:
-            payload = payload + other
+        if bit == FIRST and n_row >= 4 * bit:
+            others = []
+            for i in (1, 2, 3):
+                others.append(swap(payload, "row", i * bit, n_row))
+            bit *= 4
+            payload = payload + others[0] + others[1] + others[2]
+        else:
+            other = swap(payload, "row", bit, n_row)
+            bit *= 2
+            if bit < n_row:
+                payload = payload + other
+        hop += 1
     cuts = 3 if width % 48 == 0 else 1
     pieces = []
     for i in range(cuts):

time: 78.5 us -> 76 us (0.968)
  starting transfers between devices: 30.4 us -> 23.9 us
  waiting for transfers between devices: 23.4 us -> 28.4 us
  Pallas kernels: 22.8 us -> 21.7 us
    ppermute x16, starting transfers between devices: 19 us -> 13.4 us  [neighbour_gather(): arrived.append(lax.ppermute(moving[h], 'row', perm))]
    ppermute x16, waiting for transfers between devices: 14.9 us -> 19.8 us  [neighbour_gather(): arrived.append(lax.ppermute(moving[h], 'row', perm))]
    ppermute x7 -> x8, starting transfers between devices: 11.4 us -> 10.5 us  [swap(): return lax.ppermute(x, axis, [(i, i ^ bit) for i in range(n)])]
    ppermute x7 -> x8, waiting for transfers between devices: 8.47 us -> 8.67 us  [swap(): return lax.ppermute(x, axis, [(i, i ^ bit) for i in range(n)])]
  transfers between devices with their start and end apart: 23 -> 24, of which waited for: 8 -> 9; matrix products, arithmetic and copies ran while one was open for 0% -> 0% of each run, Pallas kernels for 21% -> 21%
where the time goes in v5:
time: 76 us; the launch traced here: 75.7 us
  waiting for transfers between devices  28.4 us (37%)
  starting transfers between devices  23.9 us (31%)
  Pallas kernels  21.7 us (29%)
  between operations  1.49 us (2%)
    ppermute x16, waiting for transfers between devices, neighbour_gather(): arrived.append(lax.ppermute(moving[h], 'row', perm))  19.8 us
    ppermute x16, starting transfers between devices, neighbour_gather(): arrived.append(lax.ppermute(moving[h], 'row', perm))  13.4 us
    ppermute x8, starting transfers between devices, swap(): return lax.ppermute(x, axis, [(i, i ^ bit) for i in range(n)])  10.5 us
    ppermute x8, waiting for transfers between devices, swap(): return lax.ppermute(x, axis, [(i, i ^ bit) for i in range(n)])  8.67 us
    pallas_call x2, Pallas kernels, prep(): pl.pallas_call(functools.partial(prep_kernel, size, turn, spans), out_sha...  6.09 us
    pallas_call x3, Pallas kernels, fetch(): pl.pallas_call(functools.partial(fetch_kernel, slots, first, rows, parts)...  5.14 us
    pallas_call x1, Pallas kernels, final(): pl.pallas_call(functools.partial(final_kernel, span, width, spec, 1.0 / t...  4.22 us
    pallas_call x1, Pallas kernels, early(): pl.pallas_call(functools.partial(early_kernel, spec, width, 8), out_shape...  1.84 us
  transfers between devices with their start and end apart: 24, of which 9 were waited for; matrix products, arithmetic and copies ran while one was open for 0% of the time, Pallas kernels for 21%

profile of v5, /device:TPU:0, one launch (start us, length us, event | category | flops | bytes accessed | tf_op | source)
XLA Modules:
  0.0 75.7 jit_solution(6056313187022336815)
XLA Ops:
  0.7 0.7 pack.1
  1.4 4.0 %collective-permute-start.2 = (f32[16,128]{1,0:T(8,128)S(1)}, f32[16,128]{1,0:T(8,128)S(1)}, u32[]{:S(2)}, u32[]{:S(2)}) collective-permute-start(f32[16,128]{1,0:T(8,128)S(1)} %pack.1), channel_id=1, source_target_pairs={{0,12},{4,8},{8,4},{12,0},{16,28},{20,24},{24,20},{28,16},{1,13},{... | collective-permute-start | bytes 24584 | tf_op jit(solution)/shard_map/ppermute | solution.py:457
  5.4 0.4 collective-permute-start.1
  5.9 0.2 collective-permute-start
  6.1 1.0 %collective-permute-done.2 = f32[16,128]{1,0:T(8,128)S(1)} collective-permute-done((f32[16,128]{1,0:T(8,128)S(1)}, f32[16,128]{1,0:T(8,128)S(1)}, u32[]{:S(2)}, u32[]{:S(2)}) %collective-permute-start.2) | collective-permute-done | bytes 8224 | tf_op jit(solution)/shard_map/ppermute | solution.py:457
  7.1 2.0 %collective-permute-done.1 = f32[16,128]{1,0:T(8,128)S(1)} collective-permute-done((f32[16,128]{1,0:T(8,128)S(1)}, f32[16,128]{1,0:T(8,128)S(1)}, u32[]{:S(2)}, u32[]{:S(2)}) %collective-permute-start.1) | collective-permute-done | bytes 8224 | tf_op jit(solution)/shard_map/ppermute | solution.py:457
  9.1 0.4 collective-permute-done
  9.5 2.6 %collective-permute-start.3 = (f32[16,128]{1,0:T(8,128)S(1)}, f32[16,128]{1,0:T(8,128)S(1)}, u32[]{:S(2)}, u32[]{:S(2)}) collective-permute-start(f32[16,128]{1,0:T(8,128)S(1)} %add_add_fusion.e0), channel_id=1, source_target_pairs={{0,16},{4,20},{8,24},{12,28},{16,0},{20,4},{24,8},{28,12},{1,17},{... | collective-permute-start | bytes 24584 | tf_op jit(solution)/shard_map/ppermute | solution.py:457
  12.1 1.7 %fetch.3 = (bf16[1,16,36864]{2,1,0:T(8,128)(2,1)S(1)}, bf16[1,16,36864]{2,1,0:T(8,128)(2,1)S(1)}) custom-call(f32[1,48,36864]{2,1,0:T(8,128)} %const.5), custom_call_target="tpu_custom_call" | custom-call | tf_op jit(solution)/shard_map/fetch/pallas_call | solution.py:120
  13.8 1.7 %fetch.5 = (bf16[1,16,36864]{2,1,0:T(8,128)(2,1)S(1)}, bf16[1,16,36864]{2,1,0:T(8,128)(2,1)S(1)}) custom-call(f32[1,48,36864]{2,1,0:T(8,128)} %const.5), custom_call_target="tpu_custom_call" | custom-call | tf_op jit(solution)/shard_map/fetch/pallas_call | solution.py:120
  15.6 1.7 %fetch.4 = (bf16[1,16,36864]{2,1,0:T(8,128)(2,1)S(1)}, bf16[1,16,36864]{2,1,0:T(8,128)(2,1)S(1)}) custom-call(f32[1,48,36864]{2,1,0:T(8,128)} %const.5), custom_call_target="tpu_custom_call" | custom-call | tf_op jit(solution)/shard_map/fetch/pallas_call | solution.py:120
  17.3 0.0 collective-permute-done.3.e1
  17.3 0.9 %contract.2 = (f32[4,1,64,384]{3,2,1,0:T(8,128)S(1)}, f32[4,1,64,384]{3,2,1,0:T(8,128)S(1)}) custom-call(f32[16,128]{1,0:T(8,128)S(1)} %add_add_fusion.e0, f32[16,128]{1,0:T(8,128)S(1)} %collective-permute-done.3.e1, bf16[1,16,36864]{2,1,0:T(8,128)(2,1)S(1)} %get-tuple-element.19.refs_0_, bf16[1,16,36864]{2,1,0:T(8,128)(2,1)S(1)} %get-tuple-element.20.refs_1_, ...), custom_call_target="tpu_custom_call" | custom-call | tf_op jit(solution)/shard_map/contract/pallas_call | solution.py:173
  18.2 0.1 collective-permute-start.4
  19.0 0.6 contract.3
  19.5 0.6 collective-permute-start.12
  20.1 1.6 %collective-permute-start.5 = (f32[2,1,64,384]{3,2,0,1:T(8,128)S(1)}, f32[2,1,64,384]{3,2,0,1:T(8,128)S(1)}, u32[]{:S(2)}, u32[]{:S(2)}) collective-permute-start(f32[2,1,64,384]{3,2,0,1:T(8,128)S(1)} %fusion), channel_id=1, source_target_pairs={{0,2},{1,3},{2,0},{3,1},{4,6},{5,7},{6,4},{7,5},{8,10},{9,11},{10,... | collective-permute-start | bytes 589832 | tf_op jit(solution)/shard_map/ppermute | solution.py:457
  21.7 1.0 %collective-permute-start.13 = (f32[2,1,32,384]{3,2,0,1:T(8,128)S(1)}, f32[2,1,32,384]{3,2,0,1:T(8,128)S(1)}, u32[]{:S(2)}, u32[]{:S(2)}) collective-permute-start(f32[2,1,32,384]{3,2,0,1:T(8,128)S(1)} %fusion.5), channel_id=1, source_target_pairs={{0,2},{1,3},{2,0},{3,1},{4,6},{5,7},{6,4},{7,5},{8,10},{9,11},{10,... | collective-permute-start | bytes 294920 | tf_op jit(solution)/shard_map/ppermute | solution.py:457
  22.8 5.2 %collective-permute-done.5 = f32[2,1,64,384]{3,2,0,1:T(8,128)S(1)} collective-permute-done((f32[2,1,64,384]{3,2,0,1:T(8,128)S(1)}, f32[2,1,64,384]{3,2,0,1:T(8,128)S(1)}, u32[]{:S(2)}, u32[]{:S(2)}) %collective-permute-start.5) | collective-permute-done | bytes 196640 | tf_op jit(solution)/shard_map/ppermute | solution.py:457
  28.0 1.6 %collective-permute-start.6 = (f32[1,2,32,384]{3,2,1,0:T(8,128)S(1)}, f32[1,2,32,384]{3,2,1,0:T(8,128)S(1)}, u32[]{:S(2)}, u32[]{:S(2)}) collective-permute-start(f32[1,2,32,384]{3,2,1,0:T(8,128)S(1)} %get-tuple-element.34), channel_id=1, source_target_pairs={{0,8},{8,0},{16,24},{24,16},{28,20},{20,28},{12,4},{4,12},{1,9},{9... | collective-permute-start | bytes 294920 | tf_op jit(solution)/shard_map/ppermute | solution.py:483
  29.7 0.0 collective-permute-done.13
  29.7 0.6 collective-permute-start.9
  30.3 2.4 %collective-permute-done.6 = f32[1,2,32,384]{3,2,1,0:T(8,128)S(1)} collective-permute-done((f32[1,2,32,384]{3,2,1,0:T(8,128)S(1)}, f32[1,2,32,384]{3,2,1,0:T(8,128)S(1)}, u32[]{:S(2)}, u32[]{:S(2)}) %collective-permute-start.6) | collective-permute-done | bytes 98336 | tf_op jit(solution)/shard_map/ppermute | solution.py:483
  32.7 0.6 collective-permute-start.7
  33.3 2.1 %collective-permute-done.9 = f32[1,2,32,384]{3,2,1,0:T(8,128)S(1)} collective-permute-done((f32[1,2,32,384]{3,2,1,0:T(8,128)S(1)}, f32[1,2,32,384]{3,2,1,0:T(8,128)S(1)}, u32[]{:S(2)}, u32[]{:S(2)}) %collective-permute-start.9) | collective-permute-done | bytes 98336 | tf_op jit(solution)/shard_map/ppermute | solution.py:483
  35.5 1.1 %collective-permute-start.10 = (f32[2,2,32,384]{3,2,1,0:T(8,128)S(1)}, f32[2,2,32,384]{3,2,1,0:T(8,128)S(1)}, u32[]{:S(2)}, u32[]{:S(2)}) collective-permute-start(f32[2,2,32,384]{3,2,1,0:T(8,128)S(1)} %pad_maximum_fusion.1.refs_3_), channel_id=1, source_target_pairs={{0,8},{8,0},{16,24},{24,16},{28,20},{20,28},{12,4},{4,12},{1,9},{9... | collective-permute-start | bytes 589832 | tf_op jit(solution)/shard_map/ppermute | solution.py:483
  36.6 1.0 %collective-permute-start.14 = (f32[1,2,16,384]{3,2,1,0:T(8,128)S(1)}, f32[1,2,16,384]{3,2,1,0:T(8,128)S(1)}, u32[]{:S(2)}, u32[]{:S(2)}) collective-permute-start(f32[1,2,16,384]{3,2,1,0:T(8,128)S(1)} %get-tuple-element.36), channel_id=1, source_target_pairs={{0,8},{8,0},{16,24},{24,16},{28,20},{20,28},{12,4},{4,12},{1,9},{9... | collective-permute-start | bytes 147464 | tf_op jit(solution)/shard_map/ppermute | solution.py:483
  37.6 0.5 collective-permute-start.17
  38.2 4.7 %collective-permute-done.14 = f32[1,2,16,384]{3,2,1,0:T(8,128)S(1)} collective-permute-done((f32[1,2,16,384]{3,2,1,0:T(8,128)S(1)}, f32[1,2,16,384]{3,2,1,0:T(8,128)S(1)}, u32[]{:S(2)}, u32[]{:S(2)}) %collective-permute-start.14) | collective-permute-done | bytes 49184 | tf_op jit(solution)/shard_map/ppermute | solution.py:483
  42.9 0.1 collective-permute-start.15
  43.0 0.8 %collective-permute-start.8 = (f32[2,2,32,384]{3,2,1,0:T(8,128)S(1)}, f32[2,2,32,384]{3,2,1,0:T(8,128)S(1)}, u32[]{:S(2)}, u32[]{:S(2)}) collective-permute-start(f32[2,2,32,384]{3,2,1,0:T(8,128)S(1)} %collective-permute-done.7.refs_1_), channel_id=1, source_target_pairs={{0,8},{8,0},{16,24},{24,16},{28,20},{20,28},{12,4},{4,12},{1,9},{9... | collective-permute-start | bytes 589832 | tf_op jit(solution)/shard_map/ppermute | solution.py:483
  43.7 0.0 collective-permute-done.10.refs_4_
  43.8 1.3 %collective-permute-start.11 = (f32[2,2,32,384]{3,2,1,0:T(8,128)S(1)}, f32[2,2,32,384]{3,2,1,0:T(8,128)S(1)}, u32[]{:S(2)}, u32[]{:S(2)}) collective-permute-start(f32[2,2,32,384]{3,2,1,0:T(8,128)S(1)} %collective-permute-done.10.refs_4_), channel_id=1, source_target_pairs={{8,16},{16,8},{24,28},{28,24},{20,12},{12,20},{4,0},{0,4},{9,17},{... | collective-permute-start | bytes 589832 | tf_op jit(solution)/shard_map/ppermute | solution.py:483
  45.1 0.8 %collective-permute-start.18 = (f32[2,2,16,384]{3,2,1,0:T(8,128)S(1)}, f32[2,2,16,384]{3,2,1,0:T(8,128)S(1)}, u32[]{:S(2)}, u32[]{:S(2)}) collective-permute-start(f32[2,2,16,384]{3,2,1,0:T(8,128)S(1)} %pad_maximum_fusion.3.refs_9_), channel_id=1, source_target_pairs={{0,8},{8,0},{16,24},{24,16},{28,20},{20,28},{12,4},{4,12},{1,9},{9... | collective-permute-start | bytes 294920 | tf_op jit(solution)/shard_map/ppermute | solution.py:483
  45.8 5.0 %collective-permute-done.8.refs_2_ = f32[2,2,32,384]{3,2,1,0:T(8,128)S(1)} collective-permute-done((f32[2,2,32,384]{3,2,1,0:T(8,128)S(1)}, f32[2,2,32,384]{3,2,1,0:T(8,128)S(1)}, u32[]{:S(2)}, u32[]{:S(2)}) %collective-permute-start.8) | collective-permute-done | bytes 196640 | tf_op jit(solution)/shard_map/ppermute | solution.py:483
  50.8 1.9 %collective-permute-start.20 = (f32[2,2,32,384]{3,2,1,0:T(8,128)S(1)}, f32[2,2,32,384]{3,2,1,0:T(8,128)S(1)}, u32[]{:S(2)}, u32[]{:S(2)}) collective-permute-start(f32[2,2,32,384]{3,2,1,0:T(8,128)S(1)} %collective-permute-done.8.refs_2_), channel_id=1, source_target_pairs={{8,16},{16,8},{24,28},{28,24},{20,12},{12,20},{4,0},{0,4},{9,17},{... | collective-permute-start | bytes 589832 | tf_op jit(solution)/shard_map/ppermute | solution.py:483
  52.8 0.7 collective-permute-start.21
  53.5 1.3 %collective-permute-start.16 = (f32[2,2,16,384]{3,2,1,0:T(8,128)S(1)}, f32[2,2,16,384]{3,2,1,0:T(8,128)S(1)}, u32[]{:S(2)}, u32[]{:S(2)}) collective-permute-start(f32[2,2,16,384]{3,2,1,0:T(8,128)S(1)} %collective-permute-done.15.refs_7_), channel_id=1, source_target_pairs={{0,8},{8,0},{16,24},{24,16},{28,20},{20,28},{12,4},{4,12},{1,9},{9... | collective-permute-start | bytes 294920 | tf_op jit(solution)/shard_map/ppermute | solution.py:483
  54.8 0.1 collective-permute-start.19
  54.9 5.5 %collective-permute-done.16.refs_8_ = f32[2,2,16,384]{3,2,1,0:T(8,128)S(1)} collective-permute-done((f32[2,2,16,384]{3,2,1,0:T(8,128)S(1)}, f32[2,2,16,384]{3,2,1,0:T(8,128)S(1)}, u32[]{:S(2)}, u32[]{:S(2)}) %collective-permute-start.16) | collective-permute-done | bytes 98336 | tf_op jit(solution)/shard_map/ppermute | solution.py:483
  60.4 0.2 collective-permute-start.22
  60.6 0.7 collective-permute-start.23
  61.3 3.4 %prep.3 = (bf16[8,3,192,192]{3,2,1,0:T(8,128)(2,1)S(1)}, bf16[8,3,192,192]{3,2,1,0:T(8,128)(2,1)S(1)}) custom-call(f32[8,576,128]{2,1,0:T(8,128)} %bitcast.59), custom_call_target="tpu_custom_call" | custom-call | tf_op jit(solution)/shard_map/prep/pallas_call | solution.py:240
  64.8 2.6 %prep.2 = (bf16[8,3,192,192]{3,2,1,0:T(8,128)(2,1)S(1)}, bf16[8,3,192,192]{3,2,1,0:T(8,128)(2,1)S(1)}) custom-call(f32[8,576,128]{2,1,0:T(8,128)} %bitcast.60), custom_call_target="tpu_custom_call" | custom-call | tf_op jit(solution)/shard_map/prep/pallas_call | solution.py:240
  67.4 0.4 angles.1.refs_12_.refs_2_
  67.9 1.8 %early.1.partial = f32[8,2,96,384]{3,2,1,0:T(8,128)S(1)} custom-call(f32[2,2,32,384]{3,2,1,0:T(8,128)S(1)} %pad_maximum_fusion.refs_0_, f32[2,2,32,384]{3,2,1,0:T(8,128)S(1)} %collective-permute-done.7.refs_1_, f32[2,2,32,384]{3,2,1,0:T(8,128)S(1)} %collective-permute-done.8.refs_2_, f32[2,2,32,384]{3,2,1,0:T(8,128)S(1)} %pad_maximum_fusion.1.refs_3_, ...), custom_call_target="tpu_custom_call" | custom-call | tf_op jit(solution)/shard_map/early/pallas_call | solution.py:337
  69.7 1.7 %inner.1.done = f32[8,2,128,192]{3,2,1,0:T(8,128)S(1)} custom-call(f32[8,2,96,384]{3,2,1,0:T(8,128)S(1)} %early.1.partial, f32[2,2,32,384]{3,2,1,0:T(8,128)S(1)} %collective-permute-done.20.refs_0_, f32[2,2,32,384]{3,2,1,0:T(8,128)S(1)} %collective-permute-done.21.refs_1_, f32[2,256,128]{2,1,0:T(8,128)S(1)} %angles.1.refs_12_.refs_2_, ...), custom_call_target="tpu_custom_call" | custom-call | tf_op jit(solution)/shard_map/inner/pallas_call | solution.py:394
  71.5 4.2 %final.1 = f32[8,288,128]{2,1,0:T(8,128)} custom-call(f32[8,2,128,192]{3,2,1,0:T(8,128)S(1)} %inner.1.done, f32[8,2,96,384]{3,2,1,0:T(8,128)S(1)} %early.1.partial, f32[2,2,16,384]{3,2,1,0:T(8,128)S(1)} %collective-permute-done.22.refs_0_, f32[2,2,16,384]{3,2,1,0:T(8,128)S(1)} %collective-permute-done.23.refs_1_, f32[2,256,128]{2,1,0:T(8,128)S(1)} %angles.1.refs_12_.refs_2_, ...), custom_call_target="tpu_custom_call" | custom-call | tf_op jit(solution)/shard_map/final/pallas_call | solution.py:443
  (25 shorter events, 0.2 us)
Async XLA Ops:
  1.4 5.7 %collective-permute-start.2 = (f32[16,128]{1,0:T(8,128)S(1)}, f32[16,128]{1,0:T(8,128)S(1)}, u32[]{:S(2)}, u32[]{:S(2)}) collective-permute-start(f32[16,128]{1,0:T(8,128)S(1)} %pack.1), channel_id=1, source_target_pairs={{0,12},{4,8},{8,4},{12,0},{16,28},{20,24},{24,20},{28,16},{1,13},{... | collective-permute-start | bytes 24584 | tf_op jit(solution)/shard_map/ppermute | solution.py:457
  5.4 3.7 %collective-permute-start.1 = (f32[16,128]{1,0:T(8,128)S(1)}, f32[16,128]{1,0:T(8,128)S(1)}, u32[]{:S(2)}, u32[]{:S(2)}) collective-permute-start(f32[16,128]{1,0:T(8,128)S(1)} %pack.1), channel_id=1, source_target_pairs={{0,8},{4,12},{8,0},{12,4},{16,24},{20,28},{24,16},{28,20},{1,9},{5... | collective-permute-start | bytes 24584 | tf_op jit(solution)/shard_map/ppermute | solution.py:457
  5.9 3.7 %collective-permute-start = (f32[16,128]{1,0:T(8,128)S(1)}, f32[16,128]{1,0:T(8,128)S(1)}, u32[]{:S(2)}, u32[]{:S(2)}) collective-permute-start(f32[16,128]{1,0:T(8,128)S(1)} %pack.1), channel_id=1, source_target_pairs={{0,4},{4,0},{8,12},{12,8},{16,20},{20,16},{24,28},{28,24},{1,5},{5... | collective-permute-start | bytes 24584 | tf_op jit(solution)/shard_map/ppermute | solution.py:457
  9.5 7.8 %collective-permute-start.3 = (f32[16,128]{1,0:T(8,128)S(1)}, f32[16,128]{1,0:T(8,128)S(1)}, u32[]{:S(2)}, u32[]{:S(2)}) collective-permute-start(f32[16,128]{1,0:T(8,128)S(1)} %add_add_fusion.e0), channel_id=1, source_target_pairs={{0,16},{4,20},{8,24},{12,28},{16,0},{20,4},{24,8},{28,12},{1,17},{... | collective-permute-start | bytes 24584 | tf_op jit(solution)/shard_map/ppermute | solution.py:457
  18.2 1.9 %collective-permute-start.4 = (f32[2,2,1,64,384]{4,3,1,2,0:T(8,128)S(1)}, f32[2,2,1,64,384]{4,3,1,2,0:T(8,128)S(1)}, u32[]{:S(2)}, u32[]{:S(2)}) collective-permute-start(f32[2,2,1,64,384]{4,3,1,2,0:T(8,128)S(1)} %bitcast.57), channel_id=1, source_target_pairs={{0,1},{1,0},{2,3},{3,2},{4,5},{5,4},{6,7},{7,6},{8,9},{9,8},{10,11... | collective-permute-start | bytes 1179656 | tf_op jit(solution)/shard_map/ppermute | solution.py:457
  19.5 2.2 %collective-permute-start.12 = (f32[2,2,1,32,384]{4,3,1,2,0:T(8,128)S(1)}, f32[2,2,1,32,384]{4,3,1,2,0:T(8,128)S(1)}, u32[]{:S(2)}, u32[]{:S(2)}) collective-permute-start(f32[2,2,1,32,384]{4,3,1,2,0:T(8,128)S(1)} %bitcast.58), channel_id=1, source_target_pairs={{0,1},{1,0},{2,3},{3,2},{4,5},{5,4},{6,7},{7,6},{8,9},{9,8},{10,11... | collective-permute-start | bytes 589832 | tf_op jit(solution)/shard_map/ppermute | solution.py:457
  20.1 7.8 %collective-permute-start.5 = (f32[2,1,64,384]{3,2,0,1:T(8,128)S(1)}, f32[2,1,64,384]{3,2,0,1:T(8,128)S(1)}, u32[]{:S(2)}, u32[]{:S(2)}) collective-permute-start(f32[2,1,64,384]{3,2,0,1:T(8,128)S(1)} %fusion), channel_id=1, source_target_pairs={{0,2},{1,3},{2,0},{3,1},{4,6},{5,7},{6,4},{7,5},{8,10},{9,11},{10,... | collective-permute-start | bytes 589832 | tf_op jit(solution)/shard_map/ppermute | solution.py:457
  21.7 7.9 %collective-permute-start.13 = (f32[2,1,32,384]{3,2,0,1:T(8,128)S(1)}, f32[2,1,32,384]{3,2,0,1:T(8,128)S(1)}, u32[]{:S(2)}, u32[]{:S(2)}) collective-permute-start(f32[2,1,32,384]{3,2,0,1:T(8,128)S(1)} %fusion.5), channel_id=1, source_target_pairs={{0,2},{1,3},{2,0},{3,1},{4,6},{5,7},{6,4},{7,5},{8,10},{9,11},{10,... | collective-permute-start | bytes 294920 | tf_op jit(solution)/shard_map/ppermute | solution.py:457
  28.0 4.7 %collective-permute-start.6 = (f32[1,2,32,384]{3,2,1,0:T(8,128)S(1)}, f32[1,2,32,384]{3,2,1,0:T(8,128)S(1)}, u32[]{:S(2)}, u32[]{:S(2)}) collective-permute-start(f32[1,2,32,384]{3,2,1,0:T(8,128)S(1)} %get-tuple-element.34), channel_id=1, source_target_pairs={{0,8},{8,0},{16,24},{24,16},{28,20},{20,28},{12,4},{4,12},{1,9},{9... | collective-permute-start | bytes 294920 | tf_op jit(solution)/shard_map/ppermute | solution.py:483
  29.7 5.7 %collective-permute-start.9 = (f32[1,2,32,384]{3,2,1,0:T(8,128)S(1)}, f32[1,2,32,384]{3,2,1,0:T(8,128)S(1)}, u32[]{:S(2)}, u32[]{:S(2)}) collective-permute-start(f32[1,2,32,384]{3,2,1,0:T(8,128)S(1)} %get-tuple-element.33), channel_id=1, source_target_pairs={{8,16},{16,8},{24,28},{28,24},{20,12},{12,20},{4,0},{0,4},{9,17},{... | collective-permute-start | bytes 294920 | tf_op jit(solution)/shard_map/ppermute | solution.py:483
  32.7 10.2 %collective-permute-start.7 = (f32[2,2,32,384]{3,2,1,0:T(8,128)S(1)}, f32[2,2,32,384]{3,2,1,0:T(8,128)S(1)}, u32[]{:S(2)}, u32[]{:S(2)}) collective-permute-start(f32[2,2,32,384]{3,2,1,0:T(8,128)S(1)} %pad_maximum_fusion.refs_0_), channel_id=1, source_target_pairs={{8,16},{16,8},{24,28},{28,24},{20,12},{12,20},{4,0},{0,4},{9,17},{... | collective-permute-start | bytes 589832 | tf_op jit(solution)/shard_map/ppermute | solution.py:483
  35.5 8.3 %collective-permute-start.10 = (f32[2,2,32,384]{3,2,1,0:T(8,128)S(1)}, f32[2,2,32,384]{3,2,1,0:T(8,128)S(1)}, u32[]{:S(2)}, u32[]{:S(2)}) collective-permute-start(f32[2,2,32,384]{3,2,1,0:T(8,128)S(1)} %pad_maximum_fusion.1.refs_3_), channel_id=1, source_target_pairs={{0,8},{8,0},{16,24},{24,16},{28,20},{20,28},{12,4},{4,12},{1,9},{9... | collective-permute-start | bytes 589832 | tf_op jit(solution)/shard_map/ppermute | solution.py:483
  36.6 6.3 %collective-permute-start.14 = (f32[1,2,16,384]{3,2,1,0:T(8,128)S(1)}, f32[1,2,16,384]{3,2,1,0:T(8,128)S(1)}, u32[]{:S(2)}, u32[]{:S(2)}) collective-permute-start(f32[1,2,16,384]{3,2,1,0:T(8,128)S(1)} %get-tuple-element.36), channel_id=1, source_target_pairs={{0,8},{8,0},{16,24},{24,16},{28,20},{20,28},{12,4},{4,12},{1,9},{9... | collective-permute-start | bytes 147464 | tf_op jit(solution)/shard_map/ppermute | solution.py:483
  37.6 7.5 %collective-permute-start.17 = (f32[1,2,16,384]{3,2,1,0:T(8,128)S(1)}, f32[1,2,16,384]{3,2,1,0:T(8,128)S(1)}, u32[]{:S(2)}, u32[]{:S(2)}) collective-permute-start(f32[1,2,16,384]{3,2,1,0:T(8,128)S(1)} %get-tuple-element.35), channel_id=1, source_target_pairs={{8,16},{16,8},{24,28},{28,24},{20,12},{12,20},{4,0},{0,4},{9,17},{... | collective-permute-start | bytes 147464 | tf_op jit(solution)/shard_map/ppermute | solution.py:483
  42.9 10.6 %collective-permute-start.15 = (f32[2,2,16,384]{3,2,1,0:T(8,128)S(1)}, f32[2,2,16,384]{3,2,1,0:T(8,128)S(1)}, u32[]{:S(2)}, u32[]{:S(2)}) collective-permute-start(f32[2,2,16,384]{3,2,1,0:T(8,128)S(1)} %pad_maximum_fusion.2.refs_6_), channel_id=1, source_target_pairs={{8,16},{16,8},{24,28},{28,24},{20,12},{12,20},{4,0},{0,4},{9,17},{... | collective-permute-start | bytes 294920 | tf_op jit(solution)/shard_map/ppermute | solution.py:483
  43.0 7.8 %collective-permute-start.8 = (f32[2,2,32,384]{3,2,1,0:T(8,128)S(1)}, f32[2,2,32,384]{3,2,1,0:T(8,128)S(1)}, u32[]{:S(2)}, u32[]{:S(2)}) collective-permute-start(f32[2,2,32,384]{3,2,1,0:T(8,128)S(1)} %collective-permute-done.7.refs_1_), channel_id=1, source_target_pairs={{0,8},{8,0},{16,24},{24,16},{28,20},{20,28},{12,4},{4,12},{1,9},{9... | collective-permute-start | bytes 589832 | tf_op jit(solution)/shard_map/ppermute | solution.py:483
  43.8 9.0 %collective-permute-start.11 = (f32[2,2,32,384]{3,2,1,0:T(8,128)S(1)}, f32[2,2,32,384]{3,2,1,0:T(8,128)S(1)}, u32[]{:S(2)}, u32[]{:S(2)}) collective-permute-start(f32[2,2,32,384]{3,2,1,0:T(8,128)S(1)} %collective-permute-done.10.refs_4_), channel_id=1, source_target_pairs={{8,16},{16,8},{24,28},{28,24},{20,12},{12,20},{4,0},{0,4},{9,17},{... | collective-permute-start | bytes 589832 | tf_op jit(solution)/shard_map/ppermute | solution.py:483
  45.1 9.7 %collective-permute-start.18 = (f32[2,2,16,384]{3,2,1,0:T(8,128)S(1)}, f32[2,2,16,384]{3,2,1,0:T(8,128)S(1)}, u32[]{:S(2)}, u32[]{:S(2)}) collective-permute-start(f32[2,2,16,384]{3,2,1,0:T(8,128)S(1)} %pad_maximum_fusion.3.refs_9_), channel_id=1, source_target_pairs={{0,8},{8,0},{16,24},{24,16},{28,20},{20,28},{12,4},{4,12},{1,9},{9... | collective-permute-start | bytes 294920 | tf_op jit(solution)/shard_map/ppermute | solution.py:483
  50.8 18.9 %collective-permute-start.20 = (f32[2,2,32,384]{3,2,1,0:T(8,128)S(1)}, f32[2,2,32,384]{3,2,1,0:T(8,128)S(1)}, u32[]{:S(2)}, u32[]{:S(2)}) collective-permute-start(f32[2,2,32,384]{3,2,1,0:T(8,128)S(1)} %collective-permute-done.8.refs_2_), channel_id=1, source_target_pairs={{8,16},{16,8},{24,28},{28,24},{20,12},{12,20},{4,0},{0,4},{9,17},{... | collective-permute-start | bytes 589832 | tf_op jit(solution)/shard_map/ppermute | solution.py:483
  52.8 16.9 %collective-permute-start.21 = (f32[2,2,32,384]{3,2,1,0:T(8,128)S(1)}, f32[2,2,32,384]{3,2,1,0:T(8,128)S(1)}, u32[]{:S(2)}, u32[]{:S(2)}) collective-permute-start(f32[2,2,32,384]{3,2,1,0:T(8,128)S(1)} %collective-permute-done.11.refs_5_), channel_id=1, source_target_pairs={{0,8},{8,0},{16,24},{24,16},{28,20},{20,28},{12,4},{4,12},{1,9},{9... | collective-permute-start | bytes 589832 | tf_op jit(solution)/shard_map/ppermute | solution.py:483
  53.5 6.9 %collective-permute-start.16 = (f32[2,2,16,384]{3,2,1,0:T(8,128)S(1)}, f32[2,2,16,384]{3,2,1,0:T(8,128)S(1)}, u32[]{:S(2)}, u32[]{:S(2)}) collective-permute-start(f32[2,2,16,384]{3,2,1,0:T(8,128)S(1)} %collective-permute-done.15.refs_7_), channel_id=1, source_target_pairs={{0,8},{8,0},{16,24},{24,16},{28,20},{20,28},{12,4},{4,12},{1,9},{9... | collective-permute-start | bytes 294920 | tf_op jit(solution)/shard_map/ppermute | solution.py:483
  54.8 5.8 %collective-permute-start.19 = (f32[2,2,16,384]{3,2,1,0:T(8,128)S(1)}, f32[2,2,16,384]{3,2,1,0:T(8,128)S(1)}, u32[]{:S(2)}, u32[]{:S(2)}) collective-permute-start(f32[2,2,16,384]{3,2,1,0:T(8,128)S(1)} %collective-permute-done.18.refs_10_), channel_id=1, source_target_pairs={{8,16},{16,8},{24,28},{28,24},{20,12},{12,20},{4,0},{0,4},{9,17},{... | collective-permute-start | bytes 294920 | tf_op jit(solution)/shard_map/ppermute | solution.py:483
  60.4 11.1 %collective-permute-start.22 = (f32[2,2,16,384]{3,2,1,0:T(8,128)S(1)}, f32[2,2,16,384]{3,2,1,0:T(8,128)S(1)}, u32[]{:S(2)}, u32[]{:S(2)}) collective-permute-start(f32[2,2,16,384]{3,2,1,0:T(8,128)S(1)} %collective-permute-done.16.refs_8_), channel_id=1, source_target_pairs={{8,16},{16,8},{24,28},{28,24},{20,12},{12,20},{4,0},{0,4},{9,17},{... | collective-permute-start | bytes 294920 | tf_op jit(solution)/shard_map/ppermute | solution.py:483
  60.6 10.8 %collective-permute-start.23 = (f32[2,2,16,384]{3,2,1,0:T(8,128)S(1)}, f32[2,2,16,384]{3,2,1,0:T(8,128)S(1)}, u32[]{:S(2)}, u32[]{:S(2)}) collective-permute-start(f32[2,2,16,384]{3,2,1,0:T(8,128)S(1)} %collective-permute-done.19.refs_11_), channel_id=1, source_target_pairs={{0,8},{8,0},{16,24},{24,16},{28,20},{20,28},{12,4},{4,12},{1,9},{9... | collective-permute-start | bytes 294920 | tf_op jit(solution)/shard_map/ppermute | solution.py:483
  61.3 6.1 %copy-start = (s32[8,3]{0,1:T(4,128)S(1)}, s32[8,3]{0,1:T(4,128)}, u32[]{:S(2)}) copy-start(s32[8,3]{0,1:T(4,128)} %param.15) | copy-start | bytes 292

commit v6 on v5

--- a/solution.py
+++ b/solution.py
@@ -10,6 +10,7 @@
 from jax.sharding import PartitionSpec as P
 
 G = 32
+UNROLL = 8
 FIRST = 1
 FULL_TURN = 2.0 * math.pi
 LANES = 128
@@ -390,7 +391,9 @@
 
 def inner(span, partial, blocks, spec, cs, weights):
     count, _, size, _ = weights[0].shape
-    unroll = 4 if count % 4 == 0 else 1
+    unroll = UNROLL
+    while count % unroll:
+        unroll //= 2
     return pl.pallas_call(
         functools.partial(inner_kernel, span, cs.shape[1] // count, spec, size, unroll),
         out_shape=kept((count, 2, 2 * span[1], size)),
@@ -405,7 +408,7 @@
 
 def final_kernel(span, width, spec, scale, size, unroll, done, partial, *refs):
     blocks = refs[: len(spec)]
-    cs, gh, gl, wh, wl, out, ph, plo = refs[len(spec) :]
+    cs, gh, gl, wh, wl, raw, ph, plo, out, sem = refs[len(spec) :]
     half = size // 2
     first = pl.program_id(0) * unroll
 
@@ -430,24 +433,34 @@
 
     for u in range(unroll):
         load(span, width, spec, first + u, u, partial, blocks, cs, ph, plo)
-    sums = [product(size, first + u, u, ph, plo, wh, wl) for u in range(unroll)]
+    sums = [product(size, first + u, u, ph, plo, wh, wl) for u in range(2)]
+    copies = []
     for u in range(unroll):
+        if u + 2 < unroll:
+            sums.append(product(size, first + u + 2, u + 2, ph, plo, wh, wl))
         store(u, outer(u, sums[u]))
+        copies.append(pltpu.make_async_copy(out.at[u], raw.at[first + u], sem.at[u]))
+        copies[-1].start()
+    for c in copies:
+        c.wait()
 
 
 def final(span, done, partial, blocks, spec, cs, lefts, weights, total):
     count, _, size, _ = weights[0].shape
     tiles = size * size // LANES
-    unroll = 4 if count % 4 == 0 else 1
+    unroll = UNROLL
+    while count % unroll:
+        unroll //= 2
     width = cs.shape[1] // count
     result = pl.pallas_call(
         functools.partial(final_kernel, span, width, spec, 1.0 / total, size, unroll),
         out_shape=jax.ShapeDtypeStruct((count, tiles, LANES), F32),
         grid=(count // unroll,),
         in_specs=[WHOLE] * (7 + len(blocks)),
-        out_specs=pl.BlockSpec((unroll, tiles, LANES), lambda k: (k, 0, 0)),
-        scratch_shapes=halves(unroll, span),
-        compiler_params=limit(20),
+        out_specs=RAW,
+        scratch_shapes=halves(unroll, span)
+        + [VMEM((unroll, tiles, LANES), F32), pltpu.SemaphoreType.DMA((unroll,))],
+        compiler_params=limit(24),
         name="final",
     )(*in_vmem(done, partial, *blocks, cs, *lefts, *weights))
     return result.reshape(count, 1, size * size)

time: 76 us -> 75.6 us (level)
  no operation moved by 1% of the time
where the time goes in v6:
time: 75.6 us; the launch traced here: 75.3 us
  waiting for transfers between devices  28.4 us (38%)
  starting transfers between devices  23.9 us (32%)
  Pallas kernels  21.1 us (28%)
  between operations  1.66 us (2%)
    ppermute x16, waiting for transfers between devices, neighbour_gather(): arrived.append(lax.ppermute(moving[h], 'row', perm))  19.8 us
    ppermute x16, starting transfers between devices, neighbour_gather(): arrived.append(lax.ppermute(moving[h], 'row', perm))  13.4 us
    ppermute x8, starting transfers between devices, swap(): return lax.ppermute(x, axis, [(i, i ^ bit) for i in range(n)])  10.5 us
    ppermute x8, waiting for transfers between devices, swap(): return lax.ppermute(x, axis, [(i, i ^ bit) for i in range(n)])  8.67 us
    pallas_call x2, Pallas kernels, prep(): pl.pallas_call(functools.partial(prep_kernel, size, turn, spans), out_sha...  6.09 us
    pallas_call x3, Pallas kernels, fetch(): pl.pallas_call(functools.partial(fetch_kernel, slots, first, rows, parts)...  5.14 us
    pallas_call x1, Pallas kernels, final(): pl.pallas_call(functools.partial(final_kernel, span, width, spec, 1.0 / t...  3.7 us
    pallas_call x1, Pallas kernels, early(): pl.pallas_call(functools.partial(early_kernel, spec, width, 8), out_shape...  2.06 us
  transfers between devices with their start and end apart: 24, of which 9 were waited for; matrix products, arithmetic and copies ran while one was open for 0% of the time, Pallas kernels for 21%

profile of v6, /device:TPU:0, one launch (start us, length us, event | category | flops | bytes accessed | tf_op | source)
XLA Modules:
  0.0 75.3 jit_solution(1625062465589687250)
XLA Ops:
  0.7 0.7 pack.1
  1.4 4.0 %collective-permute-start.2 = (f32[16,128]{1,0:T(8,128)S(1)}, f32[16,128]{1,0:T(8,128)S(1)}, u32[]{:S(2)}, u32[]{:S(2)}) collective-permute-start(f32[16,128]{1,0:T(8,128)S(1)} %pack.1), channel_id=1, source_target_pairs={{0,12},{4,8},{8,4},{12,0},{16,28},{20,24},{24,20},{28,16},{1,13},{... | collective-permute-start | bytes 24584 | tf_op jit(solution)/shard_map/ppermute | solution.py:470
  5.4 0.4 collective-permute-start.1
  5.9 0.2 collective-permute-start
  6.1 1.0 %collective-permute-done.2 = f32[16,128]{1,0:T(8,128)S(1)} collective-permute-done((f32[16,128]{1,0:T(8,128)S(1)}, f32[16,128]{1,0:T(8,128)S(1)}, u32[]{:S(2)}, u32[]{:S(2)}) %collective-permute-start.2) | collective-permute-done | bytes 8224 | tf_op jit(solution)/shard_map/ppermute | solution.py:470
  7.1 2.0 %collective-permute-done.1 = f32[16,128]{1,0:T(8,128)S(1)} collective-permute-done((f32[16,128]{1,0:T(8,128)S(1)}, f32[16,128]{1,0:T(8,128)S(1)}, u32[]{:S(2)}, u32[]{:S(2)}) %collective-permute-start.1) | collective-permute-done | bytes 8224 | tf_op jit(solution)/shard_map/ppermute | solution.py:470
  9.1 0.4 collective-permute-done
  9.5 2.6 %collective-permute-start.3 = (f32[16,128]{1,0:T(8,128)S(1)}, f32[16,128]{1,0:T(8,128)S(1)}, u32[]{:S(2)}, u32[]{:S(2)}) collective-permute-start(f32[16,128]{1,0:T(8,128)S(1)} %add_add_fusion.e0), channel_id=1, source_target_pairs={{0,16},{4,20},{8,24},{12,28},{16,0},{20,4},{24,8},{28,12},{1,17},{... | collective-permute-start | bytes 24584 | tf_op jit(solution)/shard_map/ppermute | solution.py:470
  12.1 1.7 %fetch.3 = (bf16[1,16,36864]{2,1,0:T(8,128)(2,1)S(1)}, bf16[1,16,36864]{2,1,0:T(8,128)(2,1)S(1)}) custom-call(f32[1,48,36864]{2,1,0:T(8,128)} %const.5), custom_call_target="tpu_custom_call" | custom-call | tf_op jit(solution)/shard_map/fetch/pallas_call | solution.py:121
  13.8 1.7 %fetch.5 = (bf16[1,16,36864]{2,1,0:T(8,128)(2,1)S(1)}, bf16[1,16,36864]{2,1,0:T(8,128)(2,1)S(1)}) custom-call(f32[1,48,36864]{2,1,0:T(8,128)} %const.5), custom_call_target="tpu_custom_call" | custom-call | tf_op jit(solution)/shard_map/fetch/pallas_call | solution.py:121
  15.6 1.7 %fetch.4 = (bf16[1,16,36864]{2,1,0:T(8,128)(2,1)S(1)}, bf16[1,16,36864]{2,1,0:T(8,128)(2,1)S(1)}) custom-call(f32[1,48,36864]{2,1,0:T(8,128)} %const.5), custom_call_target="tpu_custom_call" | custom-call | tf_op jit(solution)/shard_map/fetch/pallas_call | solution.py:121
  17.3 0.0 collective-permute-done.3.e1
  17.3 0.9 %contract.2 = (f32[4,1,64,384]{3,2,1,0:T(8,128)S(1)}, f32[4,1,64,384]{3,2,1,0:T(8,128)S(1)}) custom-call(f32[16,128]{1,0:T(8,128)S(1)} %add_add_fusion.e0, f32[16,128]{1,0:T(8,128)S(1)} %collective-permute-done.3.e1, bf16[1,16,36864]{2,1,0:T(8,128)(2,1)S(1)} %get-tuple-element.19.refs_0_, bf16[1,16,36864]{2,1,0:T(8,128)(2,1)S(1)} %get-tuple-element.20.refs_1_, ...), custom_call_target="tpu_custom_call" | custom-call | tf_op jit(solution)/shard_map/contract/pallas_call | solution.py:174
  18.2 0.1 collective-permute-start.4
  19.0 0.6 contract.3
  19.5 0.6 collective-permute-start.12
  20.1 0.0 collective-permute-done.4
  20.1 1.6 %collective-permute-start.5 = (f32[2,1,64,384]{3,2,0,1:T(8,128)S(1)}, f32[2,1,64,384]{3,2,0,1:T(8,128)S(1)}, u32[]{:S(2)}, u32[]{:S(2)}) collective-permute-start(f32[2,1,64,384]{3,2,0,1:T(8,128)S(1)} %fusion), channel_id=1, source_target_pairs={{0,2},{1,3},{2,0},{3,1},{4,6},{5,7},{6,4},{7,5},{8,10},{9,11},{10,... | collective-permute-start | bytes 589832 | tf_op jit(solution)/shard_map/ppermute | solution.py:470
  21.7 0.0 collective-permute-done.12
  21.7 1.0 %collective-permute-start.13 = (f32[2,1,32,384]{3,2,0,1:T(8,128)S(1)}, f32[2,1,32,384]{3,2,0,1:T(8,128)S(1)}, u32[]{:S(2)}, u32[]{:S(2)}) collective-permute-start(f32[2,1,32,384]{3,2,0,1:T(8,128)S(1)} %fusion.5), channel_id=1, source_target_pairs={{0,2},{1,3},{2,0},{3,1},{4,6},{5,7},{6,4},{7,5},{8,10},{9,11},{10,... | collective-permute-start | bytes 294920 | tf_op jit(solution)/shard_map/ppermute | solution.py:470
  22.8 5.2 %collective-permute-done.5 = f32[2,1,64,384]{3,2,0,1:T(8,128)S(1)} collective-permute-done((f32[2,1,64,384]{3,2,0,1:T(8,128)S(1)}, f32[2,1,64,384]{3,2,0,1:T(8,128)S(1)}, u32[]{:S(2)}, u32[]{:S(2)}) %collective-permute-start.5) | collective-permute-done | bytes 196640 | tf_op jit(solution)/shard_map/ppermute | solution.py:470
  28.0 1.6 %collective-permute-start.6 = (f32[1,2,32,384]{3,2,1,0:T(8,128)S(1)}, f32[1,2,32,384]{3,2,1,0:T(8,128)S(1)}, u32[]{:S(2)}, u32[]{:S(2)}) collective-permute-start(f32[1,2,32,384]{3,2,1,0:T(8,128)S(1)} %get-tuple-element.34), channel_id=1, source_target_pairs={{0,8},{8,0},{16,24},{24,16},{28,20},{20,28},{12,4},{4,12},{1,9},{9... | collective-permute-start | bytes 294920 | tf_op jit(solution)/shard_map/ppermute | solution.py:496
  29.7 0.6 collective-permute-start.9
  30.3 2.4 %collective-permute-done.6 = f32[1,2,32,384]{3,2,1,0:T(8,128)S(1)} collective-permute-done((f32[1,2,32,384]{3,2,1,0:T(8,128)S(1)}, f32[1,2,32,384]{3,2,1,0:T(8,128)S(1)}, u32[]{:S(2)}, u32[]{:S(2)}) %collective-permute-start.6) | collective-permute-done | bytes 98336 | tf_op jit(solution)/shard_map/ppermute | solution.py:496
  32.7 0.6 collective-permute-start.7
  33.3 2.1 %collective-permute-done.9 = f32[1,2,32,384]{3,2,1,0:T(8,128)S(1)} collective-permute-done((f32[1,2,32,384]{3,2,1,0:T(8,128)S(1)}, f32[1,2,32,384]{3,2,1,0:T(8,128)S(1)}, u32[]{:S(2)}, u32[]{:S(2)}) %collective-permute-start.9) | collective-permute-done | bytes 98336 | tf_op jit(solution)/shard_map/ppermute | solution.py:496
  35.5 1.1 %collective-permute-start.10 = (f32[2,2,32,384]{3,2,1,0:T(8,128)S(1)}, f32[2,2,32,384]{3,2,1,0:T(8,128)S(1)}, u32[]{:S(2)}, u32[]{:S(2)}) collective-permute-start(f32[2,2,32,384]{3,2,1,0:T(8,128)S(1)} %pad_maximum_fusion.1.refs_3_), channel_id=1, source_target_pairs={{0,8},{8,0},{16,24},{24,16},{28,20},{20,28},{12,4},{4,12},{1,9},{9... | collective-permute-start | bytes 589832 | tf_op jit(solution)/shard_map/ppermute | solution.py:496
  36.6 1.0 %collective-permute-start.14 = (f32[1,2,16,384]{3,2,1,0:T(8,128)S(1)}, f32[1,2,16,384]{3,2,1,0:T(8,128)S(1)}, u32[]{:S(2)}, u32[]{:S(2)}) collective-permute-start(f32[1,2,16,384]{3,2,1,0:T(8,128)S(1)} %get-tuple-element.36), channel_id=1, source_target_pairs={{0,8},{8,0},{16,24},{24,16},{28,20},{20,28},{12,4},{4,12},{1,9},{9... | collective-permute-start | bytes 147464 | tf_op jit(solution)/shard_map/ppermute | solution.py:496
  37.6 0.5 collective-permute-start.17
  38.1 4.7 %collective-permute-done.14 = f32[1,2,16,384]{3,2,1,0:T(8,128)S(1)} collective-permute-done((f32[1,2,16,384]{3,2,1,0:T(8,128)S(1)}, f32[1,2,16,384]{3,2,1,0:T(8,128)S(1)}, u32[]{:S(2)}, u32[]{:S(2)}) %collective-permute-start.14) | collective-permute-done | bytes 49184 | tf_op jit(solution)/shard_map/ppermute | solution.py:496
  42.9 0.1 collective-permute-start.15
  43.0 0.8 %collective-permute-start.8 = (f32[2,2,32,384]{3,2,1,0:T(8,128)S(1)}, f32[2,2,32,384]{3,2,1,0:T(8,128)S(1)}, u32[]{:S(2)}, u32[]{:S(2)}) collective-permute-start(f32[2,2,32,384]{3,2,1,0:T(8,128)S(1)} %collective-permute-done.7.refs_1_), channel_id=1, source_target_pairs={{0,8},{8,0},{16,24},{24,16},{28,20},{20,28},{12,4},{4,12},{1,9},{9... | collective-permute-start | bytes 589832 | tf_op jit(solution)/shard_map/ppermute | solution.py:496
  43.7 1.3 %collective-permute-start.11 = (f32[2,2,32,384]{3,2,1,0:T(8,128)S(1)}, f32[2,2,32,384]{3,2,1,0:T(8,128)S(1)}, u32[]{:S(2)}, u32[]{:S(2)}) collective-permute-start(f32[2,2,32,384]{3,2,1,0:T(8,128)S(1)} %collective-permute-done.10.refs_4_), channel_id=1, source_target_pairs={{8,16},{16,8},{24,28},{28,24},{20,12},{12,20},{4,0},{0,4},{9,17},{... | collective-permute-start | bytes 589832 | tf_op jit(solution)/shard_map/ppermute | solution.py:496
  45.1 0.8 %collective-permute-start.18 = (f32[2,2,16,384]{3,2,1,0:T(8,128)S(1)}, f32[2,2,16,384]{3,2,1,0:T(8,128)S(1)}, u32[]{:S(2)}, u32[]{:S(2)}) collective-permute-start(f32[2,2,16,384]{3,2,1,0:T(8,128)S(1)} %pad_maximum_fusion.3.refs_9_), channel_id=1, source_target_pairs={{0,8},{8,0},{16,24},{24,16},{28,20},{20,28},{12,4},{4,12},{1,9},{9... | collective-permute-start | bytes 294920 | tf_op jit(solution)/shard_map/ppermute | solution.py:496
  45.8 5.0 %collective-permute-done.8.refs_2_ = f32[2,2,32,384]{3,2,1,0:T(8,128)S(1)} collective-permute-done((f32[2,2,32,384]{3,2,1,0:T(8,128)S(1)}, f32[2,2,32,384]{3,2,1,0:T(8,128)S(1)}, u32[]{:S(2)}, u32[]{:S(2)}) %collective-permute-start.8) | collective-permute-done | bytes 196640 | tf_op jit(solution)/shard_map/ppermute | solution.py:496
  50.8 1.9 %collective-permute-start.20 = (f32[2,2,32,384]{3,2,1,0:T(8,128)S(1)}, f32[2,2,32,384]{3,2,1,0:T(8,128)S(1)}, u32[]{:S(2)}, u32[]{:S(2)}) collective-permute-start(f32[2,2,32,384]{3,2,1,0:T(8,128)S(1)} %collective-permute-done.8.refs_2_), channel_id=1, source_target_pairs={{8,16},{16,8},{24,28},{28,24},{20,12},{12,20},{4,0},{0,4},{9,17},{... | collective-permute-start | bytes 589832 | tf_op jit(solution)/shard_map/ppermute | solution.py:496
  52.8 0.7 collective-permute-start.21
  53.5 1.3 %collective-permute-start.16 = (f32[2,2,16,384]{3,2,1,0:T(8,128)S(1)}, f32[2,2,16,384]{3,2,1,0:T(8,128)S(1)}, u32[]{:S(2)}, u32[]{:S(2)}) collective-permute-start(f32[2,2,16,384]{3,2,1,0:T(8,128)S(1)} %collective-permute-done.15.refs_7_), channel_id=1, source_target_pairs={{0,8},{8,0},{16,24},{24,16},{28,20},{20,28},{12,4},{4,12},{1,9},{9... | collective-permute-start | bytes 294920 | tf_op jit(solution)/shard_map/ppermute | solution.py:496
  54.8 0.1 collective-permute-start.19
  54.9 5.5 %collective-permute-done.16.refs_8_ = f32[2,2,16,384]{3,2,1,0:T(8,128)S(1)} collective-permute-done((f32[2,2,16,384]{3,2,1,0:T(8,128)S(1)}, f32[2,2,16,384]{3,2,1,0:T(8,128)S(1)}, u32[]{:S(2)}, u32[]{:S(2)}) %collective-permute-start.16) | collective-permute-done | bytes 98336 | tf_op jit(solution)/shard_map/ppermute | solution.py:496
  60.4 0.2 collective-permute-start.22
  60.6 0.7 collective-permute-start.23
  61.3 3.4 %prep.3 = (bf16[8,3,192,192]{3,2,1,0:T(8,128)(2,1)S(1)}, bf16[8,3,192,192]{3,2,1,0:T(8,128)(2,1)S(1)}) custom-call(f32[8,576,128]{2,1,0:T(8,128)} %bitcast.59), custom_call_target="tpu_custom_call" | custom-call | tf_op jit(solution)/shard_map/prep/pallas_call | solution.py:241
  64.8 2.6 %prep.2 = (bf16[8,3,192,192]{3,2,1,0:T(8,128)(2,1)S(1)}, bf16[8,3,192,192]{3,2,1,0:T(8,128)(2,1)S(1)}) custom-call(f32[8,576,128]{2,1,0:T(8,128)} %bitcast.60), custom_call_target="tpu_custom_call" | custom-call | tf_op jit(solution)/shard_map/prep/pallas_call | solution.py:241
  67.4 0.4 angles.1.refs_12_.refs_2_
  67.9 2.1 %early.1.partial = f32[8,2,96,384]{3,2,1,0:T(8,128)S(1)} custom-call(f32[2,2,32,384]{3,2,1,0:T(8,128)S(1)} %pad_maximum_fusion.refs_0_, f32[2,2,32,384]{3,2,1,0:T(8,128)S(1)} %collective-permute-done.7.refs_1_, f32[2,2,32,384]{3,2,1,0:T(8,128)S(1)} %collective-permute-done.8.refs_2_, f32[2,2,32,384]{3,2,1,0:T(8,128)S(1)} %pad_maximum_fusion.1.refs_3_, ...), custom_call_target="tpu_custom_call" | custom-call | tf_op jit(solution)/shard_map/early/pallas_call | solution.py:338
  69.9 1.5 %inner.1.done = f32[8,2,128,192]{3,2,1,0:T(8,128)S(1)} custom-call(f32[8,2,96,384]{3,2,1,0:T(8,128)S(1)} %early.1.partial, f32[2,2,32,384]{3,2,1,0:T(8,128)S(1)} %collective-permute-done.20.refs_0_, f32[2,2,32,384]{3,2,1,0:T(8,128)S(1)} %collective-permute-done.21.refs_1_, f32[2,256,128]{2,1,0:T(8,128)S(1)} %angles.1.refs_12_.refs_2_, ...), custom_call_target="tpu_custom_call" | custom-call | tf_op jit(solution)/shard_map/inner/pallas_call | solution.py:397
  71.4 3.7 %final.1 = f32[8,288,128]{2,1,0:T(8,128)} custom-call(f32[8,2,128,192]{3,2,1,0:T(8,128)S(1)} %inner.1.done, f32[8,2,96,384]{3,2,1,0:T(8,128)S(1)} %early.1.partial, f32[2,2,16,384]{3,2,1,0:T(8,128)S(1)} %collective-permute-done.22.refs_0_, f32[2,2,16,384]{3,2,1,0:T(8,128)S(1)} %collective-permute-done.23.refs_1_, f32[2,256,128]{2,1,0:T(8,128)S(1)} %angles.1.refs_12_.refs_2_, ...), custom_call_target="tpu_custom_call" | custom-call | tf_op jit(solution)/shard_map/final/pallas_call | solution.py:455
  (25 shorter events, 0.2 us)
Async XLA Ops:
  1.4 5.7 %collective-permute-start.2 = (f32[16,128]{1,0:T(8,128)S(1)}, f32[16,128]{1,0:T(8,128)S(1)}, u32[]{:S(2)}, u32[]{:S(2)}) collective-permute-start(f32[16,128]{1,0:T(8,128)S(1)} %pack.1), channel_id=1, source_target_pairs={{0,12},{4,8},{8,4},{12,0},{16,28},{20,24},{24,20},{28,16},{1,13},{... | collective-permute-start | bytes 24584 | tf_op jit(solution)/shard_map/ppermute | solution.py:470
  5.4 3.7 %collective-permute-start.1 = (f32[16,128]{1,0:T(8,128)S(1)}, f32[16,128]{1,0:T(8,128)S(1)}, u32[]{:S(2)}, u32[]{:S(2)}) collective-permute-start(f32[16,128]{1,0:T(8,128)S(1)} %pack.1), channel_id=1, source_target_pairs={{0,8},{4,12},{8,0},{12,4},{16,24},{20,28},{24,16},{28,20},{1,9},{5... | collective-permute-start | bytes 24584 | tf_op jit(solution)/shard_map/ppermute | solution.py:470
  5.9 3.7 %collective-permute-start = (f32[16,128]{1,0:T(8,128)S(1)}, f32[16,128]{1,0:T(8,128)S(1)}, u32[]{:S(2)}, u32[]{:S(2)}) collective-permute-start(f32[16,128]{1,0:T(8,128)S(1)} %pack.1), channel_id=1, source_target_pairs={{0,4},{4,0},{8,12},{12,8},{16,20},{20,16},{24,28},{28,24},{1,5},{5... | collective-permute-start | bytes 24584 | tf_op jit(solution)/shard_map/ppermute | solution.py:470
  9.5 7.8 %collective-permute-start.3 = (f32[16,128]{1,0:T(8,128)S(1)}, f32[16,128]{1,0:T(8,128)S(1)}, u32[]{:S(2)}, u32[]{:S(2)}) collective-permute-start(f32[16,128]{1,0:T(8,128)S(1)} %add_add_fusion.e0), channel_id=1, source_target_pairs={{0,16},{4,20},{8,24},{12,28},{16,0},{20,4},{24,8},{28,12},{1,17},{... | collective-permute-start | bytes 24584 | tf_op jit(solution)/shard_map/ppermute | solution.py:470
  18.2 1.9 %collective-permute-start.4 = (f32[2,2,1,64,384]{4,3,1,2,0:T(8,128)S(1)}, f32[2,2,1,64,384]{4,3,1,2,0:T(8,128)S(1)}, u32[]{:S(2)}, u32[]{:S(2)}) collective-permute-start(f32[2,2,1,64,384]{4,3,1,2,0:T(8,128)S(1)} %bitcast.57), channel_id=1, source_target_pairs={{0,1},{1,0},{2,3},{3,2},{4,5},{5,4},{6,7},{7,6},{8,9},{9,8},{10,11... | collective-permute-start | bytes 1179656 | tf_op jit(solution)/shard_map/ppermute | solution.py:470
  19.5 2.2 %collective-permute-start.12 = (f32[2,2,1,32,384]{4,3,1,2,0:T(8,128)S(1)}, f32[2,2,1,32,384]{4,3,1,2,0:T(8,128)S(1)}, u32[]{:S(2)}, u32[]{:S(2)}) collective-permute-start(f32[2,2,1,32,384]{4,3,1,2,0:T(8,128)S(1)} %bitcast.58), channel_id=1, source_target_pairs={{0,1},{1,0},{2,3},{3,2},{4,5},{5,4},{6,7},{7,6},{8,9},{9,8},{10,11... | collective-permute-start | bytes 589832 | tf_op jit(solution)/shard_map/ppermute | solution.py:470
  20.1 7.8 %collective-permute-start.5 = (f32[2,1,64,384]{3,2,0,1:T(8,128)S(1)}, f32[2,1,64,384]{3,2,0,1:T(8,128)S(1)}, u32[]{:S(2)}, u32[]{:S(2)}) collective-permute-start(f32[2,1,64,384]{3,2,0,1:T(8,128)S(1)} %fusion), channel_id=1, source_target_pairs={{0,2},{1,3},{2,0},{3,1},{4,6},{5,7},{6,4},{7,5},{8,10},{9,11},{10,... | collective-permute-start | bytes 589832 | tf_op jit(solution)/shard_map/ppermute | solution.py:470
  21.7 7.9 %collective-permute-start.13 = (f32[2,1,32,384]{3,2,0,1:T(8,128)S(1)}, f32[2,1,32,384]{3,2,0,1:T(8,128)S(1)}, u32[]{:S(2)}, u32[]{:S(2)}) collective-permute-start(f32[2,1,32,384]{3,2,0,1:T(8,128)S(1)} %fusion.5), channel_id=1, source_target_pairs={{0,2},{1,3},{2,0},{3,1},{4,6},{5,7},{6,4},{7,5},{8,10},{9,11},{10,... | collective-permute-start | bytes 294920 | tf_op jit(solution)/shard_map/ppermute | solution.py:470
  28.0 4.7 %collective-permute-start.6 = (f32[1,2,32,384]{3,2,1,0:T(8,128)S(1)}, f32[1,2,32,384]{3,2,1,0:T(8,128)S(1)}, u32[]{:S(2)}, u32[]{:S(2)}) collective-permute-start(f32[1,2,32,384]{3,2,1,0:T(8,128)S(1)} %get-tuple-element.34), channel_id=1, source_target_pairs={{0,8},{8,0},{16,24},{24,16},{28,20},{20,28},{12,4},{4,12},{1,9},{9... | collective-permute-start | bytes 294920 | tf_op jit(solution)/shard_map/ppermute | solution.py:496
  29.7 5.7 %collective-permute-start.9 = (f32[1,2,32,384]{3,2,1,0:T(8,128)S(1)}, f32[1,2,32,384]{3,2,1,0:T(8,128)S(1)}, u32[]{:S(2)}, u32[]{:S(2)}) collective-permute-start(f32[1,2,32,384]{3,2,1,0:T(8,128)S(1)} %get-tuple-element.33), channel_id=1, source_target_pairs={{8,16},{16,8},{24,28},{28,24},{20,12},{12,20},{4,0},{0,4},{9,17},{... | collective-permute-start | bytes 294920 | tf_op jit(solution)/shard_map/ppermute | solution.py:496
  32.7 10.2 %collective-permute-start.7 = (f32[2,2,32,384]{3,2,1,0:T(8,128)S(1)}, f32[2,2,32,384]{3,2,1,0:T(8,128)S(1)}, u32[]{:S(2)}, u32[]{:S(2)}) collective-permute-start(f32[2,2,32,384]{3,2,1,0:T(8,128)S(1)} %pad_maximum_fusion.refs_0_), channel_id=1, source_target_pairs={{8,16},{16,8},{24,28},{28,24},{20,12},{12,20},{4,0},{0,4},{9,17},{... | collective-permute-start | bytes 589832 | tf_op jit(solution)/shard_map/ppermute | solution.py:496
  35.5 8.3 %collective-permute-start.10 = (f32[2,2,32,384]{3,2,1,0:T(8,128)S(1)}, f32[2,2,32,384]{3,2,1,0:T(8,128)S(1)}, u32[]{:S(2)}, u32[]{:S(2)}) collective-permute-start(f32[2,2,32,384]{3,2,1,0:T(8,128)S(1)} %pad_maximum_fusion.1.refs_3_), channel_id=1, source_target_pairs={{0,8},{8,0},{16,24},{24,16},{28,20},{20,28},{12,4},{4,12},{1,9},{9... | collective-permute-start | bytes 589832 | tf_op jit(solution)/shard_map/ppermute | solution.py:496
  36.6 6.3 %collective-permute-start.14 = (f32[1,2,16,384]{3,2,1,0:T(8,128)S(1)}, f32[1,2,16,384]{3,2,1,0:T(8,128)S(1)}, u32[]{:S(2)}, u32[]{:S(2)}) collective-permute-start(f32[1,2,16,384]{3,2,1,0:T(8,128)S(1)} %get-tuple-element.36), channel_id=1, source_target_pairs={{0,8},{8,0},{16,24},{24,16},{28,20},{20,28},{12,4},{4,12},{1,9},{9... | collective-permute-start | bytes 147464 | tf_op jit(solution)/shard_map/ppermute | solution.py:496
  37.6 7.4 %collective-permute-start.17 = (f32[1,2,16,384]{3,2,1,0:T(8,128)S(1)}, f32[1,2,16,384]{3,2,1,0:T(8,128)S(1)}, u32[]{:S(2)}, u32[]{:S(2)}) collective-permute-start(f32[1,2,16,384]{3,2,1,0:T(8,128)S(1)} %get-tuple-element.35), channel_id=1, source_target_pairs={{8,16},{16,8},{24,28},{28,24},{20,12},{12,20},{4,0},{0,4},{9,17},{... | collective-permute-start | bytes 147464 | tf_op jit(solution)/shard_map/ppermute | solution.py:496
  42.9 10.6 %collective-permute-start.15 = (f32[2,2,16,384]{3,2,1,0:T(8,128)S(1)}, f32[2,2,16,384]{3,2,1,0:T(8,128)S(1)}, u32[]{:S(2)}, u32[]{:S(2)}) collective-permute-start(f32[2,2,16,384]{3,2,1,0:T(8,128)S(1)} %pad_maximum_fusion.2.refs_6_), channel_id=1, source_target_pairs={{8,16},{16,8},{24,28},{28,24},{20,12},{12,20},{4,0},{0,4},{9,17},{... | collective-permute-start | bytes 294920 | tf_op jit(solution)/shard_map/ppermute | solution.py:496
  43.0 7.8 %collective-permute-start.8 = (f32[2,2,32,384]{3,2,1,0:T(8,128)S(1)}, f32[2,2,32,384]{3,2,1,0:T(8,128)S(1)}, u32[]{:S(2)}, u32[]{:S(2)}) collective-permute-start(f32[2,2,32,384]{3,2,1,0:T(8,128)S(1)} %collective-permute-done.7.refs_1_), channel_id=1, source_target_pairs={{0,8},{8,0},{16,24},{24,16},{28,20},{20,28},{12,4},{4,12},{1,9},{9... | collective-permute-start | bytes 589832 | tf_op jit(solution)/shard_map/ppermute | solution.py:496
  43.7 9.0 %collective-permute-start.11 = (f32[2,2,32,384]{3,2,1,0:T(8,128)S(1)}, f32[2,2,32,384]{3,2,1,0:T(8,128)S(1)}, u32[]{:S(2)}, u32[]{:S(2)}) collective-permute-start(f32[2,2,32,384]{3,2,1,0:T(8,128)S(1)} %collective-permute-done.10.refs_4_), channel_id=1, source_target_pairs={{8,16},{16,8},{24,28},{28,24},{20,12},{12,20},{4,0},{0,4},{9,17},{... | collective-permute-start | bytes 589832 | tf_op jit(solution)/shard_map/ppermute | solution.py:496
  45.1 9.7 %collective-permute-start.18 = (f32[2,2,16,384]{3,2,1,0:T(8,128)S(1)}, f32[2,2,16,384]{3,2,1,0:T(8,128)S(1)}, u32[]{:S(2)}, u32[]{:S(2)}) collective-permute-start(f32[2,2,16,384]{3,2,1,0:T(8,128)S(1)} %pad_maximum_fusion.3.refs_9_), channel_id=1, source_target_pairs={{0,8},{8,0},{16,24},{24,16},{28,20},{20,28},{12,4},{4,12},{1,9},{9... | collective-permute-start | bytes 294920 | tf_op jit(solution)/shard_map/ppermute | solution.py:496
  50.8 19.1 %collective-permute-start.20 = (f32[2,2,32,384]{3,2,1,0:T(8,128)S(1)}, f32[2,2,32,384]{3,2,1,0:T(8,128)S(1)}, u32[]{:S(2)}, u32[]{:S(2)}) collective-permute-start(f32[2,2,32,384]{3,2,1,0:T(8,128)S(1)} %collective-permute-done.8.refs_2_), channel_id=1, source_target_pairs={{8,16},{16,8},{24,28},{28,24},{20,12},{12,20},{4,0},{0,4},{9,17},{... | collective-permute-start | bytes 589832 | tf_op jit(solution)/shard_map/ppermute | solution.py:496
  52.8 17.2 %collective-permute-start.21 = (f32[2,2,32,384]{3,2,1,0:T(8,128)S(1)}, f32[2,2,32,384]{3,2,1,0:T(8,128)S(1)}, u32[]{:S(2)}, u32[]{:S(2)}) collective-permute-start(f32[2,2,32,384]{3,2,1,0:T(8,128)S(1)} %collective-permute-done.11.refs_5_), channel_id=1, source_target_pairs={{0,8},{8,0},{16,24},{24,16},{28,20},{20,28},{12,4},{4,12},{1,9},{9... | collective-permute-start | bytes 589832 | tf_op jit(solution)/shard_map/ppermute | solution.py:496
  53.5 6.9 %collective-permute-start.16 = (f32[2,2,16,384]{3,2,1,0:T(8,128)S(1)}, f32[2,2,16,384]{3,2,1,0:T(8,128)S(1)}, u32[]{:S(2)}, u32[]{:S(2)}) collective-permute-start(f32[2,2,16,384]{3,2,1,0:T(8,128)S(1)} %collective-permute-done.15.refs_7_), channel_id=1, source_target_pairs={{0,8},{8,0},{16,24},{24,16},{28,20},{20,28},{12,4},{4,12},{1,9},{9... | collective-permute-start | bytes 294920 | tf_op jit(solution)/shard_map/ppermute | solution.py:496
  54.8 5.8 %collective-permute-start.19 = (f32[2,2,16,384]{3,2,1,0:T(8,128)S(1)}, f32[2,2,16,384]{3,2,1,0:T(8,128)S(1)}, u32[]{:S(2)}, u32[]{:S(2)}) collective-permute-start(f32[2,2,16,384]{3,2,1,0:T(8,128)S(1)} %collective-permute-done.18.refs_10_), channel_id=1, source_target_pairs={{8,16},{16,8},{24,28},{28,24},{20,12},{12,20},{4,0},{0,4},{9,17},{... | collective-permute-start | bytes 294920 | tf_op jit(solution)/shard_map/ppermute | solution.py:496
  60.4 11.0 %collective-permute-start.22 = (f32[2,2,16,384]{3,2,1,0:T(8,128)S(1)}, f32[2,2,16,384]{3,2,1,0:T(8,128)S(1)}, u32[]{:S(2)}, u32[]{:S(2)}) collective-permute-start(f32[2,2,16,384]{3,2,1,0:T(8,128)S(1)} %collective-permute-done.16.refs_8_), channel_id=1, source_target_pairs={{8,16},{16,8},{24,28},{28,24},{20,12},{12,20},{4,0},{0,4},{9,17},{... | collective-permute-start | bytes 294920 | tf_op jit(solution)/shard_map/ppermute | solution.py:496
  60.6 10.8 %collective-permute-start.23 = (f32[2,2,16,384]{3,2,1,0:T(8,128)S(1)}, f32[2,2,16,384]{3,2,1,0:T(8,128)S(1)}, u32[]{:S(2)}, u32[]{:S(2)}) collective-permute-start(f32[2,2,16,384]{3,2,1,0:T(8,128)S(1)} %collective-permute-done.19.refs_11_), channel_id=1, source_target_pairs={{0,8},{8,0},{16,24},{24,16},{28,20},{20,28},{12,4},{4,12},{1,9},{9... | collective-permute-start | bytes 294920 | tf_op jit(solution)/shard_map/ppermute | solution.py:496
  61.3 6.1 %copy-start = (s32[8,3]{0,1:T(4,128)S(1)}, s32[8,3]{0,1:T(4,128)}, u32[]{:S(2)}) copy-start(s32[8,3]{0,1:T(4,128)} %param.15) | copy-start | bytes 292

commit v7 on v6

--- a/solution.py
+++ b/solution.py
@@ -542,10 +542,12 @@
             if bit < n_row:
                 payload = payload + other
         hop += 1
-    cuts = 3 if width % 48 == 0 else 1
-    pieces = []
-    for i in range(cuts):
-        pieces += fetch(constants, i * width // cuts, width // cuts)
+    shares = (2, 1)
+    pieces, base = [], 0
+    for i, share in enumerate(shares):
+        rows = share * width // sum(shares) if i + 1 < len(shares) else width - base
+        pieces += fetch(constants, base, rows)
+        base += rows
     spans = chunks(half)
     weight = (jnp.arange(slots, dtype=jnp.int32) < live_count[0]).astype(F32)
     owns = []

time: 75.6 us -> 75.5 us (level)
  Pallas kernels: 21.1 us -> 20.2 us
    ppermute x8, waiting for transfers between devices: 8.67 us -> 10.3 us  [swap(): return lax.ppermute(x, axis, [(i, i ^ bit) for i in range(n)])]
    ppermute x16, waiting for transfers between devices: 19.8 us -> 18.3 us  [neighbour_gather(): arrived.append(lax.ppermute(moving[h], 'row', perm))]
    pallas_call x3 -> x2, Pallas kernels: 5.14 us -> 4.2 us  [fetch(): pl.pallas_call(functools.partial(fetch_kernel, slots, first, rows, parts)...]
    ppermute x16, starting transfers between devices: 13.4 us -> 14.2 us  [neighbour_gather(): arrived.append(lax.ppermute(moving[h], 'row', perm))]
  transfers between devices with their start and end apart: 24 -> 24, of which waited for: 9 -> 10; matrix products, arithmetic and copies ran while one was open for 0% -> 0% of each run, Pallas kernels for 21% -> 20%
where the time goes in v7:
time: 75.5 us; the launch traced here: 75.2 us
  waiting for transfers between devices  28.5 us (38%)
  starting transfers between devices  24.6 us (33%)
  Pallas kernels  20.2 us (27%)
  between operations  1.65 us (2%)
    ppermute x16, waiting for transfers between devices, neighbour_gather(): arrived.append(lax.ppermute(moving[h], 'row', perm))  18.3 us
    ppermute x16, starting transfers between devices, neighbour_gather(): arrived.append(lax.ppermute(moving[h], 'row', perm))  14.2 us
    ppermute x8, starting transfers between devices, swap(): return lax.ppermute(x, axis, [(i, i ^ bit) for i in range(n)])  10.5 us
    ppermute x8, waiting for transfers between devices, swap(): return lax.ppermute(x, axis, [(i, i ^ bit) for i in range(n)])  10.3 us
    pallas_call x2, Pallas kernels, prep(): pl.pallas_call(functools.partial(prep_kernel, size, turn, spans), out_sha...  6.09 us
    pallas_call x2, Pallas kernels, fetch(): pl.pallas_call(functools.partial(fetch_kernel, slots, first, rows, parts)...  4.2 us
    pallas_call x1, Pallas kernels, final(): pl.pallas_call(functools.partial(final_kernel, span, width, spec, 1.0 / t...  3.7 us
    pallas_call x1, Pallas kernels, early(): pl.pallas_call(functools.partial(early_kernel, spec, width, 8), out_shape...  2.05 us
  transfers between devices with their start and end apart: 24, of which 10 were waited for; matrix products, arithmetic and copies ran while one was open for 0% of the time, Pallas kernels for 20%

profile of v7, /device:TPU:0, one launch (start us, length us, event | category | flops | bytes accessed | tf_op | source)
XLA Modules:
  0.0 75.2 jit_solution(10047002509759973340)
XLA Ops:
  0.7 0.7 pack.1
  1.4 3.0 %collective-permute-start = (f32[16,128]{1,0:T(8,128)S(1)}, f32[16,128]{1,0:T(8,128)S(1)}, u32[]{:S(2)}, u32[]{:S(2)}) collective-permute-start(f32[16,128]{1,0:T(8,128)S(1)} %pack.1), channel_id=1, source_target_pairs={{0,4},{4,0},{8,12},{12,8},{16,20},{20,16},{24,28},{28,24},{1,5},{5... | collective-permute-start | bytes 24584 | tf_op jit(solution)/shard_map/ppermute | solution.py:470
  4.4 1.6 %collective-permute-start.1 = (f32[16,128]{1,0:T(8,128)S(1)}, f32[16,128]{1,0:T(8,128)S(1)}, u32[]{:S(2)}, u32[]{:S(2)}) collective-permute-start(f32[16,128]{1,0:T(8,128)S(1)} %pack.1), channel_id=1, source_target_pairs={{0,8},{4,12},{8,0},{12,4},{16,24},{20,28},{24,16},{28,20},{1,9},{5... | collective-permute-start | bytes 24584 | tf_op jit(solution)/shard_map/ppermute | solution.py:470
  6.0 0.1 collective-permute-done
  6.0 2.0 %collective-permute-done.1 = f32[16,128]{1,0:T(8,128)S(1)} collective-permute-done((f32[16,128]{1,0:T(8,128)S(1)}, f32[16,128]{1,0:T(8,128)S(1)}, u32[]{:S(2)}, u32[]{:S(2)}) %collective-permute-start.1) | collective-permute-done | bytes 8224 | tf_op jit(solution)/shard_map/ppermute | solution.py:470
  8.1 2.5 %collective-permute-done.2 = f32[16,128]{1,0:T(8,128)S(1)} collective-permute-done((f32[16,128]{1,0:T(8,128)S(1)}, f32[16,128]{1,0:T(8,128)S(1)}, u32[]{:S(2)}, u32[]{:S(2)}) %collective-permute-start.2) | collective-permute-done | bytes 8224 | tf_op jit(solution)/shard_map/ppermute | solution.py:470
  10.6 2.6 %collective-permute-start.3 = (f32[16,128]{1,0:T(8,128)S(1)}, f32[16,128]{1,0:T(8,128)S(1)}, u32[]{:S(2)}, u32[]{:S(2)}) collective-permute-start(f32[16,128]{1,0:T(8,128)S(1)} %add_add_fusion.e0), channel_id=1, source_target_pairs={{0,16},{4,20},{8,24},{12,28},{16,0},{20,4},{24,8},{28,12},{1,17},{... | collective-permute-start | bytes 24584 | tf_op jit(solution)/shard_map/ppermute | solution.py:470
  13.1 2.5 %fetch.2 = (bf16[1,32,36864]{2,1,0:T(8,128)(2,1)S(1)}, bf16[1,32,36864]{2,1,0:T(8,128)(2,1)S(1)}) custom-call(f32[1,48,36864]{2,1,0:T(8,128)} %const.3), custom_call_target="tpu_custom_call" | custom-call | tf_op jit(solution)/shard_map/fetch/pallas_call | solution.py:121
  15.6 1.7 %fetch.3 = (bf16[1,16,36864]{2,1,0:T(8,128)(2,1)S(1)}, bf16[1,16,36864]{2,1,0:T(8,128)(2,1)S(1)}) custom-call(f32[1,48,36864]{2,1,0:T(8,128)} %const.3), custom_call_target="tpu_custom_call" | custom-call | tf_op jit(solution)/shard_map/fetch/pallas_call | solution.py:121
  17.4 1.0 %contract.2 = (f32[4,1,64,384]{3,2,1,0:T(8,128)S(1)}, f32[4,1,64,384]{3,2,1,0:T(8,128)S(1)}) custom-call(f32[16,128]{1,0:T(8,128)S(1)} %add_add_fusion.e0, f32[16,128]{1,0:T(8,128)S(1)} %collective-permute-done.3.e1, bf16[1,32,36864]{2,1,0:T(8,128)(2,1)S(1)} %get-tuple-element.17.refs_0_, bf16[1,32,36864]{2,1,0:T(8,128)(2,1)S(1)} %get-tuple-element.18.refs_1_, ...), custom_call_target="tpu_custom_call" | custom-call | tf_op jit(solution)/shard_map/contract/pallas_call | solution.py:174
  18.3 0.1 collective-permute-start.4
  19.1 0.6 contract.3
  19.7 0.6 collective-permute-start.12
  20.3 1.6 %collective-permute-start.5 = (f32[2,1,64,384]{3,2,0,1:T(8,128)S(1)}, f32[2,1,64,384]{3,2,0,1:T(8,128)S(1)}, u32[]{:S(2)}, u32[]{:S(2)}) collective-permute-start(f32[2,1,64,384]{3,2,0,1:T(8,128)S(1)} %fusion), channel_id=1, source_target_pairs={{0,2},{1,3},{2,0},{3,1},{4,6},{5,7},{6,4},{7,5},{8,10},{9,11},{10,... | collective-permute-start | bytes 589832 | tf_op jit(solution)/shard_map/ppermute | solution.py:470
  21.8 0.0 collective-permute-done.12
  21.9 1.0 %collective-permute-start.13 = (f32[2,1,32,384]{3,2,0,1:T(8,128)S(1)}, f32[2,1,32,384]{3,2,0,1:T(8,128)S(1)}, u32[]{:S(2)}, u32[]{:S(2)}) collective-permute-start(f32[2,1,32,384]{3,2,0,1:T(8,128)S(1)} %fusion.5), channel_id=1, source_target_pairs={{0,2},{1,3},{2,0},{3,1},{4,6},{5,7},{6,4},{7,5},{8,10},{9,11},{10,... | collective-permute-start | bytes 294920 | tf_op jit(solution)/shard_map/ppermute | solution.py:470
  22.9 5.2 %collective-permute-done.5 = f32[2,1,64,384]{3,2,0,1:T(8,128)S(1)} collective-permute-done((f32[2,1,64,384]{3,2,0,1:T(8,128)S(1)}, f32[2,1,64,384]{3,2,0,1:T(8,128)S(1)}, u32[]{:S(2)}, u32[]{:S(2)}) %collective-permute-start.5) | collective-permute-done | bytes 196640 | tf_op jit(solution)/shard_map/ppermute | solution.py:470
  28.2 0.6 collective-permute-start.9
  28.8 0.5 collective-permute-done.13
  29.3 0.5 collective-permute-start.6
  29.8 3.0 %collective-permute-done.9 = f32[1,2,32,384]{3,2,1,0:T(8,128)S(1)} collective-permute-done((f32[1,2,32,384]{3,2,1,0:T(8,128)S(1)}, f32[1,2,32,384]{3,2,1,0:T(8,128)S(1)}, u32[]{:S(2)}, u32[]{:S(2)}) %collective-permute-start.9) | collective-permute-done | bytes 98336 | tf_op jit(solution)/shard_map/ppermute | solution.py:496
  32.9 0.5 collective-permute-start.10
  33.4 1.6 %collective-permute-done.6 = f32[1,2,32,384]{3,2,1,0:T(8,128)S(1)} collective-permute-done((f32[1,2,32,384]{3,2,1,0:T(8,128)S(1)}, f32[1,2,32,384]{3,2,1,0:T(8,128)S(1)}, u32[]{:S(2)}, u32[]{:S(2)}) %collective-permute-start.6) | collective-permute-done | bytes 98336 | tf_op jit(solution)/shard_map/ppermute | solution.py:496
  35.0 1.1 %collective-permute-start.7 = (f32[2,2,32,384]{3,2,1,0:T(8,128)S(1)}, f32[2,2,32,384]{3,2,1,0:T(8,128)S(1)}, u32[]{:S(2)}, u32[]{:S(2)}) collective-permute-start(f32[2,2,32,384]{3,2,1,0:T(8,128)S(1)} %pad_maximum_fusion.refs_0_), channel_id=1, source_target_pairs={{8,16},{16,8},{24,28},{28,24},{20,12},{12,20},{4,0},{0,4},{9,17},{... | collective-permute-start | bytes 589832 | tf_op jit(solution)/shard_map/ppermute | solution.py:496
  36.1 1.1 %collective-permute-start.17 = (f32[1,2,16,384]{3,2,1,0:T(8,128)S(1)}, f32[1,2,16,384]{3,2,1,0:T(8,128)S(1)}, u32[]{:S(2)}, u32[]{:S(2)}) collective-permute-start(f32[1,2,16,384]{3,2,1,0:T(8,128)S(1)} %get-tuple-element.31), channel_id=1, source_target_pairs={{8,16},{16,8},{24,28},{28,24},{20,12},{12,20},{4,0},{0,4},{9,17},{... | collective-permute-start | bytes 147464 | tf_op jit(solution)/shard_map/ppermute | solution.py:496
  37.2 0.4 collective-permute-start.14
  37.7 4.4 %collective-permute-done.17 = f32[1,2,16,384]{3,2,1,0:T(8,128)S(1)} collective-permute-done((f32[1,2,16,384]{3,2,1,0:T(8,128)S(1)}, f32[1,2,16,384]{3,2,1,0:T(8,128)S(1)}, u32[]{:S(2)}, u32[]{:S(2)}) %collective-permute-start.17) | collective-permute-done | bytes 49184 | tf_op jit(solution)/shard_map/ppermute | solution.py:496
  42.0 0.1 collective-permute-start.18
  42.1 0.0 collective-permute-done.10.refs_4_
  42.1 1.5 %collective-permute-start.11 = (f32[2,2,32,384]{3,2,1,0:T(8,128)S(1)}, f32[2,2,32,384]{3,2,1,0:T(8,128)S(1)}, u32[]{:S(2)}, u32[]{:S(2)}) collective-permute-start(f32[2,2,32,384]{3,2,1,0:T(8,128)S(1)} %collective-permute-done.10.refs_4_), channel_id=1, source_target_pairs={{8,16},{16,8},{24,28},{28,24},{20,12},{12,20},{4,0},{0,4},{9,17},{... | collective-permute-start | bytes 589832 | tf_op jit(solution)/shard_map/ppermute | solution.py:496
  43.7 0.0 collective-permute-done.7.refs_1_
  43.7 0.6 collective-permute-start.8
  44.2 0.0 collective-permute-done.14
  44.2 1.5 %collective-permute-start.15 = (f32[2,2,16,384]{3,2,1,0:T(8,128)S(1)}, f32[2,2,16,384]{3,2,1,0:T(8,128)S(1)}, u32[]{:S(2)}, u32[]{:S(2)}) collective-permute-start(f32[2,2,16,384]{3,2,1,0:T(8,128)S(1)} %pad_maximum_fusion.2.refs_6_), channel_id=1, source_target_pairs={{8,16},{16,8},{24,28},{28,24},{20,12},{12,20},{4,0},{0,4},{9,17},{... | collective-permute-start | bytes 294920 | tf_op jit(solution)/shard_map/ppermute | solution.py:496
  45.7 3.5 %collective-permute-done.11.refs_5_ = f32[2,2,32,384]{3,2,1,0:T(8,128)S(1)} collective-permute-done((f32[2,2,32,384]{3,2,1,0:T(8,128)S(1)}, f32[2,2,32,384]{3,2,1,0:T(8,128)S(1)}, u32[]{:S(2)}, u32[]{:S(2)}) %collective-permute-start.11) | collective-permute-done | bytes 196640 | tf_op jit(solution)/shard_map/ppermute | solution.py:496
  49.3 2.7 %collective-permute-start.21 = (f32[2,2,32,384]{3,2,1,0:T(8,128)S(1)}, f32[2,2,32,384]{3,2,1,0:T(8,128)S(1)}, u32[]{:S(2)}, u32[]{:S(2)}) collective-permute-start(f32[2,2,32,384]{3,2,1,0:T(8,128)S(1)} %collective-permute-done.11.refs_5_), channel_id=1, source_target_pairs={{0,8},{8,0},{16,24},{24,16},{28,20},{20,28},{12,4},{4,12},{1,9},{9... | collective-permute-start | bytes 589832 | tf_op jit(solution)/shard_map/ppermute | solution.py:496
  51.9 1.4 %collective-permute-start.20 = (f32[2,2,32,384]{3,2,1,0:T(8,128)S(1)}, f32[2,2,32,384]{3,2,1,0:T(8,128)S(1)}, u32[]{:S(2)}, u32[]{:S(2)}) collective-permute-start(f32[2,2,32,384]{3,2,1,0:T(8,128)S(1)} %collective-permute-done.8.refs_2_), channel_id=1, source_target_pairs={{8,16},{16,8},{24,28},{28,24},{20,12},{12,20},{4,0},{0,4},{9,17},{... | collective-permute-start | bytes 589832 | tf_op jit(solution)/shard_map/ppermute | solution.py:496
  53.4 0.6 collective-permute-start.19
  54.0 0.1 collective-permute-start.16
  54.0 5.7 %collective-permute-done.19.refs_11_ = f32[2,2,16,384]{3,2,1,0:T(8,128)S(1)} collective-permute-done((f32[2,2,16,384]{3,2,1,0:T(8,128)S(1)}, f32[2,2,16,384]{3,2,1,0:T(8,128)S(1)}, u32[]{:S(2)}, u32[]{:S(2)}) %collective-permute-start.19) | collective-permute-done | bytes 98336 | tf_op jit(solution)/shard_map/ppermute | solution.py:496
  59.7 0.1 collective-permute-start.23
  59.8 1.5 %collective-permute-start.22 = (f32[2,2,16,384]{3,2,1,0:T(8,128)S(1)}, f32[2,2,16,384]{3,2,1,0:T(8,128)S(1)}, u32[]{:S(2)}, u32[]{:S(2)}) collective-permute-start(f32[2,2,16,384]{3,2,1,0:T(8,128)S(1)} %collective-permute-done.16.refs_8_), channel_id=1, source_target_pairs={{8,16},{16,8},{24,28},{28,24},{20,12},{12,20},{4,0},{0,4},{9,17},{... | collective-permute-start | bytes 294920 | tf_op jit(solution)/shard_map/ppermute | solution.py:496
  61.2 2.6 %prep.2 = (bf16[8,3,192,192]{3,2,1,0:T(8,128)(2,1)S(1)}, bf16[8,3,192,192]{3,2,1,0:T(8,128)(2,1)S(1)}) custom-call(f32[8,576,128]{2,1,0:T(8,128)} %bitcast.59), custom_call_target="tpu_custom_call" | custom-call | tf_op jit(solution)/shard_map/prep/pallas_call | solution.py:241
  63.9 3.4 %prep.3 = (bf16[8,3,192,192]{3,2,1,0:T(8,128)(2,1)S(1)}, bf16[8,3,192,192]{3,2,1,0:T(8,128)(2,1)S(1)}) custom-call(f32[8,576,128]{2,1,0:T(8,128)} %bitcast.60), custom_call_target="tpu_custom_call" | custom-call | tf_op jit(solution)/shard_map/prep/pallas_call | solution.py:241
  67.4 0.4 angles.1.refs_12_.refs_2_
  67.8 2.1 %early.1.partial = f32[8,2,96,384]{3,2,1,0:T(8,128)S(1)} custom-call(f32[2,2,32,384]{3,2,1,0:T(8,128)S(1)} %pad_maximum_fusion.refs_0_, f32[2,2,32,384]{3,2,1,0:T(8,128)S(1)} %collective-permute-done.7.refs_1_, f32[2,2,32,384]{3,2,1,0:T(8,128)S(1)} %collective-permute-done.8.refs_2_, f32[2,2,32,384]{3,2,1,0:T(8,128)S(1)} %pad_maximum_fusion.1.refs_3_, ...), custom_call_target="tpu_custom_call" | custom-call | tf_op jit(solution)/shard_map/early/pallas_call | solution.py:338
  69.9 1.5 %inner.1.done = f32[8,2,128,192]{3,2,1,0:T(8,128)S(1)} custom-call(f32[8,2,96,384]{3,2,1,0:T(8,128)S(1)} %early.1.partial, f32[2,2,32,384]{3,2,1,0:T(8,128)S(1)} %collective-permute-done.20.refs_0_, f32[2,2,32,384]{3,2,1,0:T(8,128)S(1)} %collective-permute-done.21.refs_1_, f32[2,256,128]{2,1,0:T(8,128)S(1)} %angles.1.refs_12_.refs_2_, ...), custom_call_target="tpu_custom_call" | custom-call | tf_op jit(solution)/shard_map/inner/pallas_call | solution.py:397
  71.4 3.7 %final.1 = f32[8,288,128]{2,1,0:T(8,128)} custom-call(f32[8,2,128,192]{3,2,1,0:T(8,128)S(1)} %inner.1.done, f32[8,2,96,384]{3,2,1,0:T(8,128)S(1)} %early.1.partial, f32[2,2,16,384]{3,2,1,0:T(8,128)S(1)} %collective-permute-done.22.refs_0_, f32[2,2,16,384]{3,2,1,0:T(8,128)S(1)} %collective-permute-done.23.refs_1_, f32[2,256,128]{2,1,0:T(8,128)S(1)} %angles.1.refs_12_.refs_2_, ...), custom_call_target="tpu_custom_call" | custom-call | tf_op jit(solution)/shard_map/final/pallas_call | solution.py:455
  (24 shorter events, 0.2 us)
Async XLA Ops:
  1.4 4.7 %collective-permute-start = (f32[16,128]{1,0:T(8,128)S(1)}, f32[16,128]{1,0:T(8,128)S(1)}, u32[]{:S(2)}, u32[]{:S(2)}) collective-permute-start(f32[16,128]{1,0:T(8,128)S(1)} %pack.1), channel_id=1, source_target_pairs={{0,4},{4,0},{8,12},{12,8},{16,20},{20,16},{24,28},{28,24},{1,5},{5... | collective-permute-start | bytes 24584 | tf_op jit(solution)/shard_map/ppermute | solution.py:470
  4.4 3.7 %collective-permute-start.1 = (f32[16,128]{1,0:T(8,128)S(1)}, f32[16,128]{1,0:T(8,128)S(1)}, u32[]{:S(2)}, u32[]{:S(2)}) collective-permute-start(f32[16,128]{1,0:T(8,128)S(1)} %pack.1), channel_id=1, source_target_pairs={{0,8},{4,12},{8,0},{12,4},{16,24},{20,28},{24,16},{28,20},{1,9},{5... | collective-permute-start | bytes 24584 | tf_op jit(solution)/shard_map/ppermute | solution.py:470
  6.0 4.5 %collective-permute-start.2 = (f32[16,128]{1,0:T(8,128)S(1)}, f32[16,128]{1,0:T(8,128)S(1)}, u32[]{:S(2)}, u32[]{:S(2)}) collective-permute-start(f32[16,128]{1,0:T(8,128)S(1)} %pack.1), channel_id=1, source_target_pairs={{0,12},{4,8},{8,4},{12,0},{16,28},{20,24},{24,20},{28,16},{1,13},{... | collective-permute-start | bytes 24584 | tf_op jit(solution)/shard_map/ppermute | solution.py:470
  10.6 6.8 %collective-permute-start.3 = (f32[16,128]{1,0:T(8,128)S(1)}, f32[16,128]{1,0:T(8,128)S(1)}, u32[]{:S(2)}, u32[]{:S(2)}) collective-permute-start(f32[16,128]{1,0:T(8,128)S(1)} %add_add_fusion.e0), channel_id=1, source_target_pairs={{0,16},{4,20},{8,24},{12,28},{16,0},{20,4},{24,8},{28,12},{1,17},{... | collective-permute-start | bytes 24584 | tf_op jit(solution)/shard_map/ppermute | solution.py:470
  18.3 1.9 %collective-permute-start.4 = (f32[2,2,1,64,384]{4,3,1,2,0:T(8,128)S(1)}, f32[2,2,1,64,384]{4,3,1,2,0:T(8,128)S(1)}, u32[]{:S(2)}, u32[]{:S(2)}) collective-permute-start(f32[2,2,1,64,384]{4,3,1,2,0:T(8,128)S(1)} %bitcast.57), channel_id=1, source_target_pairs={{0,1},{1,0},{2,3},{3,2},{4,5},{5,4},{6,7},{7,6},{8,9},{9,8},{10,11... | collective-permute-start | bytes 1179656 | tf_op jit(solution)/shard_map/ppermute | solution.py:470
  19.7 2.2 %collective-permute-start.12 = (f32[2,2,1,32,384]{4,3,1,2,0:T(8,128)S(1)}, f32[2,2,1,32,384]{4,3,1,2,0:T(8,128)S(1)}, u32[]{:S(2)}, u32[]{:S(2)}) collective-permute-start(f32[2,2,1,32,384]{4,3,1,2,0:T(8,128)S(1)} %bitcast.58), channel_id=1, source_target_pairs={{0,1},{1,0},{2,3},{3,2},{4,5},{5,4},{6,7},{7,6},{8,9},{9,8},{10,11... | collective-permute-start | bytes 589832 | tf_op jit(solution)/shard_map/ppermute | solution.py:470
  20.3 7.8 %collective-permute-start.5 = (f32[2,1,64,384]{3,2,0,1:T(8,128)S(1)}, f32[2,1,64,384]{3,2,0,1:T(8,128)S(1)}, u32[]{:S(2)}, u32[]{:S(2)}) collective-permute-start(f32[2,1,64,384]{3,2,0,1:T(8,128)S(1)} %fusion), channel_id=1, source_target_pairs={{0,2},{1,3},{2,0},{3,1},{4,6},{5,7},{6,4},{7,5},{8,10},{9,11},{10,... | collective-permute-start | bytes 589832 | tf_op jit(solution)/shard_map/ppermute | solution.py:470
  21.9 7.4 %collective-permute-start.13 = (f32[2,1,32,384]{3,2,0,1:T(8,128)S(1)}, f32[2,1,32,384]{3,2,0,1:T(8,128)S(1)}, u32[]{:S(2)}, u32[]{:S(2)}) collective-permute-start(f32[2,1,32,384]{3,2,0,1:T(8,128)S(1)} %fusion.5), channel_id=1, source_target_pairs={{0,2},{1,3},{2,0},{3,1},{4,6},{5,7},{6,4},{7,5},{8,10},{9,11},{10,... | collective-permute-start | bytes 294920 | tf_op jit(solution)/shard_map/ppermute | solution.py:470
  28.2 4.7 %collective-permute-start.9 = (f32[1,2,32,384]{3,2,1,0:T(8,128)S(1)}, f32[1,2,32,384]{3,2,1,0:T(8,128)S(1)}, u32[]{:S(2)}, u32[]{:S(2)}) collective-permute-start(f32[1,2,32,384]{3,2,1,0:T(8,128)S(1)} %get-tuple-element.29), channel_id=1, source_target_pairs={{8,16},{16,8},{24,28},{28,24},{20,12},{12,20},{4,0},{0,4},{9,17},{... | collective-permute-start | bytes 294920 | tf_op jit(solution)/shard_map/ppermute | solution.py:496
  29.3 5.7 %collective-permute-start.6 = (f32[1,2,32,384]{3,2,1,0:T(8,128)S(1)}, f32[1,2,32,384]{3,2,1,0:T(8,128)S(1)}, u32[]{:S(2)}, u32[]{:S(2)}) collective-permute-start(f32[1,2,32,384]{3,2,1,0:T(8,128)S(1)} %get-tuple-element.30), channel_id=1, source_target_pairs={{0,8},{8,0},{16,24},{24,16},{28,20},{20,28},{12,4},{4,12},{1,9},{9... | collective-permute-start | bytes 294920 | tf_op jit(solution)/shard_map/ppermute | solution.py:496
  32.9 9.3 %collective-permute-start.10 = (f32[2,2,32,384]{3,2,1,0:T(8,128)S(1)}, f32[2,2,32,384]{3,2,1,0:T(8,128)S(1)}, u32[]{:S(2)}, u32[]{:S(2)}) collective-permute-start(f32[2,2,32,384]{3,2,1,0:T(8,128)S(1)} %pad_maximum_fusion.1.refs_3_), channel_id=1, source_target_pairs={{0,8},{8,0},{16,24},{24,16},{28,20},{20,28},{12,4},{4,12},{1,9},{9... | collective-permute-start | bytes 589832 | tf_op jit(solution)/shard_map/ppermute | solution.py:496
  35.0 8.6 %collective-permute-start.7 = (f32[2,2,32,384]{3,2,1,0:T(8,128)S(1)}, f32[2,2,32,384]{3,2,1,0:T(8,128)S(1)}, u32[]{:S(2)}, u32[]{:S(2)}) collective-permute-start(f32[2,2,32,384]{3,2,1,0:T(8,128)S(1)} %pad_maximum_fusion.refs_0_), channel_id=1, source_target_pairs={{8,16},{16,8},{24,28},{28,24},{20,12},{12,20},{4,0},{0,4},{9,17},{... | collective-permute-start | bytes 589832 | tf_op jit(solution)/shard_map/ppermute | solution.py:496
  36.1 5.9 %collective-permute-start.17 = (f32[1,2,16,384]{3,2,1,0:T(8,128)S(1)}, f32[1,2,16,384]{3,2,1,0:T(8,128)S(1)}, u32[]{:S(2)}, u32[]{:S(2)}) collective-permute-start(f32[1,2,16,384]{3,2,1,0:T(8,128)S(1)} %get-tuple-element.31), channel_id=1, source_target_pairs={{8,16},{16,8},{24,28},{28,24},{20,12},{12,20},{4,0},{0,4},{9,17},{... | collective-permute-start | bytes 147464 | tf_op jit(solution)/shard_map/ppermute | solution.py:496
  37.2 7.0 %collective-permute-start.14 = (f32[1,2,16,384]{3,2,1,0:T(8,128)S(1)}, f32[1,2,16,384]{3,2,1,0:T(8,128)S(1)}, u32[]{:S(2)}, u32[]{:S(2)}) collective-permute-start(f32[1,2,16,384]{3,2,1,0:T(8,128)S(1)} %get-tuple-element.32), channel_id=1, source_target_pairs={{0,8},{8,0},{16,24},{24,16},{28,20},{20,28},{12,4},{4,12},{1,9},{9... | collective-permute-start | bytes 147464 | tf_op jit(solution)/shard_map/ppermute | solution.py:496
  42.0 11.3 %collective-permute-start.18 = (f32[2,2,16,384]{3,2,1,0:T(8,128)S(1)}, f32[2,2,16,384]{3,2,1,0:T(8,128)S(1)}, u32[]{:S(2)}, u32[]{:S(2)}) collective-permute-start(f32[2,2,16,384]{3,2,1,0:T(8,128)S(1)} %pad_maximum_fusion.3.refs_9_), channel_id=1, source_target_pairs={{0,8},{8,0},{16,24},{24,16},{28,20},{20,28},{12,4},{4,12},{1,9},{9... | collective-permute-start | bytes 294920 | tf_op jit(solution)/shard_map/ppermute | solution.py:496
  42.1 7.1 %collective-permute-start.11 = (f32[2,2,32,384]{3,2,1,0:T(8,128)S(1)}, f32[2,2,32,384]{3,2,1,0:T(8,128)S(1)}, u32[]{:S(2)}, u32[]{:S(2)}) collective-permute-start(f32[2,2,32,384]{3,2,1,0:T(8,128)S(1)} %collective-permute-done.10.refs_4_), channel_id=1, source_target_pairs={{8,16},{16,8},{24,28},{28,24},{20,12},{12,20},{4,0},{0,4},{9,17},{... | collective-permute-start | bytes 589832 | tf_op jit(solution)/shard_map/ppermute | solution.py:496
  43.7 8.3 %collective-permute-start.8 = (f32[2,2,32,384]{3,2,1,0:T(8,128)S(1)}, f32[2,2,32,384]{3,2,1,0:T(8,128)S(1)}, u32[]{:S(2)}, u32[]{:S(2)}) collective-permute-start(f32[2,2,32,384]{3,2,1,0:T(8,128)S(1)} %collective-permute-done.7.refs_1_), channel_id=1, source_target_pairs={{0,8},{8,0},{16,24},{24,16},{28,20},{20,28},{12,4},{4,12},{1,9},{9... | collective-permute-start | bytes 589832 | tf_op jit(solution)/shard_map/ppermute | solution.py:496
  44.2 9.7 %collective-permute-start.15 = (f32[2,2,16,384]{3,2,1,0:T(8,128)S(1)}, f32[2,2,16,384]{3,2,1,0:T(8,128)S(1)}, u32[]{:S(2)}, u32[]{:S(2)}) collective-permute-start(f32[2,2,16,384]{3,2,1,0:T(8,128)S(1)} %pad_maximum_fusion.2.refs_6_), channel_id=1, source_target_pairs={{8,16},{16,8},{24,28},{28,24},{20,12},{12,20},{4,0},{0,4},{9,17},{... | collective-permute-start | bytes 294920 | tf_op jit(solution)/shard_map/ppermute | solution.py:496
  49.3 20.6 %collective-permute-start.21 = (f32[2,2,32,384]{3,2,1,0:T(8,128)S(1)}, f32[2,2,32,384]{3,2,1,0:T(8,128)S(1)}, u32[]{:S(2)}, u32[]{:S(2)}) collective-permute-start(f32[2,2,32,384]{3,2,1,0:T(8,128)S(1)} %collective-permute-done.11.refs_5_), channel_id=1, source_target_pairs={{0,8},{8,0},{16,24},{24,16},{28,20},{20,28},{12,4},{4,12},{1,9},{9... | collective-permute-start | bytes 589832 | tf_op jit(solution)/shard_map/ppermute | solution.py:496
  51.9 17.9 %collective-permute-start.20 = (f32[2,2,32,384]{3,2,1,0:T(8,128)S(1)}, f32[2,2,32,384]{3,2,1,0:T(8,128)S(1)}, u32[]{:S(2)}, u32[]{:S(2)}) collective-permute-start(f32[2,2,32,384]{3,2,1,0:T(8,128)S(1)} %collective-permute-done.8.refs_2_), channel_id=1, source_target_pairs={{8,16},{16,8},{24,28},{28,24},{20,12},{12,20},{4,0},{0,4},{9,17},{... | collective-permute-start | bytes 589832 | tf_op jit(solution)/shard_map/ppermute | solution.py:496
  53.4 6.3 %collective-permute-start.19 = (f32[2,2,16,384]{3,2,1,0:T(8,128)S(1)}, f32[2,2,16,384]{3,2,1,0:T(8,128)S(1)}, u32[]{:S(2)}, u32[]{:S(2)}) collective-permute-start(f32[2,2,16,384]{3,2,1,0:T(8,128)S(1)} %collective-permute-done.18.refs_10_), channel_id=1, source_target_pairs={{8,16},{16,8},{24,28},{28,24},{20,12},{12,20},{4,0},{0,4},{9,17},{... | collective-permute-start | bytes 294920 | tf_op jit(solution)/shard_map/ppermute | solution.py:496
  54.0 5.8 %collective-permute-start.16 = (f32[2,2,16,384]{3,2,1,0:T(8,128)S(1)}, f32[2,2,16,384]{3,2,1,0:T(8,128)S(1)}, u32[]{:S(2)}, u32[]{:S(2)}) collective-permute-start(f32[2,2,16,384]{3,2,1,0:T(8,128)S(1)} %collective-permute-done.15.refs_7_), channel_id=1, source_target_pairs={{0,8},{8,0},{16,24},{24,16},{28,20},{20,28},{12,4},{4,12},{1,9},{9... | collective-permute-start | bytes 294920 | tf_op jit(solution)/shard_map/ppermute | solution.py:496
  59.7 11.6 %collective-permute-start.23 = (f32[2,2,16,384]{3,2,1,0:T(8,128)S(1)}, f32[2,2,16,384]{3,2,1,0:T(8,128)S(1)}, u32[]{:S(2)}, u32[]{:S(2)}) collective-permute-start(f32[2,2,16,384]{3,2,1,0:T(8,128)S(1)} %collective-permute-done.19.refs_11_), channel_id=1, source_target_pairs={{0,8},{8,0},{16,24},{24,16},{28,20},{20,28},{12,4},{4,12},{1,9},{9... | collective-permute-start | bytes 294920 | tf_op jit(solution)/shard_map/ppermute | solution.py:496
  59.8 11.6 %collective-permute-start.22 = (f32[2,2,16,384]{3,2,1,0:T(8,128)S(1)}, f32[2,2,16,384]{3,2,1,0:T(8,128)S(1)}, u32[]{:S(2)}, u32[]{:S(2)}) collective-permute-start(f32[2,2,16,384]{3,2,1,0:T(8,128)S(1)} %collective-permute-done.16.refs_8_), channel_id=1, source_target_pairs={{8,16},{16,8},{24,28},{28,24},{20,12},{12,20},{4,0},{0,4},{9,17},{... | collective-permute-start | bytes 294920 | tf_op jit(solution)/shard_map/ppermute | solution.py:496
  61.2 6.1 %copy-start = (s32[8,3]{0,1:T(4,128)S(1)}, s32[8,3]{0,1:T(4,128)}, u32[]{:S(2)}) copy-start(s32[8,3]{0,1:T(4,128)} %param.15) | copy-start | bytes 292

commit v8 on v7

--- a/solution.py
+++ b/solution.py
@@ -133,7 +133,7 @@
 
 
 def contract_kernel(bands, slots, first, lines, e0, e1, *refs):
-    pieces, (keep, send) = refs[:-2], refs[-2:]
+    pieces, (keep, send, turn) = refs[:-3], refs[-3:]
     his, los = pieces[0::2], pieces[1::2]
     width = sum(h.shape[1] for h in his)
     total = e0[...] + e1[...]
@@ -164,9 +164,14 @@
                 t1 = jnp.where(low, j1, j2)
                 t2 = jnp.where(low, pltpu.roll(j1, 64, 1), pltpu.roll(j2, 64, 1))
                 for j, t in enumerate((j0, t1, t2)):
+                    turn[base // lines, j, pl.ds(q, 2 * bands, stride=lines), :] = t
+            for row in range(2 * bands):
+                dst = (keep, send)[row // bands]
+                for j in range(3):
                     spot = slice(j * LANES, (j + 1) * LANES)
-                    keep[:, r, base + q, spot] = t[0:bands]
-                    send[:, r, base + q, spot] = t[bands:]
+                    dst[row % bands, r, base : base + lines, spot] = turn[
+                        base // lines, j, row * lines : (row + 1) * lines, :
+                    ]
 
 
 def contract(pieces, e0, e1, bands, first, count):
@@ -176,6 +181,7 @@
         out_shape=(kept((bands, slots, count, 3 * LANES)),) * 2,
         in_specs=[WHOLE] * (2 + len(pieces)),
         out_specs=[WHOLE] * 2,
+        scratch_shapes=[VMEM((count // 8, 3, 2 * bands * 8, LANES), F32)],
         compiler_params=limit(8),
         name="contract",
     )(*in_vmem(e0, e1, *pieces))

time: 75.5 us -> 75.3 us (level)
  no operation moved by 1% of the time
where the time goes in v8:
time: 75.3 us; the launch traced here: 75.1 us
  waiting for transfers between devices  28.5 us (38%)
  starting transfers between devices  24.6 us (33%)
  Pallas kernels  20.2 us (27%)
  between operations  1.65 us (2%)
    ppermute x16, waiting for transfers between devices, neighbour_gather(): arrived.append(lax.ppermute(moving[h], 'row', perm))  18.2 us
    ppermute x16, starting transfers between devices, neighbour_gather(): arrived.append(lax.ppermute(moving[h], 'row', perm))  14.1 us
    ppermute x8, starting transfers between devices, swap(): return lax.ppermute(x, axis, [(i, i ^ bit) for i in range(n)])  10.4 us
    ppermute x8, waiting for transfers between devices, swap(): return lax.ppermute(x, axis, [(i, i ^ bit) for i in range(n)])  10.3 us
    pallas_call x2, Pallas kernels, prep(): pl.pallas_call(functools.partial(prep_kernel, size, turn, spans), out_sha...  6.09 us
    pallas_call x2, Pallas kernels, fetch(): pl.pallas_call(functools.partial(fetch_kernel, slots, first, rows, parts)...  4.2 us
    pallas_call x1, Pallas kernels, final(): pl.pallas_call(functools.partial(final_kernel, span, width, spec, 1.0 / t...  3.7 us
    pallas_call x1, Pallas kernels, early(): pl.pallas_call(functools.partial(early_kernel, spec, width, 8), out_shape...  2.05 us
  transfers between devices with their start and end apart: 24, of which 10 were waited for; matrix products, arithmetic and copies ran while one was open for 0% of the time, Pallas kernels for 20%

profile of v8, /device:TPU:0, one launch (start us, length us, event | category | flops | bytes accessed | tf_op | source)
XLA Modules:
  0.0 75.1 jit_solution(18152042882252290918)
XLA Ops:
  0.7 0.7 pack.1
  1.4 3.0 %collective-permute-start = (f32[16,128]{1,0:T(8,128)S(1)}, f32[16,128]{1,0:T(8,128)S(1)}, u32[]{:S(2)}, u32[]{:S(2)}) collective-permute-start(f32[16,128]{1,0:T(8,128)S(1)} %pack.1), channel_id=1, source_target_pairs={{0,4},{4,0},{8,12},{12,8},{16,20},{20,16},{24,28},{28,24},{1,5},{5... | collective-permute-start | bytes 24584 | tf_op jit(solution)/shard_map/ppermute | solution.py:476
  4.4 1.6 %collective-permute-start.1 = (f32[16,128]{1,0:T(8,128)S(1)}, f32[16,128]{1,0:T(8,128)S(1)}, u32[]{:S(2)}, u32[]{:S(2)}) collective-permute-start(f32[16,128]{1,0:T(8,128)S(1)} %pack.1), channel_id=1, source_target_pairs={{0,8},{4,12},{8,0},{12,4},{16,24},{20,28},{24,16},{28,20},{1,9},{5... | collective-permute-start | bytes 24584 | tf_op jit(solution)/shard_map/ppermute | solution.py:476
  6.0 0.1 collective-permute-done
  6.0 2.0 %collective-permute-done.1 = f32[16,128]{1,0:T(8,128)S(1)} collective-permute-done((f32[16,128]{1,0:T(8,128)S(1)}, f32[16,128]{1,0:T(8,128)S(1)}, u32[]{:S(2)}, u32[]{:S(2)}) %collective-permute-start.1) | collective-permute-done | bytes 8224 | tf_op jit(solution)/shard_map/ppermute | solution.py:476
  8.1 2.5 %collective-permute-done.2 = f32[16,128]{1,0:T(8,128)S(1)} collective-permute-done((f32[16,128]{1,0:T(8,128)S(1)}, f32[16,128]{1,0:T(8,128)S(1)}, u32[]{:S(2)}, u32[]{:S(2)}) %collective-permute-start.2) | collective-permute-done | bytes 8224 | tf_op jit(solution)/shard_map/ppermute | solution.py:476
  10.6 2.6 %collective-permute-start.3 = (f32[16,128]{1,0:T(8,128)S(1)}, f32[16,128]{1,0:T(8,128)S(1)}, u32[]{:S(2)}, u32[]{:S(2)}) collective-permute-start(f32[16,128]{1,0:T(8,128)S(1)} %add_add_fusion.e0), channel_id=1, source_target_pairs={{0,16},{4,20},{8,24},{12,28},{16,0},{20,4},{24,8},{28,12},{1,17},{... | collective-permute-start | bytes 24584 | tf_op jit(solution)/shard_map/ppermute | solution.py:476
  13.1 2.5 %fetch.2 = (bf16[1,32,36864]{2,1,0:T(8,128)(2,1)S(1)}, bf16[1,32,36864]{2,1,0:T(8,128)(2,1)S(1)}) custom-call(f32[1,48,36864]{2,1,0:T(8,128)} %const.3), custom_call_target="tpu_custom_call" | custom-call | tf_op jit(solution)/shard_map/fetch/pallas_call | solution.py:121
  15.6 1.7 %fetch.3 = (bf16[1,16,36864]{2,1,0:T(8,128)(2,1)S(1)}, bf16[1,16,36864]{2,1,0:T(8,128)(2,1)S(1)}) custom-call(f32[1,48,36864]{2,1,0:T(8,128)} %const.3), custom_call_target="tpu_custom_call" | custom-call | tf_op jit(solution)/shard_map/fetch/pallas_call | solution.py:121
  17.4 0.9 %contract.2 = (f32[4,1,64,384]{3,2,1,0:T(8,128)S(1)}, f32[4,1,64,384]{3,2,1,0:T(8,128)S(1)}) custom-call(f32[16,128]{1,0:T(8,128)S(1)} %add_add_fusion.e0, f32[16,128]{1,0:T(8,128)S(1)} %collective-permute-done.3.e1, bf16[1,32,36864]{2,1,0:T(8,128)(2,1)S(1)} %get-tuple-element.17.refs_0_, bf16[1,32,36864]{2,1,0:T(8,128)(2,1)S(1)} %get-tuple-element.18.refs_1_, ...), custom_call_target="tpu_custom_call" | custom-call | tf_op jit(solution)/shard_map/contract/pallas_call | solution.py:179
  18.3 0.1 collective-permute-start.4
  19.0 0.6 contract.3
  19.6 0.6 collective-permute-start.12
  20.2 1.6 %collective-permute-start.5 = (f32[2,1,64,384]{3,2,0,1:T(8,128)S(1)}, f32[2,1,64,384]{3,2,0,1:T(8,128)S(1)}, u32[]{:S(2)}, u32[]{:S(2)}) collective-permute-start(f32[2,1,64,384]{3,2,0,1:T(8,128)S(1)} %fusion), channel_id=1, source_target_pairs={{0,2},{1,3},{2,0},{3,1},{4,6},{5,7},{6,4},{7,5},{8,10},{9,11},{10,... | collective-permute-start | bytes 589832 | tf_op jit(solution)/shard_map/ppermute | solution.py:476
  21.7 0.0 collective-permute-done.12
  21.8 1.0 %collective-permute-start.13 = (f32[2,1,32,384]{3,2,0,1:T(8,128)S(1)}, f32[2,1,32,384]{3,2,0,1:T(8,128)S(1)}, u32[]{:S(2)}, u32[]{:S(2)}) collective-permute-start(f32[2,1,32,384]{3,2,0,1:T(8,128)S(1)} %fusion.5), channel_id=1, source_target_pairs={{0,2},{1,3},{2,0},{3,1},{4,6},{5,7},{6,4},{7,5},{8,10},{9,11},{10,... | collective-permute-start | bytes 294920 | tf_op jit(solution)/shard_map/ppermute | solution.py:476
  22.8 5.2 %collective-permute-done.5 = f32[2,1,64,384]{3,2,0,1:T(8,128)S(1)} collective-permute-done((f32[2,1,64,384]{3,2,0,1:T(8,128)S(1)}, f32[2,1,64,384]{3,2,0,1:T(8,128)S(1)}, u32[]{:S(2)}, u32[]{:S(2)}) %collective-permute-start.5) | collective-permute-done | bytes 196640 | tf_op jit(solution)/shard_map/ppermute | solution.py:476
  28.1 0.6 collective-permute-start.9
  28.7 0.5 collective-permute-done.13
  29.2 0.5 collective-permute-start.6
  29.7 3.0 %collective-permute-done.9 = f32[1,2,32,384]{3,2,1,0:T(8,128)S(1)} collective-permute-done((f32[1,2,32,384]{3,2,1,0:T(8,128)S(1)}, f32[1,2,32,384]{3,2,1,0:T(8,128)S(1)}, u32[]{:S(2)}, u32[]{:S(2)}) %collective-permute-start.9) | collective-permute-done | bytes 98336 | tf_op jit(solution)/shard_map/ppermute | solution.py:502
  32.8 0.5 collective-permute-start.10
  33.3 1.7 %collective-permute-done.6 = f32[1,2,32,384]{3,2,1,0:T(8,128)S(1)} collective-permute-done((f32[1,2,32,384]{3,2,1,0:T(8,128)S(1)}, f32[1,2,32,384]{3,2,1,0:T(8,128)S(1)}, u32[]{:S(2)}, u32[]{:S(2)}) %collective-permute-start.6) | collective-permute-done | bytes 98336 | tf_op jit(solution)/shard_map/ppermute | solution.py:502
  35.0 1.0 %collective-permute-start.7 = (f32[2,2,32,384]{3,2,1,0:T(8,128)S(1)}, f32[2,2,32,384]{3,2,1,0:T(8,128)S(1)}, u32[]{:S(2)}, u32[]{:S(2)}) collective-permute-start(f32[2,2,32,384]{3,2,1,0:T(8,128)S(1)} %pad_maximum_fusion.refs_0_), channel_id=1, source_target_pairs={{8,16},{16,8},{24,28},{28,24},{20,12},{12,20},{4,0},{0,4},{9,17},{... | collective-permute-start | bytes 589832 | tf_op jit(solution)/shard_map/ppermute | solution.py:502
  36.0 1.1 %collective-permute-start.17 = (f32[1,2,16,384]{3,2,1,0:T(8,128)S(1)}, f32[1,2,16,384]{3,2,1,0:T(8,128)S(1)}, u32[]{:S(2)}, u32[]{:S(2)}) collective-permute-start(f32[1,2,16,384]{3,2,1,0:T(8,128)S(1)} %get-tuple-element.31), channel_id=1, source_target_pairs={{8,16},{16,8},{24,28},{28,24},{20,12},{12,20},{4,0},{0,4},{9,17},{... | collective-permute-start | bytes 147464 | tf_op jit(solution)/shard_map/ppermute | solution.py:502
  37.1 0.4 collective-permute-start.14
  37.6 4.4 %collective-permute-done.17 = f32[1,2,16,384]{3,2,1,0:T(8,128)S(1)} collective-permute-done((f32[1,2,16,384]{3,2,1,0:T(8,128)S(1)}, f32[1,2,16,384]{3,2,1,0:T(8,128)S(1)}, u32[]{:S(2)}, u32[]{:S(2)}) %collective-permute-start.17) | collective-permute-done | bytes 49184 | tf_op jit(solution)/shard_map/ppermute | solution.py:502
  42.0 0.1 collective-permute-start.18
  42.0 0.0 collective-permute-done.10.refs_4_
  42.0 1.5 %collective-permute-start.11 = (f32[2,2,32,384]{3,2,1,0:T(8,128)S(1)}, f32[2,2,32,384]{3,2,1,0:T(8,128)S(1)}, u32[]{:S(2)}, u32[]{:S(2)}) collective-permute-start(f32[2,2,32,384]{3,2,1,0:T(8,128)S(1)} %collective-permute-done.10.refs_4_), channel_id=1, source_target_pairs={{8,16},{16,8},{24,28},{28,24},{20,12},{12,20},{4,0},{0,4},{9,17},{... | collective-permute-start | bytes 589832 | tf_op jit(solution)/shard_map/ppermute | solution.py:502
  43.5 0.0 collective-permute-done.7.refs_1_
  43.5 0.6 collective-permute-start.8
  44.1 0.0 collective-permute-done.14
  44.1 1.5 %collective-permute-start.15 = (f32[2,2,16,384]{3,2,1,0:T(8,128)S(1)}, f32[2,2,16,384]{3,2,1,0:T(8,128)S(1)}, u32[]{:S(2)}, u32[]{:S(2)}) collective-permute-start(f32[2,2,16,384]{3,2,1,0:T(8,128)S(1)} %pad_maximum_fusion.2.refs_6_), channel_id=1, source_target_pairs={{8,16},{16,8},{24,28},{28,24},{20,12},{12,20},{4,0},{0,4},{9,17},{... | collective-permute-start | bytes 294920 | tf_op jit(solution)/shard_map/ppermute | solution.py:502
  45.6 3.5 %collective-permute-done.11.refs_5_ = f32[2,2,32,384]{3,2,1,0:T(8,128)S(1)} collective-permute-done((f32[2,2,32,384]{3,2,1,0:T(8,128)S(1)}, f32[2,2,32,384]{3,2,1,0:T(8,128)S(1)}, u32[]{:S(2)}, u32[]{:S(2)}) %collective-permute-start.11) | collective-permute-done | bytes 196640 | tf_op jit(solution)/shard_map/ppermute | solution.py:502
  49.1 2.7 %collective-permute-start.21 = (f32[2,2,32,384]{3,2,1,0:T(8,128)S(1)}, f32[2,2,32,384]{3,2,1,0:T(8,128)S(1)}, u32[]{:S(2)}, u32[]{:S(2)}) collective-permute-start(f32[2,2,32,384]{3,2,1,0:T(8,128)S(1)} %collective-permute-done.11.refs_5_), channel_id=1, source_target_pairs={{0,8},{8,0},{16,24},{24,16},{28,20},{20,28},{12,4},{4,12},{1,9},{9... | collective-permute-start | bytes 589832 | tf_op jit(solution)/shard_map/ppermute | solution.py:502
  51.8 1.4 %collective-permute-start.20 = (f32[2,2,32,384]{3,2,1,0:T(8,128)S(1)}, f32[2,2,32,384]{3,2,1,0:T(8,128)S(1)}, u32[]{:S(2)}, u32[]{:S(2)}) collective-permute-start(f32[2,2,32,384]{3,2,1,0:T(8,128)S(1)} %collective-permute-done.8.refs_2_), channel_id=1, source_target_pairs={{8,16},{16,8},{24,28},{28,24},{20,12},{12,20},{4,0},{0,4},{9,17},{... | collective-permute-start | bytes 589832 | tf_op jit(solution)/shard_map/ppermute | solution.py:502
  53.2 0.6 collective-permute-start.19
  53.9 0.1 collective-permute-start.16
  53.9 5.7 %collective-permute-done.19.refs_11_ = f32[2,2,16,384]{3,2,1,0:T(8,128)S(1)} collective-permute-done((f32[2,2,16,384]{3,2,1,0:T(8,128)S(1)}, f32[2,2,16,384]{3,2,1,0:T(8,128)S(1)}, u32[]{:S(2)}, u32[]{:S(2)}) %collective-permute-start.19) | collective-permute-done | bytes 98336 | tf_op jit(solution)/shard_map/ppermute | solution.py:502
  59.6 0.1 collective-permute-start.23
  59.7 1.4 %collective-permute-start.22 = (f32[2,2,16,384]{3,2,1,0:T(8,128)S(1)}, f32[2,2,16,384]{3,2,1,0:T(8,128)S(1)}, u32[]{:S(2)}, u32[]{:S(2)}) collective-permute-start(f32[2,2,16,384]{3,2,1,0:T(8,128)S(1)} %collective-permute-done.16.refs_8_), channel_id=1, source_target_pairs={{8,16},{16,8},{24,28},{28,24},{20,12},{12,20},{4,0},{0,4},{9,17},{... | collective-permute-start | bytes 294920 | tf_op jit(solution)/shard_map/ppermute | solution.py:502
  61.1 2.6 %prep.2 = (bf16[8,3,192,192]{3,2,1,0:T(8,128)(2,1)S(1)}, bf16[8,3,192,192]{3,2,1,0:T(8,128)(2,1)S(1)}) custom-call(f32[8,576,128]{2,1,0:T(8,128)} %bitcast.59), custom_call_target="tpu_custom_call" | custom-call | tf_op jit(solution)/shard_map/prep/pallas_call | solution.py:247
  63.7 3.4 %prep.3 = (bf16[8,3,192,192]{3,2,1,0:T(8,128)(2,1)S(1)}, bf16[8,3,192,192]{3,2,1,0:T(8,128)(2,1)S(1)}) custom-call(f32[8,576,128]{2,1,0:T(8,128)} %bitcast.60), custom_call_target="tpu_custom_call" | custom-call | tf_op jit(solution)/shard_map/prep/pallas_call | solution.py:247
  67.2 0.4 angles.1.refs_12_.refs_2_
  67.6 2.1 %early.1.partial = f32[8,2,96,384]{3,2,1,0:T(8,128)S(1)} custom-call(f32[2,2,32,384]{3,2,1,0:T(8,128)S(1)} %pad_maximum_fusion.refs_0_, f32[2,2,32,384]{3,2,1,0:T(8,128)S(1)} %collective-permute-done.7.refs_1_, f32[2,2,32,384]{3,2,1,0:T(8,128)S(1)} %collective-permute-done.8.refs_2_, f32[2,2,32,384]{3,2,1,0:T(8,128)S(1)} %pad_maximum_fusion.1.refs_3_, ...), custom_call_target="tpu_custom_call" | custom-call | tf_op jit(solution)/shard_map/early/pallas_call | solution.py:344
  69.7 1.5 %inner.1.done = f32[8,2,128,192]{3,2,1,0:T(8,128)S(1)} custom-call(f32[8,2,96,384]{3,2,1,0:T(8,128)S(1)} %early.1.partial, f32[2,2,32,384]{3,2,1,0:T(8,128)S(1)} %collective-permute-done.20.refs_0_, f32[2,2,32,384]{3,2,1,0:T(8,128)S(1)} %collective-permute-done.21.refs_1_, f32[2,256,128]{2,1,0:T(8,128)S(1)} %angles.1.refs_12_.refs_2_, ...), custom_call_target="tpu_custom_call" | custom-call | tf_op jit(solution)/shard_map/inner/pallas_call | solution.py:403
  71.2 3.7 %final.1 = f32[8,288,128]{2,1,0:T(8,128)} custom-call(f32[8,2,128,192]{3,2,1,0:T(8,128)S(1)} %inner.1.done, f32[8,2,96,384]{3,2,1,0:T(8,128)S(1)} %early.1.partial, f32[2,2,16,384]{3,2,1,0:T(8,128)S(1)} %collective-permute-done.22.refs_0_, f32[2,2,16,384]{3,2,1,0:T(8,128)S(1)} %collective-permute-done.23.refs_1_, f32[2,256,128]{2,1,0:T(8,128)S(1)} %angles.1.refs_12_.refs_2_, ...), custom_call_target="tpu_custom_call" | custom-call | tf_op jit(solution)/shard_map/final/pallas_call | solution.py:461
  (24 shorter events, 0.2 us)
Async XLA Ops:
  1.4 4.7 %collective-permute-start = (f32[16,128]{1,0:T(8,128)S(1)}, f32[16,128]{1,0:T(8,128)S(1)}, u32[]{:S(2)}, u32[]{:S(2)}) collective-permute-start(f32[16,128]{1,0:T(8,128)S(1)} %pack.1), channel_id=1, source_target_pairs={{0,4},{4,0},{8,12},{12,8},{16,20},{20,16},{24,28},{28,24},{1,5},{5... | collective-permute-start | bytes 24584 | tf_op jit(solution)/shard_map/ppermute | solution.py:476
  4.4 3.7 %collective-permute-start.1 = (f32[16,128]{1,0:T(8,128)S(1)}, f32[16,128]{1,0:T(8,128)S(1)}, u32[]{:S(2)}, u32[]{:S(2)}) collective-permute-start(f32[16,128]{1,0:T(8,128)S(1)} %pack.1), channel_id=1, source_target_pairs={{0,8},{4,12},{8,0},{12,4},{16,24},{20,28},{24,16},{28,20},{1,9},{5... | collective-permute-start | bytes 24584 | tf_op jit(solution)/shard_map/ppermute | solution.py:476
  6.0 4.5 %collective-permute-start.2 = (f32[16,128]{1,0:T(8,128)S(1)}, f32[16,128]{1,0:T(8,128)S(1)}, u32[]{:S(2)}, u32[]{:S(2)}) collective-permute-start(f32[16,128]{1,0:T(8,128)S(1)} %pack.1), channel_id=1, source_target_pairs={{0,12},{4,8},{8,4},{12,0},{16,28},{20,24},{24,20},{28,16},{1,13},{... | collective-permute-start | bytes 24584 | tf_op jit(solution)/shard_map/ppermute | solution.py:476
  10.6 6.8 %collective-permute-start.3 = (f32[16,128]{1,0:T(8,128)S(1)}, f32[16,128]{1,0:T(8,128)S(1)}, u32[]{:S(2)}, u32[]{:S(2)}) collective-permute-start(f32[16,128]{1,0:T(8,128)S(1)} %add_add_fusion.e0), channel_id=1, source_target_pairs={{0,16},{4,20},{8,24},{12,28},{16,0},{20,4},{24,8},{28,12},{1,17},{... | collective-permute-start | bytes 24584 | tf_op jit(solution)/shard_map/ppermute | solution.py:476
  18.3 1.8 %collective-permute-start.4 = (f32[2,2,1,64,384]{4,3,1,2,0:T(8,128)S(1)}, f32[2,2,1,64,384]{4,3,1,2,0:T(8,128)S(1)}, u32[]{:S(2)}, u32[]{:S(2)}) collective-permute-start(f32[2,2,1,64,384]{4,3,1,2,0:T(8,128)S(1)} %bitcast.57), channel_id=1, source_target_pairs={{0,1},{1,0},{2,3},{3,2},{4,5},{5,4},{6,7},{7,6},{8,9},{9,8},{10,11... | collective-permute-start | bytes 1179656 | tf_op jit(solution)/shard_map/ppermute | solution.py:476
  19.6 2.2 %collective-permute-start.12 = (f32[2,2,1,32,384]{4,3,1,2,0:T(8,128)S(1)}, f32[2,2,1,32,384]{4,3,1,2,0:T(8,128)S(1)}, u32[]{:S(2)}, u32[]{:S(2)}) collective-permute-start(f32[2,2,1,32,384]{4,3,1,2,0:T(8,128)S(1)} %bitcast.58), channel_id=1, source_target_pairs={{0,1},{1,0},{2,3},{3,2},{4,5},{5,4},{6,7},{7,6},{8,9},{9,8},{10,11... | collective-permute-start | bytes 589832 | tf_op jit(solution)/shard_map/ppermute | solution.py:476
  20.2 7.8 %collective-permute-start.5 = (f32[2,1,64,384]{3,2,0,1:T(8,128)S(1)}, f32[2,1,64,384]{3,2,0,1:T(8,128)S(1)}, u32[]{:S(2)}, u32[]{:S(2)}) collective-permute-start(f32[2,1,64,384]{3,2,0,1:T(8,128)S(1)} %fusion), channel_id=1, source_target_pairs={{0,2},{1,3},{2,0},{3,1},{4,6},{5,7},{6,4},{7,5},{8,10},{9,11},{10,... | collective-permute-start | bytes 589832 | tf_op jit(solution)/shard_map/ppermute | solution.py:476
  21.8 7.4 %collective-permute-start.13 = (f32[2,1,32,384]{3,2,0,1:T(8,128)S(1)}, f32[2,1,32,384]{3,2,0,1:T(8,128)S(1)}, u32[]{:S(2)}, u32[]{:S(2)}) collective-permute-start(f32[2,1,32,384]{3,2,0,1:T(8,128)S(1)} %fusion.5), channel_id=1, source_target_pairs={{0,2},{1,3},{2,0},{3,1},{4,6},{5,7},{6,4},{7,5},{8,10},{9,11},{10,... | collective-permute-start | bytes 294920 | tf_op jit(solution)/shard_map/ppermute | solution.py:476
  28.1 4.7 %collective-permute-start.9 = (f32[1,2,32,384]{3,2,1,0:T(8,128)S(1)}, f32[1,2,32,384]{3,2,1,0:T(8,128)S(1)}, u32[]{:S(2)}, u32[]{:S(2)}) collective-permute-start(f32[1,2,32,384]{3,2,1,0:T(8,128)S(1)} %get-tuple-element.29), channel_id=1, source_target_pairs={{8,16},{16,8},{24,28},{28,24},{20,12},{12,20},{4,0},{0,4},{9,17},{... | collective-permute-start | bytes 294920 | tf_op jit(solution)/shard_map/ppermute | solution.py:502
  29.2 5.7 %collective-permute-start.6 = (f32[1,2,32,384]{3,2,1,0:T(8,128)S(1)}, f32[1,2,32,384]{3,2,1,0:T(8,128)S(1)}, u32[]{:S(2)}, u32[]{:S(2)}) collective-permute-start(f32[1,2,32,384]{3,2,1,0:T(8,128)S(1)} %get-tuple-element.30), channel_id=1, source_target_pairs={{0,8},{8,0},{16,24},{24,16},{28,20},{20,28},{12,4},{4,12},{1,9},{9... | collective-permute-start | bytes 294920 | tf_op jit(solution)/shard_map/ppermute | solution.py:502
  32.8 9.3 %collective-permute-start.10 = (f32[2,2,32,384]{3,2,1,0:T(8,128)S(1)}, f32[2,2,32,384]{3,2,1,0:T(8,128)S(1)}, u32[]{:S(2)}, u32[]{:S(2)}) collective-permute-start(f32[2,2,32,384]{3,2,1,0:T(8,128)S(1)} %pad_maximum_fusion.1.refs_3_), channel_id=1, source_target_pairs={{0,8},{8,0},{16,24},{24,16},{28,20},{20,28},{12,4},{4,12},{1,9},{9... | collective-permute-start | bytes 589832 | tf_op jit(solution)/shard_map/ppermute | solution.py:502
  35.0 8.5 %collective-permute-start.7 = (f32[2,2,32,384]{3,2,1,0:T(8,128)S(1)}, f32[2,2,32,384]{3,2,1,0:T(8,128)S(1)}, u32[]{:S(2)}, u32[]{:S(2)}) collective-permute-start(f32[2,2,32,384]{3,2,1,0:T(8,128)S(1)} %pad_maximum_fusion.refs_0_), channel_id=1, source_target_pairs={{8,16},{16,8},{24,28},{28,24},{20,12},{12,20},{4,0},{0,4},{9,17},{... | collective-permute-start | bytes 589832 | tf_op jit(solution)/shard_map/ppermute | solution.py:502
  36.0 5.9 %collective-permute-start.17 = (f32[1,2,16,384]{3,2,1,0:T(8,128)S(1)}, f32[1,2,16,384]{3,2,1,0:T(8,128)S(1)}, u32[]{:S(2)}, u32[]{:S(2)}) collective-permute-start(f32[1,2,16,384]{3,2,1,0:T(8,128)S(1)} %get-tuple-element.31), channel_id=1, source_target_pairs={{8,16},{16,8},{24,28},{28,24},{20,12},{12,20},{4,0},{0,4},{9,17},{... | collective-permute-start | bytes 147464 | tf_op jit(solution)/shard_map/ppermute | solution.py:502
  37.1 7.0 %collective-permute-start.14 = (f32[1,2,16,384]{3,2,1,0:T(8,128)S(1)}, f32[1,2,16,384]{3,2,1,0:T(8,128)S(1)}, u32[]{:S(2)}, u32[]{:S(2)}) collective-permute-start(f32[1,2,16,384]{3,2,1,0:T(8,128)S(1)} %get-tuple-element.32), channel_id=1, source_target_pairs={{0,8},{8,0},{16,24},{24,16},{28,20},{20,28},{12,4},{4,12},{1,9},{9... | collective-permute-start | bytes 147464 | tf_op jit(solution)/shard_map/ppermute | solution.py:502
  42.0 11.3 %collective-permute-start.18 = (f32[2,2,16,384]{3,2,1,0:T(8,128)S(1)}, f32[2,2,16,384]{3,2,1,0:T(8,128)S(1)}, u32[]{:S(2)}, u32[]{:S(2)}) collective-permute-start(f32[2,2,16,384]{3,2,1,0:T(8,128)S(1)} %pad_maximum_fusion.3.refs_9_), channel_id=1, source_target_pairs={{0,8},{8,0},{16,24},{24,16},{28,20},{20,28},{12,4},{4,12},{1,9},{9... | collective-permute-start | bytes 294920 | tf_op jit(solution)/shard_map/ppermute | solution.py:502
  42.0 7.1 %collective-permute-start.11 = (f32[2,2,32,384]{3,2,1,0:T(8,128)S(1)}, f32[2,2,32,384]{3,2,1,0:T(8,128)S(1)}, u32[]{:S(2)}, u32[]{:S(2)}) collective-permute-start(f32[2,2,32,384]{3,2,1,0:T(8,128)S(1)} %collective-permute-done.10.refs_4_), channel_id=1, source_target_pairs={{8,16},{16,8},{24,28},{28,24},{20,12},{12,20},{4,0},{0,4},{9,17},{... | collective-permute-start | bytes 589832 | tf_op jit(solution)/shard_map/ppermute | solution.py:502
  43.5 8.3 %collective-permute-start.8 = (f32[2,2,32,384]{3,2,1,0:T(8,128)S(1)}, f32[2,2,32,384]{3,2,1,0:T(8,128)S(1)}, u32[]{:S(2)}, u32[]{:S(2)}) collective-permute-start(f32[2,2,32,384]{3,2,1,0:T(8,128)S(1)} %collective-permute-done.7.refs_1_), channel_id=1, source_target_pairs={{0,8},{8,0},{16,24},{24,16},{28,20},{20,28},{12,4},{4,12},{1,9},{9... | collective-permute-start | bytes 589832 | tf_op jit(solution)/shard_map/ppermute | solution.py:502
  44.1 9.7 %collective-permute-start.15 = (f32[2,2,16,384]{3,2,1,0:T(8,128)S(1)}, f32[2,2,16,384]{3,2,1,0:T(8,128)S(1)}, u32[]{:S(2)}, u32[]{:S(2)}) collective-permute-start(f32[2,2,16,384]{3,2,1,0:T(8,128)S(1)} %pad_maximum_fusion.2.refs_6_), channel_id=1, source_target_pairs={{8,16},{16,8},{24,28},{28,24},{20,12},{12,20},{4,0},{0,4},{9,17},{... | collective-permute-start | bytes 294920 | tf_op jit(solution)/shard_map/ppermute | solution.py:502
  49.1 20.6 %collective-permute-start.21 = (f32[2,2,32,384]{3,2,1,0:T(8,128)S(1)}, f32[2,2,32,384]{3,2,1,0:T(8,128)S(1)}, u32[]{:S(2)}, u32[]{:S(2)}) collective-permute-start(f32[2,2,32,384]{3,2,1,0:T(8,128)S(1)} %collective-permute-done.11.refs_5_), channel_id=1, source_target_pairs={{0,8},{8,0},{16,24},{24,16},{28,20},{20,28},{12,4},{4,12},{1,9},{9... | collective-permute-start | bytes 589832 | tf_op jit(solution)/shard_map/ppermute | solution.py:502
  51.8 17.9 %collective-permute-start.20 = (f32[2,2,32,384]{3,2,1,0:T(8,128)S(1)}, f32[2,2,32,384]{3,2,1,0:T(8,128)S(1)}, u32[]{:S(2)}, u32[]{:S(2)}) collective-permute-start(f32[2,2,32,384]{3,2,1,0:T(8,128)S(1)} %collective-permute-done.8.refs_2_), channel_id=1, source_target_pairs={{8,16},{16,8},{24,28},{28,24},{20,12},{12,20},{4,0},{0,4},{9,17},{... | collective-permute-start | bytes 589832 | tf_op jit(solution)/shard_map/ppermute | solution.py:502
  53.2 6.4 %collective-permute-start.19 = (f32[2,2,16,384]{3,2,1,0:T(8,128)S(1)}, f32[2,2,16,384]{3,2,1,0:T(8,128)S(1)}, u32[]{:S(2)}, u32[]{:S(2)}) collective-permute-start(f32[2,2,16,384]{3,2,1,0:T(8,128)S(1)} %collective-permute-done.18.refs_10_), channel_id=1, source_target_pairs={{8,16},{16,8},{24,28},{28,24},{20,12},{12,20},{4,0},{0,4},{9,17},{... | collective-permute-start | bytes 294920 | tf_op jit(solution)/shard_map/ppermute | solution.py:502
  53.9 5.8 %collective-permute-start.16 = (f32[2,2,16,384]{3,2,1,0:T(8,128)S(1)}, f32[2,2,16,384]{3,2,1,0:T(8,128)S(1)}, u32[]{:S(2)}, u32[]{:S(2)}) collective-permute-start(f32[2,2,16,384]{3,2,1,0:T(8,128)S(1)} %collective-permute-done.15.refs_7_), channel_id=1, source_target_pairs={{0,8},{8,0},{16,24},{24,16},{28,20},{20,28},{12,4},{4,12},{1,9},{9... | collective-permute-start | bytes 294920 | tf_op jit(solution)/shard_map/ppermute | solution.py:502
  59.6 11.6 %collective-permute-start.23 = (f32[2,2,16,384]{3,2,1,0:T(8,128)S(1)}, f32[2,2,16,384]{3,2,1,0:T(8,128)S(1)}, u32[]{:S(2)}, u32[]{:S(2)}) collective-permute-start(f32[2,2,16,384]{3,2,1,0:T(8,128)S(1)} %collective-permute-done.19.refs_11_), channel_id=1, source_target_pairs={{0,8},{8,0},{16,24},{24,16},{28,20},{20,28},{12,4},{4,12},{1,9},{9... | collective-permute-start | bytes 294920 | tf_op jit(solution)/shard_map/ppermute | solution.py:502
  59.7 11.5 %collective-permute-start.22 = (f32[2,2,16,384]{3,2,1,0:T(8,128)S(1)}, f32[2,2,16,384]{3,2,1,0:T(8,128)S(1)}, u32[]{:S(2)}, u32[]{:S(2)}) collective-permute-start(f32[2,2,16,384]{3,2,1,0:T(8,128)S(1)} %collective-permute-done.16.refs_8_), channel_id=1, source_target_pairs={{8,16},{16,8},{24,28},{28,24},{20,12},{12,20},{4,0},{0,4},{9,17},{... | collective-permute-start | bytes 294920 | tf_op jit(solution)/shard_map/ppermute | solution.py:502
  61.1 6.1 %copy-start = (s32[8,3]{0,1:T(4,128)S(1)}, s32[8,3]{0,1:T(4,128)}, u32[]{:S(2)}) copy-start(s32[8,3]{0,1:T(4,128)} %param.15) | copy-start | bytes 292
